TPU v7x, 32 devices: a whole 2x2x4 slice. The times are simulated.
32 devices in a mesh: groups: 2 (over x), blk: 4 (over y, core), width: 4 (over z).
Axes of the slice: x: 2, y: 2, z: 4, core: 2. Of those that a mesh axis runs over, the one named last changes fastest.
Arguments:
- activations: float32 [8192, 8192], P(('groups', 'blk'), 'width'), parts along dimension 0, may hold values from -6 to 6
- query_grads: float32 [16, 8192, 128], P(('groups', 'blk'), 'width'), parts along dimension 0, may hold values from -0.0625 to 0.0625
- outgrad_proj: float32 [8192, 128], P(('groups', 'blk', 'width')), parts along dimension 0, may hold values from -0.6 to 0.6
- doc_ids: int32 [8192], P(('groups', 'blk', 'width')), parts along dimension 0, may hold values from 0 to 15, never falling along the last dimension, each value on 1 to 512 neighbouring positions
Outputs:
- token_scores: float32 [8192, 8], P(('groups', 'blk', 'width')), parts along dimension 0
- doc_scores: float32 [32, 8], P('groups'), parts along dimension 0
There are 2 independent parts, one for each index of `groups`. A program takes and returns all parts, laid end to end along the dimension named above; each array names one. Nothing has to cross between parts.
Inputs may be any that keep to these rules, and one draw needn't show every extreme that they name: `doc_ids`: never falls along the tokens; every document 0 to 15 holds 1 to 512 tokens, one exactly 512.
All inputs are finite; a program needn't handle non-finite values.
Results may differ from a plain program's by a relative error of at most 0.000078.
Values sent between devices are 32-bit elements; how exact they have to be, the bound alone decides.
No kernel may reach another device: no remote copies, remote signals or barrier semaphores. Data moves between devices by JAX's collectives and lax.ppermute only.
A program may use at most 128 MiB of HBM per device.

v0:
```python
import functools

import jax
import jax.numpy as jnp
from jax import lax
from jax.experimental import pallas as pl
from jax.experimental.pallas import tpu as pltpu
from jax.sharding import PartitionSpec as P

DOC_BLK = 4
LANES = 128
F32, BF16 = jnp.float32, jnp.bfloat16
TILE = 256
PARTS = (2, 4, 8, 16, 16)
VMEM = pl.BlockSpec(memory_space=pltpu.VMEM)
HBM = pl.BlockSpec(memory_space=pltpu.HBM)
PARAMS = pltpu.CompilerParams(vmem_limit_bytes=16 << 20)
COST = pl.CostEstimate(flops=1, bytes_accessed=1, transcendentals=0)


def split(x):
    high = x.astype(BF16)
    return high, (x - high.astype(F32)).astype(BF16)


def in_hbm(x):
    return pltpu.with_memory_space_constraint(x, pltpu.HBM)


def cut_kernel(pieces, g_ref, *refs):
    outs, sems = refs[:-1], refs[-1]
    copies = [
        pltpu.make_async_copy(g_ref.at[:, at : at + n], out, sems.at[i])
        for i, ((at, n), out) in enumerate(zip(pieces, outs))
    ]
    for copy in copies:
        copy.start()
    for copy in copies:
        copy.wait()


def cut(g, pieces):
    nq, _, r = g.shape
    return pl.pallas_call(
        functools.partial(cut_kernel, pieces),
        in_specs=[HBM],
        out_specs=[VMEM] * len(pieces),
        out_shape=[jax.ShapeDtypeStruct((nq, n, r), F32) for _, n in pieces],
        scratch_shapes=[pltpu.SemaphoreType.DMA((len(pieces),))],
        compiler_params=PARAMS,
        cost_estimate=COST,
    )(in_hbm(g))


def weigh(g_ref, step):
    nq, n, _ = g_ref.shape
    return [
        split(jnp.concatenate([g_ref[q, k : k + step] for q in range(nq)], axis=1))
        for k in range(0, n, step)
    ]


def score_tile(a, weights, o, step):
    dot = functools.partial(jnp.dot, preferred_element_type=F32)
    p = None
    for i, (gh, gl) in enumerate(weights):
        gh, gl = gh[...], gl[...]
        ah, al = split(a[:, i * step : (i + 1) * step])
        if step < 256:
            part = dot(jnp.concatenate([ah, al, ah], axis=1), jnp.concatenate([gh, gh, gl], axis=0))
        else:
            part = dot(ah, gh) + dot(al, gh) + dot(ah, gl)
        p = part if p is None else p + part
    r = o.shape[1]
    return [jnp.sum(p[:, q : q + r] * o, axis=1) for q in range(0, p.shape[1], r)]


def stream_kernel(first, staged, *refs):
    a_refs, o_refs, refs = refs[:2], refs[2:4], refs[4:]
    g_ref, prev_ref, s_ref, *stage_refs, high_ref, low_ref = refs
    tile, n = a_refs[0].shape
    t = s_ref.shape[1] // 2
    i = pl.program_id(0)
    step = high_ref.shape[1]

    @pl.when(i == 0)
    def _():
        s_ref[...] = prev_ref[...]
        for k, (gh, gl) in enumerate(weigh(g_ref, step)):
            high_ref[k] = gh
            low_ref[k] = gl

    weights = [(high_ref.at[k], low_ref.at[k]) for k in range(n // step)]
    for h in range(2):
        a = a_refs[h][...]
        at = pl.multiple_of(h * t + i * tile, tile)
        for q, row in enumerate(score_tile(a, weights, o_refs[h][...], step)):
            s_ref[first + q, pl.ds(at, tile)] += row
        if staged:
            stage_refs[h][...] = a[:, n - staged :]


def stream_scores(s, activations, outgrads, g, start, first, staged=0):
    t = activations[0].shape[0]
    nq, n, r = g.shape
    tile = min(t, TILE)
    step = min(n, 512)
    col = start // n
    whole = pl.BlockSpec(s.shape, lambda i: (0, 0))
    stage = jax.ShapeDtypeStruct((t, staged), F32)
    out = pl.pallas_call(
        functools.partial(stream_kernel, first, staged),
        grid=(t // tile,),
        in_specs=[pl.BlockSpec((tile, n), lambda i: (i, col))] * 2
        + [pl.BlockSpec((tile, r), lambda i: (i, 0))] * 2
        + [pl.BlockSpec((nq, n, r), lambda i: (0, 0, 0), pipeline_mode=pl.Buffered(1)), whole],
        out_specs=[whole] + [pl.BlockSpec((tile, staged), lambda i: (i, 0))] * (2 if staged else 0),
        out_shape=[jax.ShapeDtypeStruct(s.shape, F32)] + [stage] * (2 if staged else 0),
        scratch_shapes=[pltpu.VMEM((n // step, step, nq * r), BF16)] * 2,
        compiler_params=PARAMS,
        cost_estimate=COST,
    )(*[in_hbm(a) for a in activations], *outgrads, g, s)
    return out if staged else out[0]


def staged_kernel(start, first, *refs):
    a_refs, o_refs, (g_ref, prev_ref, s_ref) = refs[:2], refs[2:4], refs[4:]
    n = g_ref.shape[1]
    t = a_refs[0].shape[0]
    tile = min(t, 256)
    weights = weigh(g_ref, n)
    s_ref[...] = prev_ref[...]
    for h in range(2):
        for m in range(0, t, tile):
            a = a_refs[h][m : m + tile, start : start + n]
            at = h * t + m
            for q, row in enumerate(score_tile(a, weights, o_refs[h][m : m + tile, :], n)):
                s_ref[first + q, at : at + tile] += row


def staged_scores(s, stages, outgrads, g, start, first):
    return pl.pallas_call(
        functools.partial(staged_kernel, start, first),
        in_specs=[VMEM] * 6,
        out_specs=VMEM,
        out_shape=jax.ShapeDtypeStruct(s.shape, F32),
        compiler_params=PARAMS,
        cost_estimate=COST,
    )(*stages, *outgrads, g, s)


def per_device(a, g, o, ids):
    nb, nw = lax.axis_size("blk"), lax.axis_size("width")
    b, w = lax.axis_index("blk"), lax.axis_index("width")
    nq, d, r = g.shape
    t = a.shape[0]
    own = o.shape[0]
    docs = DOC_BLK * nb
    pairs = lambda n, k: [(i, i ^ k) for i in range(n)]
    to_core = lambda x: lax.ppermute(x, "blk", pairs(nb, 1))

    def after(x, *others):
        return lax.optimization_barrier((x, *others))[0]

    pieces, at = [], 0
    for part in PARTS:
        n = max(d // part, LANES)
        if at < d:
            pieces.append((at, n))
        at += n
    cuts = cut(g, pieces[:1])
    ids_other = to_core(after(ids, cuts[0]))
    cuts += cut(after(g, ids_other), pieces[1:])
    sends = [(j, at, x) for j in range(2, nb, 2) for (at, _), x in zip(pieces, cuts)]

    def send(i, *others):
        j, _, x = sends[i]
        return lax.ppermute(after(x, *others), "blk", pairs(nb, j))

    arrived = [send(0), send(1)]
    a_other = to_core(after(a, ids_other))

    rows = own // LANES
    flat = ids.astype(F32).reshape(rows, LANES)
    mine = after(jnp.concatenate([o, flat], axis=0), ids_other)
    table = jnp.zeros((t + t // LANES, LANES), F32)
    for k in range(nw):
        got = lax.ppermute(mine, "width", pairs(nw, k)) if k else mine
        src = w ^ k
        table = lax.dynamic_update_slice(table, got[:own], (src * own, 0))
        table = lax.dynamic_update_slice(table, got[own:], (t + src * rows, 0))
    other = to_core(table)

    both, outgrads = [a, a_other], [table, other]
    s = jnp.zeros((nb // 2 * nq, 2 * t), F32)
    late = d - pieces[-3][0]
    s, *stages = stream_scores(s, both, outgrads, g, 0, 0, late)
    for i, (j, at, x) in enumerate(sends):
        if i + 2 < len(sends):
            arrived.append(send(i + 2, s))
        first = j // 2 * nq
        if at < d - late:
            s = stream_scores(s, both, outgrads, arrived[i], at, first)
        else:
            s = staged_scores(s, stages, outgrads, arrived[i], at - (d - late), first)

    number = jnp.arange(docs, dtype=F32)
    marks = lambda x: (x.reshape(-1)[:, None] == number[None, :]).astype(F32)
    count = jnp.sum(marks(flat), axis=0) + jnp.sum(marks(ids_other.astype(F32)), axis=0)
    onehot = marks(jnp.concatenate([table[t:], other[t:]], axis=0))
    doc = jnp.dot(s, onehot, precision=lax.Precision.HIGHEST, preferred_element_type=F32)

    keep = jnp.concatenate([s[:, :t], doc], axis=1)
    got = to_core(jnp.concatenate([s[:, t:], doc], axis=1))
    blocks = []
    for k in range(0, nb // 2 * nq, nq):
        blocks += [keep[k : k + nq], got[k : k + nq]]
    bit = 1
    while bit < nb:
        swap = (b & bit) != 0
        blocks = [jnp.where(swap, blocks[i ^ bit], blocks[i]) for i in range(nb)]
        bit *= 2
    s = jnp.concatenate(blocks, axis=0)
    s, doc = s[:, :t], s[:, t:]
    doc = jnp.concatenate([doc, jnp.broadcast_to(count[None, :], doc.shape)], axis=1)

    k = 2
    while k < nb:
        doc = doc + lax.ppermute(doc, "blk", pairs(nb, k))
        k *= 2
    k = nw // 2
    while k:
        half = s.shape[1] // 2
        low = (w & k) == 0
        keep = jnp.where(low, s[:, :half], s[:, half:])
        give = jnp.where(low, s[:, half:], s[:, :half])
        got = lax.ppermute(jnp.concatenate([give, doc], axis=1), "width", pairs(nw, k))
        s = keep + got[:, :half]
        doc = doc + got[:, half:]
        k //= 2
    doc_scores = (doc[:, :docs] / jnp.sqrt(doc[:, docs:])).T
    return (s.T, doc_scores)


def solution(mesh):
    return jax.shard_map(
        per_device,
        mesh=mesh,
        in_specs=(
            P(("groups", "blk"), "width"),
            P(("groups", "blk"), "width", None),
            P(("groups", "blk", "width"), None),
            P(("groups", "blk", "width")),
        ),
        out_specs=(P(("groups", "blk", "width"), None), P("groups", None)),
        check_vma=False,
    )
```

profile of v0, /device:TPU:0, one launch (start us, length us, event | category | flops | bytes accessed | tf_op | source)
XLA Modules:
  0.0 75.3 jit_solution(10556239097083272298)
XLA Ops:
  0.6 0.0 copy-start.6
  0.6 0.0 copy-start.5
  0.6 2.3 %shard_map.59 = f32[2,1024,128]{2,1,0:T(8,128)} custom-call(f32[2,2048,128]{2,1,0:T(8,128)} %g_ref.2), custom_call_target="tpu_custom_call" | custom-call | flops 1 | bytes 1 | tf_op jit(solution)/shard_map/pallas_call | solution.py:44
  3.0 0.0 copy-done.6
  3.0 0.0 copy-start
  3.0 0.5 collective-permute-start
  3.5 0.8 %collective-permute-done = s32[256]{0:T(256)S(1)} collective-permute-done((s32[256]{0:T(256)S(1)}, s32[256]{0:T(256)S(1)}, u32[]{:S(2)}, u32[]{:S(2)}) %collective-permute-start) | collective-permute-done | bytes 1056 | tf_op jit(solution)/shard_map/ppermute | solution.py:160
  4.3 0.3 collective-permute-start.1
  4.6 2.7 %collective-permute-start.7 = (f32[2,1024,128]{2,1,0:T(8,128)}, f32[2,1024,128]{2,1,0:T(8,128)}, u32[]{:S(2)}, u32[]{:S(2)}) collective-permute-start(f32[2,1024,128]{2,1,0:T(8,128)} %shard_map.59), channel_id=1, source_target_pairs={{0,8},{4,12},{8,0},{12,4},{1,9},{5,13},{9,1},{13,5},{2,10},{6,14},... | collective-permute-start | bytes 3145736 | tf_op jit(solution)/shard_map/ppermute | solution.py:178
  7.3 0.0 copy-done.5
  7.4 1.6 %collective-permute-start.2 = (f32[258,128]{1,0:T(8,128)S(1)}, f32[258,128]{1,0:T(8,128)S(1)}, u32[]{:S(2)}, u32[]{:S(2)}) collective-permute-start(f32[258,128]{1,0:T(8,128)S(1)} %pad_maximum_fusion), channel_id=1, source_target_pairs={{0,1},{1,0},{2,3},{3,2},{4,5},{5,4},{6,7},{7,6},{8,9},{9,8},{10,11... | collective-permute-start | bytes 396296 | tf_op jit(solution)/shard_map/ppermute | solution.py:188
  9.0 2.6 %collective-permute-start.3 = (f32[258,128]{1,0:T(8,128)S(1)}, f32[258,128]{1,0:T(8,128)S(1)}, u32[]{:S(2)}, u32[]{:S(2)}) collective-permute-start(f32[258,128]{1,0:T(8,128)S(1)} %pad_maximum_fusion), channel_id=1, source_target_pairs={{0,2},{1,3},{2,0},{3,1},{4,6},{5,7},{6,4},{7,5},{8,10},{9,11},{10,... | collective-permute-start | bytes 396296 | tf_op jit(solution)/shard_map/ppermute | solution.py:188
  11.6 0.2 collective-permute-start.4
  11.9 3.0 %collective-permute-done.2 = f32[258,128]{1,0:T(8,128)S(1)} collective-permute-done((f32[258,128]{1,0:T(8,128)S(1)}, f32[258,128]{1,0:T(8,128)S(1)}, u32[]{:S(2)}, u32[]{:S(2)}) %collective-permute-start.2) | collective-permute-done | bytes 132128 | tf_op jit(solution)/shard_map/ppermute | solution.py:188
  14.9 7.3 %collective-permute-done.3 = f32[258,128]{1,0:T(8,128)S(1)} collective-permute-done((f32[258,128]{1,0:T(8,128)S(1)}, f32[258,128]{1,0:T(8,128)S(1)}, u32[]{:S(2)}, u32[]{:S(2)}) %collective-permute-start.3) | collective-permute-done | bytes 132128 | tf_op jit(solution)/shard_map/ppermute | solution.py:188
  22.2 0.0 collective-permute-done.4
  22.3 0.1 collective-permute-start.5
  22.4 2.0 %shard_map.61 = (f32[2,512,128]{2,1,0:T(8,128)S(1)}, f32[2,256,128]{2,1,0:T(8,128)}, f32[2,128,128]{2,1,0:T(8,128)}, f32[2,128,128]{2,1,0:T(8,128)}) custom-call(f32[2,2048,128]{2,1,0:T(8,128)} %g_ref.2), custom_call_target="tpu_custom_call" | custom-call | flops 1 | bytes 1 | tf_op jit(solution)/shard_map/pallas_call | solution.py:44
  24.4 0.6 collective-permute-start.6
  24.9 0.0 collective-permute-done.5.refs_3_
  24.9 0.0 collective-permute-done.1.refs_1_
  25.0 0.0 copy-done
  25.0 10.8 %shard_map.60 = (f32[4,2048]{1,0:T(4,128)S(1)}, f32[1024,512]{1,0:T(8,128)S(1)}, f32[1024,512]{1,0:T(8,128)S(1)}) custom-call(f32[1024,2048]{1,0:T(8,128)} %refs_0_.5, f32[1024,2048]{1,0:T(8,128)} %collective-permute-done.1.refs_1_, f32[1032,128]{1,0:T(8,128)S(1)} %constant_dynamic-update-slice_fusion.refs_2_, ...), custom_call_target="tpu_custom_call" | custom-call | flops 1 | bytes 1 | tf_op jit(solution)/shard_map/pallas_call | solution.py:111
  35.8 0.0 copy-start.3
  35.8 1.4 %copy-done.3 = f32[1024,512]{1,0:T(8,128)} copy-done((f32[1024,512]{1,0:T(8,128)}, f32[1024,512]{1,0:T(8,128)S(1)}, u32[]{:S(2)}) %copy-start.3) | copy-done | bytes 2097176
  37.2 0.0 copy-start.1
  37.2 1.5 %collective-permute-start.10 = (f32[2,256,128]{2,1,0:T(8,128)}, f32[2,256,128]{2,1,0:T(8,128)S(1)}, u32[]{:S(2)}, u32[]{:S(2)}) collective-permute-start(f32[2,256,128]{2,1,0:T(8,128)} %get-tuple-element.29), channel_id=1, source_target_pairs={{0,8},{4,12},{8,0},{12,4},{1,9},{5,13},{9,1},{13,5},{2,10},{6,14},... | collective-permute-start | bytes 786440 | tf_op jit(solution)/shard_map/ppermute | solution.py:178
  38.8 0.0 collective-permute-done.7.refs_4_
  38.8 7.2 %shard_map.62.refs_5_ = f32[4,2048]{1,0:T(4,128)S(1)} custom-call(f32[1024,2048]{1,0:T(8,128)} %refs_0_.5, f32[1024,2048]{1,0:T(8,128)} %collective-permute-done.1.refs_1_, f32[1032,128]{1,0:T(8,128)S(1)} %constant_dynamic-update-slice_fusion.refs_2_, f32[1032,128]{1,0:T(8,128)S(1)} %collective-permute-done.5.refs_3_, ...), custom_call_target="tpu_custom_call" | custom-call | flops 1 | bytes 1 | tf_op jit(solution)/shard_map/pallas_call | solution.py:111
  45.9 0.0 copy-done.1
  45.9 0.0 copy-start.2
  46.0 0.8 %collective-permute-start.9 = (f32[2,128,128]{2,1,0:T(8,128)}, f32[2,128,128]{2,1,0:T(8,128)}, u32[]{:S(2)}, u32[]{:S(2)}) collective-permute-start(f32[2,128,128]{2,1,0:T(8,128)} %get-tuple-element.27), channel_id=1, source_target_pairs={{0,8},{4,12},{8,0},{12,4},{1,9},{5,13},{9,1},{13,5},{2,10},{6,14},... | collective-permute-start | bytes 393224 | tf_op jit(solution)/shard_map/ppermute | solution.py:178
  46.7 0.0 collective-permute-done.6.refs_4_
  46.7 4.8 %shard_map.63.refs_5_ = f32[4,2048]{1,0:T(4,128)S(1)} custom-call(f32[1024,2048]{1,0:T(8,128)} %refs_0_.5, f32[1024,2048]{1,0:T(8,128)} %collective-permute-done.1.refs_1_, f32[1032,128]{1,0:T(8,128)S(1)} %constant_dynamic-update-slice_fusion.refs_2_, f32[1032,128]{1,0:T(8,128)S(1)} %collective-permute-done.5.refs_3_, ...), custom_call_target="tpu_custom_call" | custom-call | flops 1 | bytes 1 | tf_op jit(solution)/shard_map/pallas_call | solution.py:111
  51.6 1.4 %collective-permute-start.8 = (f32[2,128,128]{2,1,0:T(8,128)}, f32[2,128,128]{2,1,0:T(8,128)}, u32[]{:S(2)}, u32[]{:S(2)}) collective-permute-start(f32[2,128,128]{2,1,0:T(8,128)} %get-tuple-element.25), channel_id=1, source_target_pairs={{0,8},{4,12},{8,0},{12,4},{1,9},{5,13},{9,1},{13,5},{2,10},{6,14},... | collective-permute-start | bytes 393224 | tf_op jit(solution)/shard_map/ppermute | solution.py:178
  53.0 0.1 convert_reduce_fusion.1
  53.1 0.0 collective-permute-done.10.refs_4_
  53.1 0.0 copy-done.2
  53.1 0.0 copy-start.4
  53.2 1.6 %copy-done.4 = f32[1024,512]{1,0:T(8,128)S(1)} copy-done((f32[1024,512]{1,0:T(8,128)S(1)}, f32[1024,512]{1,0:T(8,128)}, u32[]{:S(2)}) %copy-start.4) | copy-done | bytes 2097176
  54.7 1.2 %shard_map.64.refs_5_ = f32[4,2048]{1,0:T(4,128)S(1)} custom-call(f32[1024,512]{1,0:T(8,128)S(1)} %copy-done.2, f32[1024,512]{1,0:T(8,128)S(1)} %copy-done.4, f32[1032,128]{1,0:T(8,128)S(1)} %constant_dynamic-update-slice_fusion.refs_2_, f32[1032,128]{1,0:T(8,128)S(1)} %collective-permute-done.5.refs_3_, f32[2,256,128]{2,1,0:T(8,128)S(1)} %collective-permute-done.10.refs_4_, ...), custom_call_target="tpu_custom_call" | custom-call | flops 1 | bytes 1 | tf_op jit(solution)/shard_map/pallas_call | solution.py:142
  55.9 0.0 collective-permute-done.9.refs_4_
  55.9 1.8 %shard_map.65.refs_5_ = f32[4,2048]{1,0:T(4,128)S(1)} custom-call(f32[1024,512]{1,0:T(8,128)S(1)} %copy-done.2, f32[1024,512]{1,0:T(8,128)S(1)} %copy-done.4, f32[1032,128]{1,0:T(8,128)S(1)} %constant_dynamic-update-slice_fusion.refs_2_, f32[1032,128]{1,0:T(8,128)S(1)} %collective-permute-done.5.refs_3_, f32[2,128,128]{2,1,0:T(8,128)} %collective-permute-done.9.refs_4_, ...), custom_call_target="tpu_custom_call" | custom-call | flops 1 | bytes 1 | tf_op jit(solution)/shard_map/pallas_call | solution.py:142
  57.7 0.0 collective-permute-done.8.refs_4_
  57.7 1.8 %shard_map.66 = f32[4,2048]{1,0:T(4,128)S(1)} custom-call(f32[1024,512]{1,0:T(8,128)S(1)} %copy-done.2, f32[1024,512]{1,0:T(8,128)S(1)} %copy-done.4, f32[1032,128]{1,0:T(8,128)S(1)} %constant_dynamic-update-slice_fusion.refs_2_, f32[1032,128]{1,0:T(8,128)S(1)} %collective-permute-done.5.refs_3_, f32[2,128,128]{2,1,0:T(8,128)} %collective-permute-done.8.refs_4_, ...), custom_call_target="tpu_custom_call" | custom-call | flops 1 | bytes 1 | tf_op jit(solution)/shard_map/pallas_call | solution.py:142
  59.5 0.6 fusion
  60.1 0.1 collective-permute-start.11
  60.2 0.1 convert_reduce_fusion
  60.3 0.1 pad.5.clone
  60.4 1.0 %collective-permute-done.11 = f32[4,1040]{1,0:T(4,128)S(1)} collective-permute-done((f32[4,1040]{1,0:T(4,128)S(1)}, f32[4,1040]{1,0:T(4,128)S(1)}, u32[]{:S(2)}, u32[]{:S(2)}) %collective-permute-start.11) | collective-permute-done | bytes 16672 | tf_op jit(solution)/shard_map/ppermute | solution.py:160
  61.5 0.8 %collective-permute-start.12 = (f32[8,32]{1,0:T(8,128)S(1)}, f32[8,32]{1,0:T(8,128)S(1)}, u32[]{:S(2)}, u32[]{:S(2)}) collective-permute-start(f32[8,32]{1,0:T(8,128)S(1)} %fusion.4), channel_id=1, source_target_pairs={{0,8},{4,12},{8,0},{12,4},{1,9},{5,13},{9,1},{13,5},{2,10},{6,14},... | collective-permute-start | bytes 3080 | tf_op jit(solution)/shard_map/ppermute | solution.py:229
  62.2 2.9 %collective-permute-done.12 = f32[8,32]{1,0:T(8,128)S(1)} collective-permute-done((f32[8,32]{1,0:T(8,128)S(1)}, f32[8,32]{1,0:T(8,128)S(1)}, u32[]{:S(2)}, u32[]{:S(2)}) %collective-permute-start.12) | collective-permute-done | bytes 1056 | tf_op jit(solution)/shard_map/ppermute | solution.py:229
  65.1 3.3 %collective-permute-start.13 = (f32[8,544]{1,0:T(8,128)S(1)}, f32[8,544]{1,0:T(8,128)S(1)}, u32[]{:S(2)}, u32[]{:S(2)}) collective-permute-start(f32[8,544]{1,0:T(8,128)S(1)} %pad_maximum_fusion.3), channel_id=1, source_target_pairs={{0,2},{1,3},{2,0},{3,1},{4,6},{5,7},{6,4},{7,5},{8,10},{9,11},{10,... | collective-permute-start | bytes 52232 | tf_op jit(solution)/shard_map/ppermute | solution.py:237
  68.4 1.8 %collective-permute-done.13 = f32[8,544]{1,0:T(8,128)S(1)} collective-permute-done((f32[8,544]{1,0:T(8,128)S(1)}, f32[8,544]{1,0:T(8,128)S(1)}, u32[]{:S(2)}, u32[]{:S(2)}) %collective-permute-start.13) | collective-permute-done | bytes 17440 | tf_op jit(solution)/shard_map/ppermute | solution.py:237
  70.2 2.0 %collective-permute-start.14 = (f32[8,288]{1,0:T(8,128)S(1)}, f32[8,288]{1,0:T(8,128)S(1)}, u32[]{:S(2)}, u32[]{:S(2)}) collective-permute-start(f32[8,288]{1,0:T(8,128)S(1)} %pad_maximum_fusion.4), channel_id=1, source_target_pairs={{0,1},{1,0},{2,3},{3,2},{4,5},{5,4},{6,7},{7,6},{8,9},{9,8},{10,11... | collective-permute-start | bytes 27656 | tf_op jit(solution)/shard_map/ppermute | solution.py:237
  72.2 1.8 %collective-permute-done.14 = f32[8,288]{1,0:T(8,128)S(1)} collective-permute-done((f32[8,288]{1,0:T(8,128)S(1)}, f32[8,288]{1,0:T(8,128)S(1)}, u32[]{:S(2)}, u32[]{:S(2)}) %collective-permute-start.14) | collective-permute-done | bytes 9248 | tf_op jit(solution)/shard_map/ppermute | solution.py:237
  74.0 0.7 multiply_bitcast_fusion
  74.7 0.6 fusion.3
  (31 shorter events, 0.3 us)
Async XLA Ops:
  0.6 2.3 %copy-start.6 = (s32[256]{0:T(256)S(1)}, s32[256]{0:T(256)}, u32[]{:S(2)}) copy-start(s32[256]{0:T(256)} %param.7) | copy-start | bytes 3076
  0.6 6.7 %copy-start.5 = (f32[256,128]{1,0:T(8,128)S(1)}, f32[256,128]{1,0:T(8,128)}, u32[]{:S(2)}) copy-start(f32[256,128]{1,0:T(8,128)} %param.6) | copy-start | bytes 393220
  3.0 22.0 %copy-start = (f32[2,2048,128]{2,1,0:T(8,128)S(1)}, f32[2,2048,128]{2,1,0:T(8,128)}, u32[]{:S(2)}) copy-start(f32[2,2048,128]{2,1,0:T(8,128)} %g_ref.2) | copy-start | bytes 6291460
  3.0 1.3 %collective-permute-start = (s32[256]{0:T(256)S(1)}, s32[256]{0:T(256)S(1)}, u32[]{:S(2)}, u32[]{:S(2)}) collective-permute-start(s32[256]{0:T(256)S(1)} %copy-done.6), channel_id=1, source_target_pairs={{0,4},{4,0},{8,12},{12,8},{1,5},{5,1},{9,13},{13,9},{2,6},{6,2},{1... | collective-permute-start | bytes 3080 | tf_op jit(solution)/shard_map/ppermute | solution.py:160
  4.3 20.6 %collective-permute-start.1 = (f32[1024,2048]{1,0:T(8,128)}, f32[1024,2048]{1,0:T(8,128)}, u32[]{:S(2)}, u32[]{:S(2)}) collective-permute-start(f32[1024,2048]{1,0:T(8,128)} %refs_0_.5), channel_id=1, source_target_pairs={{0,4},{4,0},{8,12},{12,8},{1,5},{5,1},{9,13},{13,9},{2,6},{6,2},{1... | collective-permute-start | bytes 25165832 | tf_op jit(solution)/shard_map/ppermute | solution.py:160
  4.6 34.1 %collective-permute-start.7 = (f32[2,1024,128]{2,1,0:T(8,128)}, f32[2,1024,128]{2,1,0:T(8,128)}, u32[]{:S(2)}, u32[]{:S(2)}) collective-permute-start(f32[2,1024,128]{2,1,0:T(8,128)} %shard_map.59), channel_id=1, source_target_pairs={{0,8},{4,12},{8,0},{12,4},{1,9},{5,13},{9,1},{13,5},{2,10},{6,14},... | collective-permute-start | bytes 3145736 | tf_op jit(solution)/shard_map/ppermute | solution.py:178
  7.4 7.5 %collective-permute-start.2 = (f32[258,128]{1,0:T(8,128)S(1)}, f32[258,128]{1,0:T(8,128)S(1)}, u32[]{:S(2)}, u32[]{:S(2)}) collective-permute-start(f32[258,128]{1,0:T(8,128)S(1)} %pad_maximum_fusion), channel_id=1, source_target_pairs={{0,1},{1,0},{2,3},{3,2},{4,5},{5,4},{6,7},{7,6},{8,9},{9,8},{10,11... | collective-permute-start | bytes 396296 | tf_op jit(solution)/shard_map/ppermute | solution.py:188
  9.0 13.2 %collective-permute-start.3 = (f32[258,128]{1,0:T(8,128)S(1)}, f32[258,128]{1,0:T(8,128)S(1)}, u32[]{:S(2)}, u32[]{:S(2)}) collective-permute-start(f32[258,128]{1,0:T(8,128)S(1)} %pad_maximum_fusion), channel_id=1, source_target_pairs={{0,2},{1,3},{2,0},{3,1},{4,6},{5,7},{6,4},{7,5},{8,10},{9,11},{10,... | collective-permute-start | bytes 396296 | tf_op jit(solution)/shard_map/ppermute | solution.py:188
  11.6 10.6 %collective-permute-start.4 = (f32[258,128]{1,0:T(8,128)S(1)}, f32[258,128]{1,0:T(8,128)S(1)}, u32[]{:S(2)}, u32[]{:S(2)}) collective-permute-start(f32[258,128]{1,0:T(8,128)S(1)} %pad_maximum_fusion), channel_id=1, source_target_pairs={{0,3},{1,2},{2,1},{3,0},{4,7},{5,6},{6,5},{7,4},{8,11},{9,10},{10,... | collective-permute-start | bytes 396296 | tf_op jit(solution)/shard_map/ppermute | solution.py:188
  22.3 2.7 %collective-permute-start.5 = (f32[1032,128]{1,0:T(8,128)S(1)}, f32[1032,128]{1,0:T(8,128)S(1)}, u32[]{:S(2)}, u32[]{:S(2)}) collective-permute-start(f32[1032,128]{1,0:T(8,128)S(1)} %constant_dynamic-update-slice_fusion.refs_2_), channel_id=1, source_target_pairs={{0,4},{4,0},{8,12},{12,8},{1,5},{5,1},{9,13},{13,9},{2,6},{6,2},{1... | collective-permute-start | bytes 1585160 | tf_op jit(solution)/shard_map/ppermute | solution.py:160
  24.4 22.4 %collective-permute-start.6 = (f32[2,512,128]{2,1,0:T(8,128)S(1)}, f32[2,512,128]{2,1,0:T(8,128)S(1)}, u32[]{:S(2)}, u32[]{:S(2)}) collective-permute-start(f32[2,512,128]{2,1,0:T(8,128)S(1)} %get-tuple-element.23), channel_id=1, source_target_pairs={{0,8},{4,12},{8,0},{12,4},{1,9},{5,13},{9,1},{13,5},{2,10},{6,14},... | collective-permute-start | bytes 1572872 | tf_op jit(solution)/shard_map/ppermute | solution.py:178
  35.8 1.4 %copy-start.3 = (f32[1024,512]{1,0:T(8,128)}, f32[1024,512]{1,0:T(8,128)S(1)}, u32[]{:S(2)}) copy-start(f32[1024,512]{1,0:T(8,128)S(1)} %get-tuple-element.20.refs_1_) | copy-start | bytes 6291460
  37.2 8.7 %copy-start.1 = (f32[1024,512]{1,0:T(8,128)}, f32[1024,512]{1,0:T(8,128)S(1)}, u32[]{:S(2)}) copy-start(f32[1024,512]{1,0:T(8,128)S(1)} %get-tuple-element.19.refs_0_) | copy-start | bytes 6291460
  37.2 15.9 %collective-permute-start.10 = (f32[2,256,128]{2,1,0:T(8,128)}, f32[2,256,128]{2,1,0:T(8,128)S(1)}, u32[]{:S(2)}, u32[]{:S(2)}) collective-permute-start(f32[2,256,128]{2,1,0:T(8,128)} %get-tuple-element.29), channel_id=1, source_target_pairs={{0,8},{4,12},{8,0},{12,4},{1,9},{5,13},{9,1},{13,5},{2,10},{6,14},... | collective-permute-start | bytes 786440 | tf_op jit(solution)/shard_map/ppermute | solution.py:178
  45.9 7.2 %copy-start.2 = (f32[1024,512]{1,0:T(8,128)S(1)}, f32[1024,512]{1,0:T(8,128)}, u32[]{:S(2)}) copy-start(f32[1024,512]{1,0:T(8,128)} %copy-done.1) | copy-start | bytes 6291460
  46.0 10.0 %collective-permute-start.9 = (f32[2,128,128]{2,1,0:T(8,128)}, f32[2,128,128]{2,1,0:T(8,128)}, u32[]{:S(2)}, u32[]{:S(2)}) collective-permute-start(f32[2,128,128]{2,1,0:T(8,128)} %get-tuple-element.27), channel_id=1, source_target_pairs={{0,8},{4,12},{8,0},{12,4},{1,9},{5,13},{9,1},{13,5},{2,10},{6,14},... | collective-permute-start | bytes 393224 | tf_op jit(solution)/shard_map/ppermute | solution.py:178
  51.6 6.1 %collective-permute-start.8 = (f32[2,128,128]{2,1,0:T(8,128)}, f32[2,128,128]{2,1,0:T(8,128)}, u32[]{:S(2)}, u32[]{:S(2)}) collective-permute-start(f32[2,128,128]{2,1,0:T(8,128)} %get-tuple-element.25), channel_id=1, source_target_pairs={{0,8},{4,12},{8,0},{12,4},{1,9},{5,13},{9,1},{13,5},{2,10},{6,14},... | collective-permute-start | bytes 393224 | tf_op jit(solution)/shard_map/ppermute | solution.py:178
  53.1 1.6 %copy-start.4 = (f32[1024,512]{1,0:T(8,128)S(1)}, f32[1024,512]{1,0:T(8,128)}, u32[]{:S(2)}) copy-start(f32[1024,512]{1,0:T(8,128)} %copy-done.3) | copy-start | bytes 6291460
  60.1 1.3 %collective-permute-start.11 = (f32[4,1040]{1,0:T(4,128)S(1)}, f32[4,1040]{1,0:T(4,128)S(1)}, u32[]{:S(2)}, u32[]{:S(2)}) collective-permute-start(f32[4,1040]{1,0:T(4,128)S(1)} %pad_maximum_fusion.2), channel_id=1, source_target_pairs={{0,4},{4,0},{8,12},{12,8},{1,5},{5,1},{9,13},{13,9},{2,6},{6,2},{1... | collective-permute-start | bytes 49928 | tf_op jit(solution)/shard_map/ppermute | solution.py:160
  61.5 3.7 %collective-permute-start.12 = (f32[8,32]{1,0:T(8,128)S(1)}, f32[8,32]{1,0:T(8,128)S(1)}, u32[]{:S(2)}, u32[]{:S(2)}) collective-permute-start(f32[8,32]{1,0:T(8,128)S(1)} %fusion.4), channel_id=1, source_target_pairs={{0,8},{4,12},{8,0},{12,4},{1,9},{5,13},{9,1},{13,5},{2,10},{6,14},... | collective-permute-start | bytes 3080 | tf_op jit(solution)/shard_map/ppermute | solution.py:229
  65.1 5.0 %collective-permute-start.13 = (f32[8,544]{1,0:T(8,128)S(1)}, f32[8,544]{1,0:T(8,128)S(1)}, u32[]{:S(2)}, u32[]{:S(2)}) collective-permute-start(f32[8,544]{1,0:T(8,128)S(1)} %pad_maximum_fusion.3), channel_id=1, source_target_pairs={{0,2},{1,3},{2,0},{3,1},{4,6},{5,7},{6,4},{7,5},{8,10},{9,11},{10,... | collective-permute-start | bytes 52232 | tf_op jit(solution)/shard_map/ppermute | solution.py:237
  70.2 3.8 %collective-permute-start.14 = (f32[8,288]{1,0:T(8,128)S(1)}, f32[8,288]{1,0:T(8,128)S(1)}, u32[]{:S(2)}, u32[]{:S(2)}) collective-permute-start(f32[8,288]{1,0:T(8,128)S(1)} %pad_maximum_fusion.4), channel_id=1, source_target_pairs={{0,1},{1,0},{2,3},{3,2},{4,5},{5,4},{6,7},{7,6},{8,9},{9,8},{10,11... | collective-permute-start | bytes 27656 | tf_op jit(solution)/shard_map/ppermute | solution.py:237
where the time goes:
time: 75.6 us; the launch traced here: 75.3 us
  Pallas kernels  31.9 us (42%)
  waiting for transfers between devices  18.5 us (24%)
  starting transfers between devices  18.4 us (24%)
  local copies, waits for them, and re-layouts  3.23 us (4%)
  other arithmetic  1.68 us (2%)
  between operations  0.97 us (1%)
    pallas_call x3, Pallas kernels, stream_scores(): pl.pallas_call(functools.partial(stream_kernel, first, staged), grid=(t /...  22.9 us
    ppermute x3, waiting for transfers between devices, per_device(): got = lax.ppermute(mine, 'width', pairs(nw, k)) if k else mine  10.3 us
    ppermute x5, starting transfers between devices, send(): return lax.ppermute(after(x, *others), 'blk', pairs(nb, j))  6.96 us
    ppermute x2, starting transfers between devices, per_device(): lax.ppermute(jnp.concatenate([give, doc], axis=1), 'width', pairs(nw, k))  5.26 us
    pallas_call x3, Pallas kernels, staged_scores(): pl.pallas_call(functools.partial(staged_kernel, start, first), in_specs=[...  4.71 us
    ppermute x3, starting transfers between devices, per_device(): got = lax.ppermute(mine, 'width', pairs(nw, k)) if k else mine  4.45 us
    pallas_call x2, Pallas kernels, cut(): pl.pallas_call(functools.partial(cut_kernel, pieces), in_specs=[HBM], out...  4.32 us
    ppermute x2, waiting for transfers between devices, per_device(): lax.ppermute(jnp.concatenate([give, doc], axis=1), 'width', pairs(nw, k))  3.55 us
  transfers between devices with their start and end apart: 15, of which 7 were waited for; matrix products, arithmetic and copies ran while one was open for 1% of the time, Pallas kernels for 37%

commit v1 on v0

--- a/solution.py
+++ b/solution.py
@@ -11,6 +11,9 @@
 LANES = 128
 F32, BF16 = jnp.float32, jnp.bfloat16
 TILE = 256
+LATE = 2
+Z_ORDER = 1
+MERGE = False
 PARTS = (2, 4, 8, 16, 16)
 VMEM = pl.BlockSpec(memory_space=pltpu.VMEM)
 HBM = pl.BlockSpec(memory_space=pltpu.HBM)
@@ -60,7 +63,7 @@
     ]
 
 
-def score_tile(a, weights, o, step):
+def project(a, weights, step):
     dot = functools.partial(jnp.dot, preferred_element_type=F32)
     p = None
     for i, (gh, gl) in enumerate(weights):
@@ -71,13 +74,92 @@
         else:
             part = dot(ah, gh) + dot(al, gh) + dot(ah, gl)
         p = part if p is None else p + part
+    return p
+
+
+def contract(p, o):
     r = o.shape[1]
     return [jnp.sum(p[:, q : q + r] * o, axis=1) for q in range(0, p.shape[1], r)]
 
 
-def stream_kernel(first, staged, *refs):
+def score_tile(a, weights, o, step):
+    return contract(project(a, weights, step), o)
+
+
+def project_kernel(staged, a_ref, g_ref, p_ref, stage_ref, high_ref, low_ref):
+    step = high_ref.shape[1]
+    n = a_ref.shape[1]
+
+    @pl.when(pl.program_id(0) == 0)
+    def _():
+        for k, (gh, gl) in enumerate(weigh(g_ref, step)):
+            high_ref[k] = gh
+            low_ref[k] = gl
+
+    a = a_ref[...]
+    here = pl.ds(pl.multiple_of(pl.program_id(0) * a.shape[0], a.shape[0]), a.shape[0])
+    p_ref[here, :] = project(a, [(high_ref.at[k], low_ref.at[k]) for k in range(n // step)], step)
+    stage_ref[here, :] = a[:, n - staged :]
+
+
+def own_projection(a, g, staged):
+    t = a.shape[0]
+    nq, n, r = g.shape
+    tile, step = min(t, TILE), min(n, 512)
+    return pl.pallas_call(
+        functools.partial(project_kernel, staged),
+        grid=(t // tile,),
+        in_specs=[pl.BlockSpec((tile, n), lambda i: (i, 0)), VMEM],
+        out_specs=[VMEM, VMEM],
+        out_shape=[jax.ShapeDtypeStruct((t, w), F32) for w in (nq * r, staged)],
+        scratch_shapes=[pltpu.VMEM((n // step, step, nq * r), BF16)] * 2,
+        compiler_params=PARAMS,
+        cost_estimate=COST,
+    )(in_hbm(a), g)
+
+
+def near_kernel(staged, a_ref, o_ref, oo_ref, p_ref, g_ref, s_ref, stage_ref, high_ref, low_ref):
+    tile, n = a_ref.shape
+    t = s_ref.shape[1] // 2
+    i = pl.program_id(0)
+    step = high_ref.shape[1]
+
+    @pl.when(i == 0)
+    def _():
+        s_ref[...] = jnp.zeros_like(s_ref)
+        for k, (gh, gl) in enumerate(weigh(g_ref, step)):
+            high_ref[k] = gh
+            low_ref[k] = gl
+
+    a = a_ref[...]
+    p = project(a, [(high_ref.at[k], low_ref.at[k]) for k in range(n // step)], step)
+    here = pl.ds(pl.multiple_of(i * tile, tile), tile)
+    there = pl.ds(pl.multiple_of(t + i * tile, tile), tile)
+    for at, p, o in ((here, p_ref[here, :], o_ref[here, :]), (there, p, oo_ref[here, :])):
+        for q, row in enumerate(contract(p, o)):
+            s_ref[q, at] = row
+    stage_ref[here, :] = a[:, n - staged :]
+
+
+def near_scores(rows, a, outgrads, p, g, staged):
+    t = a.shape[0]
+    nq, n, r = g.shape
+    tile, step = min(t, TILE), min(n, 512)
+    return pl.pallas_call(
+        functools.partial(near_kernel, staged),
+        grid=(t // tile,),
+        in_specs=[pl.BlockSpec((tile, n), lambda i: (i, 0)), VMEM, VMEM, VMEM, VMEM],
+        out_specs=[VMEM, VMEM],
+        out_shape=[jax.ShapeDtypeStruct((rows, 2 * t), F32), jax.ShapeDtypeStruct((t, staged), F32)],
+        scratch_shapes=[pltpu.VMEM((n // step, step, nq * r), BF16)] * 2,
+        compiler_params=PARAMS,
+        cost_estimate=COST,
+    )(in_hbm(a), *outgrads, p, g)
+
+
+def stream_kernel(first, *refs):
     a_refs, o_refs, refs = refs[:2], refs[2:4], refs[4:]
-    g_ref, prev_ref, s_ref, *stage_refs, high_ref, low_ref = refs
+    g_ref, prev_ref, s_ref, high_ref, low_ref = refs
     tile, n = a_refs[0].shape
     t = s_ref.shape[1] // 2
     i = pl.program_id(0)
@@ -94,33 +176,28 @@
     for h in range(2):
         a = a_refs[h][...]
         at = pl.multiple_of(h * t + i * tile, tile)
-        for q, row in enumerate(score_tile(a, weights, o_refs[h][...], step)):
+        o = o_refs[h][pl.ds(pl.multiple_of(i * tile, tile), tile), :]
+        for q, row in enumerate(score_tile(a, weights, o, step)):
             s_ref[first + q, pl.ds(at, tile)] += row
-        if staged:
-            stage_refs[h][...] = a[:, n - staged :]
-
-
-def stream_scores(s, activations, outgrads, g, start, first, staged=0):
+
+
+def stream_scores(s, activations, outgrads, g, start, first):
     t = activations[0].shape[0]
     nq, n, r = g.shape
-    tile = min(t, TILE)
+    tile = min(t, 512)
     step = min(n, 512)
     col = start // n
-    whole = pl.BlockSpec(s.shape, lambda i: (0, 0))
-    stage = jax.ShapeDtypeStruct((t, staged), F32)
-    out = pl.pallas_call(
-        functools.partial(stream_kernel, first, staged),
+    return pl.pallas_call(
+        functools.partial(stream_kernel, first),
         grid=(t // tile,),
         in_specs=[pl.BlockSpec((tile, n), lambda i: (i, col))] * 2
-        + [pl.BlockSpec((tile, r), lambda i: (i, 0))] * 2
-        + [pl.BlockSpec((nq, n, r), lambda i: (0, 0, 0), pipeline_mode=pl.Buffered(1)), whole],
-        out_specs=[whole] + [pl.BlockSpec((tile, staged), lambda i: (i, 0))] * (2 if staged else 0),
-        out_shape=[jax.ShapeDtypeStruct(s.shape, F32)] + [stage] * (2 if staged else 0),
+        + [VMEM] * 4,
+        out_specs=VMEM,
+        out_shape=jax.ShapeDtypeStruct(s.shape, F32),
         scratch_shapes=[pltpu.VMEM((n // step, step, nq * r), BF16)] * 2,
         compiler_params=PARAMS,
         cost_estimate=COST,
     )(*[in_hbm(a) for a in activations], *outgrads, g, s)
-    return out if staged else out[0]
 
 
 def staged_kernel(start, first, *refs):
@@ -149,6 +226,27 @@
     )(*stages, *outgrads, g, s)
 
 
+def finish_kernel(s_ref, doc_ref, scores_ref, doc_scores_ref):
+    docs = doc_scores_ref.shape[1]
+    scores_ref[...] = s_ref[...]
+    doc = doc_ref[...]
+    doc_scores_ref[...] = doc[:, :docs] / jnp.sqrt(doc[:, docs : 2 * docs])
+
+
+def finish(s, doc, docs):
+    return pl.pallas_call(
+        finish_kernel,
+        in_specs=[VMEM] * 2,
+        out_specs=[VMEM] * 2,
+        out_shape=[
+            jax.ShapeDtypeStruct(s.shape, F32),
+            jax.ShapeDtypeStruct((s.shape[0], docs), F32),
+        ],
+        compiler_params=PARAMS,
+        cost_estimate=COST,
+    )(s, doc)
+
+
 def per_device(a, g, o, ids):
     nb, nw = lax.axis_size("blk"), lax.axis_size("width")
     b, w = lax.axis_index("blk"), lax.axis_index("width")
@@ -169,7 +267,7 @@
             pieces.append((at, n))
         at += n
     cuts = cut(g, pieces[:1])
-    ids_other = to_core(after(ids, cuts[0]))
+    ids_other = to_core(ids)
     cuts += cut(after(g, ids_other), pieces[1:])
     sends = [(j, at, x) for j in range(2, nb, 2) for (at, _), x in zip(pieces, cuts)]
 
@@ -183,7 +281,9 @@
     rows = own // LANES
     flat = ids.astype(F32).reshape(rows, LANES)
     mine = after(jnp.concatenate([o, flat], axis=0), ids_other)
-    table = jnp.zeros((t + t // LANES, LANES), F32)
+    late = d - pieces[-LATE][0]
+    p, stage = own_projection(a, after(g, ids_other), late)
+    table = after(jnp.zeros((t + t // LANES, LANES), F32), p)
     for k in range(nw):
         got = lax.ppermute(mine, "width", pairs(nw, k)) if k else mine
         src = w ^ k
@@ -192,12 +292,12 @@
     other = to_core(table)
 
     both, outgrads = [a, a_other], [table, other]
-    s = jnp.zeros((nb // 2 * nq, 2 * t), F32)
-    late = d - pieces[-3][0]
-    s, *stages = stream_scores(s, both, outgrads, g, 0, 0, late)
+    s, stage_other = near_scores(nb // 2 * nq, a_other, outgrads, p, g, late)
+    stages = [stage, stage_other]
+    arrived.append(send(2, s))
     for i, (j, at, x) in enumerate(sends):
-        if i + 2 < len(sends):
-            arrived.append(send(i + 2, s))
+        if i + 3 < len(sends):
+            arrived.append(send(i + 3, s))
         first = j // 2 * nq
         if at < d - late:
             s = stream_scores(s, both, outgrads, arrived[i], at, first)
@@ -224,22 +324,33 @@
     s, doc = s[:, :t], s[:, t:]
     doc = jnp.concatenate([doc, jnp.broadcast_to(count[None, :], doc.shape)], axis=1)
 
-    k = 2
-    while k < nb:
-        doc = doc + lax.ppermute(doc, "blk", pairs(nb, k))
-        k *= 2
-    k = nw // 2
-    while k:
-        half = s.shape[1] // 2
-        low = (w & k) == 0
-        keep = jnp.where(low, s[:, :half], s[:, half:])
-        give = jnp.where(low, s[:, half:], s[:, :half])
-        got = lax.ppermute(jnp.concatenate([give, doc], axis=1), "width", pairs(nw, k))
-        s = keep + got[:, :half]
-        doc = doc + got[:, half:]
-        k //= 2
-    doc_scores = (doc[:, :docs] / jnp.sqrt(doc[:, docs:])).T
-    return (s.T, doc_scores)
+    swap = lambda x, y_bit, z_bit: lax.ppermute(
+        x,
+        ("blk", "width"),
+        [(i * nw + k, (i ^ y_bit) * nw + (k ^ z_bit)) for i in range(nb) for k in range(nw)],
+    )
+    blocks = {i: s[:, i * own : (i + 1) * own] for i in range(nw)}
+    y_bits = [1 << i for i in range(1, nb.bit_length() - 1)]
+    z_bits = [1 << i for i in range(nw.bit_length() - 1)][:: Z_ORDER]
+    for y_bit in y_bits[:-1]:
+        doc = doc + swap(doc, y_bit, 0)
+    for z_bit in z_bits:
+        low = (w & z_bit) == 0
+        at = [i for i in blocks if not i & z_bit]
+        give = [jnp.where(low, blocks[i | z_bit], blocks[i]) for i in at]
+        keep = [jnp.where(low, blocks[i], blocks[i | z_bit]) for i in at]
+        if z_bit == z_bits[0] and MERGE:
+            cross, up = swap(doc, y_bits[-1], z_bit), swap(doc, y_bits[-1], 0)
+        elif z_bit == z_bits[0]:
+            doc = doc + swap(doc, y_bits[-1], 0)
+        got = swap(jnp.concatenate(give + [doc], axis=1), 0, z_bit)
+        blocks = {i: x + got[:, n * own : (n + 1) * own] for n, (i, x) in enumerate(zip(at, keep))}
+        side = got[:, len(at) * own :]
+        if z_bit == z_bits[0] and MERGE:
+            doc, side = doc + up, side + cross
+        doc = doc + side
+    scores, doc_scores = finish(blocks[0], doc, docs)
+    return (scores.T, doc_scores.T)
 
 
 def solution(mesh):

time: 75.6 us -> 69.9 us (0.925)
  waiting for transfers between devices: 18.5 us -> 10.7 us
  Pallas kernels: 31.9 us -> 34.5 us
  local copies, waits for them, and re-layouts: 3.23 us -> 1.85 us
    ppermute x3, waiting for transfers between devices: 10.3 us -> 1.92 us  [per_device(): got = lax.ppermute(mine, 'width', pairs(nw, k)) if k else mine]
    pallas_call x3 -> x6, Pallas kernels: 22.9 us -> 28.4 us  [the longest x3 14.1 us: stream_scores(): pl.pallas_call(functools.partial(stream_kernel, first), grid=(t // tile,)...]
    pallas_call x3 -> x2, Pallas kernels: 4.71 us -> 1.73 us  [staged_scores(): pl.pallas_call(functools.partial(staged_kernel, start, first), in_specs=[...]
    unnamed x14 -> x12, local copies, waits for them, and re-layouts: 2.99 us -> 1.61 us
    transpose x2 -> x0, other arithmetic: 1.27 us -> none  [the longest x1 0.67 us: per_device(): doc_scores = (doc[:, :docs] / jnp.sqrt(doc[:, docs:])).T]
    ppermute x5, waiting for transfers between devices: 0.01 us -> 1.18 us  [send(): return lax.ppermute(after(x, *others), 'blk', pairs(nb, j))]
    concatenate x1, other arithmetic: 0.01 us -> 0.91 us  [per_device(): mine = after(jnp.concatenate([o, flat], axis=0), ids_other)]
    ppermute x3, waiting for transfers between devices: 6.43 us -> 5.63 us  [per_device(): lax.ppermute(x, ('blk', 'width'), [(i * nw + k, (i ^ y_bit) * nw + (k ^ z...]
  transfers between devices with their start and end apart: 15 -> 15, of which waited for: 7 -> 7; matrix products, arithmetic and copies ran while one was open for 1% -> 3% of each run, Pallas kernels for 37% -> 47%
where the time goes in v1:
time: 69.9 us; the launch traced here: 69.6 us
  Pallas kernels  34.5 us (49%)
  starting transfers between devices  19 us (27%)
  waiting for transfers between devices  10.7 us (15%)
  other arithmetic  1.98 us (3%)
  local copies, waits for them, and re-layouts  1.85 us (3%)
  between operations  0.98 us (1%)
    pallas_call x3, Pallas kernels, stream_scores(): pl.pallas_call(functools.partial(stream_kernel, first), grid=(t // tile,)...  14.1 us
    ppermute x5, starting transfers between devices, send(): return lax.ppermute(after(x, *others), 'blk', pairs(nb, j))  7.01 us
    pallas_call x1, Pallas kernels, near_scores(): pl.pallas_call(functools.partial(near_kernel, staged), grid=(t // tile,),...  6.94 us
    pallas_call x1, Pallas kernels, own_projection(): pl.pallas_call(functools.partial(project_kernel, staged), grid=(t // tile...  6.7 us
    ppermute x3, starting transfers between devices, per_device(): lax.ppermute(x, ('blk', 'width'), [(i * nw + k, (i ^ y_bit) * nw + (k ^ z...  6.54 us
    ppermute x3, waiting for transfers between devices, per_device(): lax.ppermute(x, ('blk', 'width'), [(i * nw + k, (i ^ y_bit) * nw + (k ^ z...  5.63 us
    ppermute x3, starting transfers between devices, per_device(): got = lax.ppermute(mine, 'width', pairs(nw, k)) if k else mine  4.45 us
    pallas_call x2, Pallas kernels, cut(): pl.pallas_call(functools.partial(cut_kernel, pieces), in_specs=[HBM], out...  4.31 us
  transfers between devices with their start and end apart: 15, of which 7 were waited for; matrix products, arithmetic and copies ran while one was open for 3% of the time, Pallas kernels for 47%

profile of v1, /device:TPU:0, one launch (start us, length us, event | category | flops | bytes accessed | tf_op | source)
XLA Modules:
  0.0 69.6 jit_solution(17749123323714315377)
XLA Ops:
  0.6 0.0 copy-start.1
  0.6 0.5 collective-permute-start
  1.2 1.0 %collective-permute-done = s32[256]{0:T(256)S(1)} collective-permute-done((s32[256]{0:T(256)}, s32[256]{0:T(256)S(1)}, u32[]{:S(2)}, u32[]{:S(2)}) %collective-permute-start) | collective-permute-done | bytes 1056 | tf_op jit(solution)/shard_map/ppermute | solution.py:258
  2.2 0.3 collective-permute-start.1
  2.5 2.2 %shard_map.62 = f32[2,1024,128]{2,1,0:T(8,128)} custom-call(f32[2,2048,128]{2,1,0:T(8,128)} %g_ref.5), custom_call_target="tpu_custom_call" | custom-call | flops 1 | bytes 1 | tf_op jit(solution)/shard_map/pallas_call | solution.py:47
  4.7 2.8 %collective-permute-start.6 = (f32[2,1024,128]{2,1,0:T(8,128)}, f32[2,1024,128]{2,1,0:T(8,128)}, u32[]{:S(2)}, u32[]{:S(2)}) collective-permute-start(f32[2,1024,128]{2,1,0:T(8,128)} %shard_map.62), channel_id=1, source_target_pairs={{0,8},{4,12},{8,0},{12,4},{1,9},{5,13},{9,1},{13,5},{2,10},{6,14},... | collective-permute-start | bytes 3145736 | tf_op jit(solution)/shard_map/ppermute | solution.py:276
  7.5 0.7 fusion.6
  8.2 0.9 %pad_maximum_fusion = f32[258,128]{1,0:T(8,128)S(1)} fusion(f32[2,128]{1,0:T(2,128)S(1)} %get-tuple-element.50, f32[256,128]{1,0:T(8,128)} %param.6), kind=kLoop, calls=%fused_computation.3 | loop fusion | flops 33024 | bytes 264192 | tf_op jit(solution)/shard_map/concatenate | solution.py:283
  9.1 1.6 %collective-permute-start.2 = (f32[258,128]{1,0:T(8,128)S(1)}, f32[258,128]{1,0:T(8,128)S(1)}, u32[]{:S(2)}, u32[]{:S(2)}) collective-permute-start(f32[258,128]{1,0:T(8,128)S(1)} %pad_maximum_fusion), channel_id=1, source_target_pairs={{0,1},{1,0},{2,3},{3,2},{4,5},{5,4},{6,7},{7,6},{8,9},{9,8},{10,11... | collective-permute-start | bytes 396296 | tf_op jit(solution)/shard_map/ppermute | solution.py:288
  10.7 2.6 %collective-permute-start.3 = (f32[258,128]{1,0:T(8,128)S(1)}, f32[258,128]{1,0:T(8,128)S(1)}, u32[]{:S(2)}, u32[]{:S(2)}) collective-permute-start(f32[258,128]{1,0:T(8,128)S(1)} %pad_maximum_fusion), channel_id=1, source_target_pairs={{0,2},{1,3},{2,0},{3,1},{4,6},{5,7},{6,4},{7,5},{8,10},{9,11},{10,... | collective-permute-start | bytes 396296 | tf_op jit(solution)/shard_map/ppermute | solution.py:288
  13.3 0.2 collective-permute-start.4
  13.6 0.0 copy-start
  13.6 1.6 %copy-done = f32[2,2048,128]{2,1,0:T(8,128)S(1)} copy-done((f32[2,2048,128]{2,1,0:T(8,128)S(1)}, f32[2,2048,128]{2,1,0:T(8,128)}, u32[]{:S(2)}) %copy-start) | copy-done | bytes 2097176
  15.2 6.7 %shard_map.59 = (f32[1024,256]{1,0:T(8,128)S(1)}, f32[1024,256]{1,0:T(8,128)S(1)}) custom-call(f32[1024,2048]{1,0:T(8,128)} %refs_0_.5, f32[2,2048,128]{2,1,0:T(8,128)S(1)} %copy-done), custom_call_target="tpu_custom_call" | custom-call | flops 1 | bytes 1 | tf_op jit(solution)/shard_map/pallas_call | solution.py:109
  21.9 0.0 copy-start.2
  22.0 0.0 collective-permute-done.2
  22.0 1.9 %collective-permute-done.3 = f32[258,128]{1,0:T(8,128)S(1)} collective-permute-done((f32[258,128]{1,0:T(8,128)S(1)}, f32[258,128]{1,0:T(8,128)S(1)}, u32[]{:S(2)}, u32[]{:S(2)}) %collective-permute-start.3) | collective-permute-done | bytes 132128 | tf_op jit(solution)/shard_map/ppermute | solution.py:288
  24.0 0.0 collective-permute-done.4
  24.0 0.1 collective-permute-start.5
  24.1 2.1 %shard_map.61 = (f32[2,512,128]{2,1,0:T(8,128)}, f32[2,256,128]{2,1,0:T(8,128)S(1)}, f32[2,128,128]{2,1,0:T(8,128)}, f32[2,128,128]{2,1,0:T(8,128)S(1)}) custom-call(f32[2,2048,128]{2,1,0:T(8,128)} %g_ref.5), custom_call_target="tpu_custom_call" | custom-call | flops 1 | bytes 1 | tf_op jit(solution)/shard_map/pallas_call | solution.py:47
  26.2 0.6 collective-permute-start.10
  26.8 0.0 collective-permute-done.5.oo_ref.refs_3_
  26.8 0.0 collective-permute-done.1.a_ref.refs_1_
  26.8 0.0 copy-done.1
  26.8 6.9 %shard_map.60 = (f32[4,2048]{1,0:T(4,128)S(1)}, f32[1024,256]{1,0:T(8,128)S(1)}) custom-call(f32[1024,2048]{1,0:T(8,128)} %collective-permute-done.1.a_ref.refs_1_, f32[1032,128]{1,0:T(8,128)S(1)} %constant_dynamic-update-slice_fusion.o_ref.refs_2_, f32[1032,128]{1,0:T(8,128)S(1)} %collective-permute-done.5.oo_ref.refs_3_, ...), custom_call_target="tpu_custom_call" | custom-call | flops 1 | bytes 1 | tf_op jit(solution)/shard_map/pallas_call | solution.py:148
  33.7 0.0 copy-start.4
  33.7 1.6 %collective-permute-start.9 = (f32[2,256,128]{2,1,0:T(8,128)S(1)}, f32[2,256,128]{2,1,0:T(8,128)S(1)}, u32[]{:S(2)}, u32[]{:S(2)}) collective-permute-start(f32[2,256,128]{2,1,0:T(8,128)S(1)} %get-tuple-element.32), channel_id=1, source_target_pairs={{0,8},{4,12},{8,0},{12,4},{1,9},{5,13},{9,1},{13,5},{2,10},{6,14},... | collective-permute-start | bytes 786440 | tf_op jit(solution)/shard_map/ppermute | solution.py:276
  35.3 0.5 collective-permute-start.8
  35.8 0.0 collective-permute-done.6.refs_4_
  35.8 6.8 %shard_map.63.refs_5_ = f32[4,2048]{1,0:T(4,128)S(1)} custom-call(f32[1024,2048]{1,0:T(8,128)} %refs_0_.5, f32[1024,2048]{1,0:T(8,128)} %collective-permute-done.1.a_ref.refs_1_, f32[1032,128]{1,0:T(8,128)S(1)} %constant_dynamic-update-slice_fusion.o_ref.refs_2_, f32[1032,128]{1,0:T(8,128)S(1)} %collective-permute-done.5.oo_ref.refs_3_, ...), custom_call_target="tpu_custom_call" | custom-call | flops 1 | bytes 1 | tf_op jit(solution)/shard_map/pallas_call | solution.py:190
  42.6 0.0 copy-done.2
  42.6 0.0 copy-done.4
  42.6 1.6 %collective-permute-start.7 = (f32[2,128,128]{2,1,0:T(8,128)S(1)}, f32[2,128,128]{2,1,0:T(8,128)S(1)}, u32[]{:S(2)}, u32[]{:S(2)}) collective-permute-start(f32[2,128,128]{2,1,0:T(8,128)S(1)} %get-tuple-element.28), channel_id=1, source_target_pairs={{0,8},{4,12},{8,0},{12,4},{1,9},{5,13},{9,1},{13,5},{2,10},{6,14},... | collective-permute-start | bytes 393224 | tf_op jit(solution)/shard_map/ppermute | solution.py:276
  44.2 0.1 convert_reduce_fusion.1
  44.4 0.0 collective-permute-done.10.refs_4_
  44.4 4.3 %shard_map.64.refs_5_ = f32[4,2048]{1,0:T(4,128)S(1)} custom-call(f32[1024,2048]{1,0:T(8,128)} %refs_0_.5, f32[1024,2048]{1,0:T(8,128)} %collective-permute-done.1.a_ref.refs_1_, f32[1032,128]{1,0:T(8,128)S(1)} %constant_dynamic-update-slice_fusion.o_ref.refs_2_, f32[1032,128]{1,0:T(8,128)S(1)} %collective-permute-done.5.oo_ref.refs_3_, ...), custom_call_target="tpu_custom_call" | custom-call | flops 1 | bytes 1 | tf_op jit(solution)/shard_map/pallas_call | solution.py:190
  48.7 0.0 copy-start.3
  48.7 0.0 copy-start.5
  48.7 0.0 collective-permute-done.9.refs_4_
  48.7 3.1 %shard_map.65.refs_5_ = f32[4,2048]{1,0:T(4,128)S(1)} custom-call(f32[1024,2048]{1,0:T(8,128)} %refs_0_.5, f32[1024,2048]{1,0:T(8,128)} %collective-permute-done.1.a_ref.refs_1_, f32[1032,128]{1,0:T(8,128)S(1)} %constant_dynamic-update-slice_fusion.o_ref.refs_2_, f32[1032,128]{1,0:T(8,128)S(1)} %collective-permute-done.5.oo_ref.refs_3_, ...), custom_call_target="tpu_custom_call" | custom-call | flops 1 | bytes 1 | tf_op jit(solution)/shard_map/pallas_call | solution.py:190
  51.8 0.0 collective-permute-done.8.refs_4_
  51.8 0.0 copy-done.3
  51.8 0.0 copy-done.5
  51.8 0.9 %shard_map.66.refs_5_ = f32[4,2048]{1,0:T(4,128)S(1)} custom-call(f32[1024,256]{1,0:T(8,128)S(1)} %copy-done.3, f32[1024,256]{1,0:T(8,128)S(1)} %copy-done.5, f32[1032,128]{1,0:T(8,128)S(1)} %constant_dynamic-update-slice_fusion.o_ref.refs_2_, f32[1032,128]{1,0:T(8,128)S(1)} %collective-permute-done.5.oo_ref.refs_3_, ...), custom_call_target="tpu_custom_call" | custom-call | flops 1 | bytes 1 | tf_op jit(solution)/shard_map/pallas_call | solution.py:219
  52.7 1.2 %collective-permute-done.7.refs_4_ = f32[2,128,128]{2,1,0:T(8,128)S(1)} collective-permute-done((f32[2,128,128]{2,1,0:T(8,128)S(1)}, f32[2,128,128]{2,1,0:T(8,128)S(1)}, u32[]{:S(2)}, u32[]{:S(2)}) %collective-permute-start.7) | collective-permute-done | bytes 131104 | tf_op jit(solution)/shard_map/ppermute | solution.py:276
  53.8 0.9 %shard_map.67 = f32[4,2048]{1,0:T(4,128)S(1)} custom-call(f32[1024,256]{1,0:T(8,128)S(1)} %copy-done.3, f32[1024,256]{1,0:T(8,128)S(1)} %copy-done.5, f32[1032,128]{1,0:T(8,128)S(1)} %constant_dynamic-update-slice_fusion.o_ref.refs_2_, f32[1032,128]{1,0:T(8,128)S(1)} %collective-permute-done.5.oo_ref.refs_3_, ...), custom_call_target="tpu_custom_call" | custom-call | flops 1 | bytes 1 | tf_op jit(solution)/shard_map/pallas_call | solution.py:219
  54.7 0.6 fusion
  55.3 0.1 collective-permute-start.11
  55.4 0.1 convert_reduce_fusion
  55.5 0.1 pad.6.clone
  55.6 1.0 %collective-permute-done.11 = f32[4,1040]{1,0:T(4,128)S(1)} collective-permute-done((f32[4,1040]{1,0:T(4,128)S(1)}, f32[4,1040]{1,0:T(4,128)S(1)}, u32[]{:S(2)}, u32[]{:S(2)}) %collective-permute-start.11) | collective-permute-done | bytes 16672 | tf_op jit(solution)/shard_map/ppermute | solution.py:258
  56.7 1.8 %collective-permute-start.12 = (f32[8,32]{1,0:T(8,128)S(1)}, f32[8,32]{1,0:T(8,128)S(1)}, u32[]{:S(2)}, u32[]{:S(2)}) collective-permute-start(f32[8,32]{1,0:T(8,128)S(1)} %fusion.3), channel_id=1, source_target_pairs={{0,8},{1,9},{2,10},{3,11},{4,12},{5,13},{6,14},{7,15},{8,0},{9,1},... | collective-permute-start | bytes 3080 | tf_op jit(solution)/shard_map/ppermute | solution.py:327
  58.5 1.9 %collective-permute-done.12 = f32[8,32]{1,0:T(8,128)S(1)} collective-permute-done((f32[8,32]{1,0:T(8,128)S(1)}, f32[8,32]{1,0:T(8,128)S(1)}, u32[]{:S(2)}, u32[]{:S(2)}) %collective-permute-start.12) | collective-permute-done | bytes 1056 | tf_op jit(solution)/shard_map/ppermute | solution.py:327
  60.4 1.9 %collective-permute-start.13 = (f32[8,544]{1,0:T(8,128)S(1)}, f32[8,544]{1,0:T(8,128)S(1)}, u32[]{:S(2)}, u32[]{:S(2)}) collective-permute-start(f32[8,544]{1,0:T(8,128)S(1)} %pad_maximum_fusion.3), channel_id=1, source_target_pairs={{0,1},{1,0},{2,3},{3,2},{4,5},{5,4},{6,7},{7,6},{8,9},{9,8},{10,11... | collective-permute-start | bytes 52232 | tf_op jit(solution)/shard_map/ppermute | solution.py:327
  62.2 2.0 %collective-permute-done.13 = f32[8,544]{1,0:T(8,128)S(1)} collective-permute-done((f32[8,544]{1,0:T(8,128)S(1)}, f32[8,544]{1,0:T(8,128)S(1)}, u32[]{:S(2)}, u32[]{:S(2)}) %collective-permute-start.13) | collective-permute-done | bytes 17440 | tf_op jit(solution)/shard_map/ppermute | solution.py:327
  64.2 2.9 %collective-permute-start.14 = (f32[8,288]{1,0:T(8,128)S(1)}, f32[8,288]{1,0:T(8,128)S(1)}, u32[]{:S(2)}, u32[]{:S(2)}) collective-permute-start(f32[8,288]{1,0:T(8,128)S(1)} %pad_maximum_fusion.4), channel_id=1, source_target_pairs={{0,2},{1,3},{2,0},{3,1},{4,6},{5,7},{6,4},{7,5},{8,10},{9,11},{10,... | collective-permute-start | bytes 27656 | tf_op jit(solution)/shard_map/ppermute | solution.py:327
  67.1 1.8 %collective-permute-done.14 = f32[8,288]{1,0:T(8,128)S(1)} collective-permute-done((f32[8,288]{1,0:T(8,128)S(1)}, f32[8,288]{1,0:T(8,128)S(1)}, u32[]{:S(2)}, u32[]{:S(2)}) %collective-permute-start.14) | collective-permute-done | bytes 9248 | tf_op jit(solution)/shard_map/ppermute | solution.py:327
  68.9 0.7 shard_map.68
  (28 shorter events, 0.3 us)
Async XLA Ops:
  0.6 26.1 %copy-start.1 = (f32[2,2048,128]{2,1,0:T(8,128)S(1)}, f32[2,2048,128]{2,1,0:T(8,128)}, u32[]{:S(2)}) copy-start(f32[2,2048,128]{2,1,0:T(8,128)} %g_ref.5) | copy-start | bytes 6291460
  0.6 1.5 %collective-permute-start = (s32[256]{0:T(256)}, s32[256]{0:T(256)S(1)}, u32[]{:S(2)}, u32[]{:S(2)}) collective-permute-start(s32[256]{0:T(256)} %param.7), channel_id=1, source_target_pairs={{0,4},{4,0},{8,12},{12,8},{1,5},{5,1},{9,13},{13,9},{2,6},{6,2},{1... | collective-permute-start | bytes 3080 | tf_op jit(solution)/shard_map/ppermute | solution.py:258
  2.2 24.6 %collective-permute-start.1 = (f32[1024,2048]{1,0:T(8,128)}, f32[1024,2048]{1,0:T(8,128)}, u32[]{:S(2)}, u32[]{:S(2)}) collective-permute-start(f32[1024,2048]{1,0:T(8,128)} %refs_0_.5), channel_id=1, source_target_pairs={{0,4},{4,0},{8,12},{12,8},{1,5},{5,1},{9,13},{13,9},{2,6},{6,2},{1... | collective-permute-start | bytes 25165832 | tf_op jit(solution)/shard_map/ppermute | solution.py:258
  4.7 31.1 %collective-permute-start.6 = (f32[2,1024,128]{2,1,0:T(8,128)}, f32[2,1024,128]{2,1,0:T(8,128)}, u32[]{:S(2)}, u32[]{:S(2)}) collective-permute-start(f32[2,1024,128]{2,1,0:T(8,128)} %shard_map.62), channel_id=1, source_target_pairs={{0,8},{4,12},{8,0},{12,4},{1,9},{5,13},{9,1},{13,5},{2,10},{6,14},... | collective-permute-start | bytes 3145736 | tf_op jit(solution)/shard_map/ppermute | solution.py:276
  9.1 12.9 %collective-permute-start.2 = (f32[258,128]{1,0:T(8,128)S(1)}, f32[258,128]{1,0:T(8,128)S(1)}, u32[]{:S(2)}, u32[]{:S(2)}) collective-permute-start(f32[258,128]{1,0:T(8,128)S(1)} %pad_maximum_fusion), channel_id=1, source_target_pairs={{0,1},{1,0},{2,3},{3,2},{4,5},{5,4},{6,7},{7,6},{8,9},{9,8},{10,11... | collective-permute-start | bytes 396296 | tf_op jit(solution)/shard_map/ppermute | solution.py:288
  10.7 13.2 %collective-permute-start.3 = (f32[258,128]{1,0:T(8,128)S(1)}, f32[258,128]{1,0:T(8,128)S(1)}, u32[]{:S(2)}, u32[]{:S(2)}) collective-permute-start(f32[258,128]{1,0:T(8,128)S(1)} %pad_maximum_fusion), channel_id=1, source_target_pairs={{0,2},{1,3},{2,0},{3,1},{4,6},{5,7},{6,4},{7,5},{8,10},{9,11},{10,... | collective-permute-start | bytes 396296 | tf_op jit(solution)/shard_map/ppermute | solution.py:288
  13.3 10.6 %collective-permute-start.4 = (f32[258,128]{1,0:T(8,128)S(1)}, f32[258,128]{1,0:T(8,128)S(1)}, u32[]{:S(2)}, u32[]{:S(2)}) collective-permute-start(f32[258,128]{1,0:T(8,128)S(1)} %pad_maximum_fusion), channel_id=1, source_target_pairs={{0,3},{1,2},{2,1},{3,0},{4,7},{5,6},{6,5},{7,4},{8,11},{9,10},{10,... | collective-permute-start | bytes 396296 | tf_op jit(solution)/shard_map/ppermute | solution.py:288
  13.6 1.6 %copy-start = (f32[2,2048,128]{2,1,0:T(8,128)S(1)}, f32[2,2048,128]{2,1,0:T(8,128)}, u32[]{:S(2)}) copy-start(f32[2,2048,128]{2,1,0:T(8,128)} %g_ref.5) | copy-start | bytes 6291460
  21.9 20.7 %copy-start.2 = (f32[1024,256]{1,0:T(8,128)}, f32[1024,256]{1,0:T(8,128)S(1)}, u32[]{:S(2)}) copy-start(f32[1024,256]{1,0:T(8,128)S(1)} %get-tuple-element.20.refs_0_) | copy-start | bytes 3145732
  24.0 2.8 %collective-permute-start.5 = (f32[1032,128]{1,0:T(8,128)S(1)}, f32[1032,128]{1,0:T(8,128)S(1)}, u32[]{:S(2)}, u32[]{:S(2)}) collective-permute-start(f32[1032,128]{1,0:T(8,128)S(1)} %constant_dynamic-update-slice_fusion.o_ref.refs_2_), channel_id=1, source_target_pairs={{0,4},{4,0},{8,12},{12,8},{1,5},{5,1},{9,13},{13,9},{2,6},{6,2},{1... | collective-permute-start | bytes 1585160 | tf_op jit(solution)/shard_map/ppermute | solution.py:258
  26.2 18.2 %collective-permute-start.10 = (f32[2,512,128]{2,1,0:T(8,128)}, f32[2,512,128]{2,1,0:T(8,128)}, u32[]{:S(2)}, u32[]{:S(2)}) collective-permute-start(f32[2,512,128]{2,1,0:T(8,128)} %get-tuple-element.33), channel_id=1, source_target_pairs={{0,8},{4,12},{8,0},{12,4},{1,9},{5,13},{9,1},{13,5},{2,10},{6,14},... | collective-permute-start | bytes 1572872 | tf_op jit(solution)/shard_map/ppermute | solution.py:276
  33.7 8.9 %copy-start.4 = (f32[1024,256]{1,0:T(8,128)}, f32[1024,256]{1,0:T(8,128)S(1)}, u32[]{:S(2)}) copy-start(f32[1024,256]{1,0:T(8,128)S(1)} %get-tuple-element.25.refs_1_) | copy-start | bytes 3145732
  33.7 15.0 %collective-permute-start.9 = (f32[2,256,128]{2,1,0:T(8,128)S(1)}, f32[2,256,128]{2,1,0:T(8,128)S(1)}, u32[]{:S(2)}, u32[]{:S(2)}) collective-permute-start(f32[2,256,128]{2,1,0:T(8,128)S(1)} %get-tuple-element.32), channel_id=1, source_target_pairs={{0,8},{4,12},{8,0},{12,4},{1,9},{5,13},{9,1},{13,5},{2,10},{6,14},... | collective-permute-start | bytes 786440 | tf_op jit(solution)/shard_map/ppermute | solution.py:276
  35.3 16.4 %collective-permute-start.8 = (f32[2,128,128]{2,1,0:T(8,128)}, f32[2,128,128]{2,1,0:T(8,128)S(1)}, u32[]{:S(2)}, u32[]{:S(2)}) collective-permute-start(f32[2,128,128]{2,1,0:T(8,128)} %get-tuple-element.30), channel_id=1, source_target_pairs={{0,8},{4,12},{8,0},{12,4},{1,9},{5,13},{9,1},{13,5},{2,10},{6,14},... | collective-permute-start | bytes 393224 | tf_op jit(solution)/shard_map/ppermute | solution.py:276
  42.6 11.2 %collective-permute-start.7 = (f32[2,128,128]{2,1,0:T(8,128)S(1)}, f32[2,128,128]{2,1,0:T(8,128)S(1)}, u32[]{:S(2)}, u32[]{:S(2)}) collective-permute-start(f32[2,128,128]{2,1,0:T(8,128)S(1)} %get-tuple-element.28), channel_id=1, source_target_pairs={{0,8},{4,12},{8,0},{12,4},{1,9},{5,13},{9,1},{13,5},{2,10},{6,14},... | collective-permute-start | bytes 393224 | tf_op jit(solution)/shard_map/ppermute | solution.py:276
  48.7 3.1 %copy-start.3 = (f32[1024,256]{1,0:T(8,128)S(1)}, f32[1024,256]{1,0:T(8,128)}, u32[]{:S(2)}) copy-start(f32[1024,256]{1,0:T(8,128)} %copy-done.2) | copy-start | bytes 3145732
  48.7 3.1 %copy-start.5 = (f32[1024,256]{1,0:T(8,128)S(1)}, f32[1024,256]{1,0:T(8,128)}, u32[]{:S(2)}) copy-start(f32[1024,256]{1,0:T(8,128)} %copy-done.4) | copy-start | bytes 3145732
  55.3 1.3 %collective-permute-start.11 = (f32[4,1040]{1,0:T(4,128)S(1)}, f32[4,1040]{1,0:T(4,128)S(1)}, u32[]{:S(2)}, u32[]{:S(2)}) collective-permute-start(f32[4,1040]{1,0:T(4,128)S(1)} %pad_maximum_fusion.2), channel_id=1, source_target_pairs={{0,4},{4,0},{8,12},{12,8},{1,5},{5,1},{9,13},{13,9},{2,6},{6,2},{1... | collective-permute-start | bytes 49928 | tf_op jit(solution)/shard_map/ppermute | solution.py:258
  56.7 3.7 %collective-permute-start.12 = (f32[8,32]{1,0:T(8,128)S(1)}, f32[8,32]{1,0:T(8,128)S(1)}, u32[]{:S(2)}, u32[]{:S(2)}) collective-permute-start(f32[8,32]{1,0:T(8,128)S(1)} %fusion.3), channel_id=1, source_target_pairs={{0,8},{1,9},{2,10},{3,11},{4,12},{5,13},{6,14},{7,15},{8,0},{9,1},... | collective-permute-start | bytes 3080 | tf_op jit(solution)/shard_map/ppermute | solution.py:327
  60.4 3.8 %collective-permute-start.13 = (f32[8,544]{1,0:T(8,128)S(1)}, f32[8,544]{1,0:T(8,128)S(1)}, u32[]{:S(2)}, u32[]{:S(2)}) collective-permute-start(f32[8,544]{1,0:T(8,128)S(1)} %pad_maximum_fusion.3), channel_id=1, source_target_pairs={{0,1},{1,0},{2,3},{3,2},{4,5},{5,4},{6,7},{7,6},{8,9},{9,8},{10,11... | collective-permute-start | bytes 52232 | tf_op jit(solution)/shard_map/ppermute | solution.py:327
  64.2 4.7 %collective-permute-start.14 = (f32[8,288]{1,0:T(8,128)S(1)}, f32[8,288]{1,0:T(8,128)S(1)}, u32[]{:S(2)}, u32[]{:S(2)}) collective-permute-start(f32[8,288]{1,0:T(8,128)S(1)} %pad_maximum_fusion.4), channel_id=1, source_target_pairs={{0,2},{1,3},{2,0},{3,1},{4,6},{5,7},{6,4},{7,5},{8,10},{9,11},{10,... | collective-permute-start | bytes 27656 | tf_op jit(solution)/shard_map/ppermute | solution.py:327

commit v2 on v1

--- a/solution.py
+++ b/solution.py
@@ -11,7 +11,6 @@
 LANES = 128
 F32, BF16 = jnp.float32, jnp.bfloat16
 TILE = 256
-LATE = 2
 Z_ORDER = 1
 MERGE = False
 PARTS = (2, 4, 8, 16, 16)
@@ -86,75 +85,74 @@
     return contract(project(a, weights, step), o)
 
 
-def project_kernel(staged, a_ref, g_ref, p_ref, stage_ref, high_ref, low_ref):
+def prepare(g_ref, lead_ref, refs):
+    high_ref, low_ref, lead_high_ref, lead_low_ref = refs
     step = high_ref.shape[1]
-    n = a_ref.shape[1]
 
     @pl.when(pl.program_id(0) == 0)
     def _():
         for k, (gh, gl) in enumerate(weigh(g_ref, step)):
             high_ref[k] = gh
             low_ref[k] = gl
-
+        lead_high_ref[...], lead_low_ref[...] = weigh(lead_ref, lead_ref.shape[1])[0]
+
+    weights = [(high_ref.at[k], low_ref.at[k]) for k in range(high_ref.shape[0])]
+    return weights, [(lead_high_ref, lead_low_ref)]
+
+
+def project_both(a, weights, lead_weights, at):
+    step, n = weights[0][0].shape[0], lead_weights[0][0].shape[0]
+    return project(a, weights, step), project(a[:, at : at + n], lead_weights, n)
+
+
+def own_kernel(at, cols, a_ref, g_ref, lead_ref, p_ref, lead_p_ref, stage_ref, *refs):
+    weights, lead_weights = prepare(g_ref, lead_ref, refs)
     a = a_ref[...]
     here = pl.ds(pl.multiple_of(pl.program_id(0) * a.shape[0], a.shape[0]), a.shape[0])
-    p_ref[here, :] = project(a, [(high_ref.at[k], low_ref.at[k]) for k in range(n // step)], step)
-    stage_ref[here, :] = a[:, n - staged :]
-
-
-def own_projection(a, g, staged):
+    p_ref[here, :], lead_p_ref[here, :] = project_both(a, weights, lead_weights, at)
+    stage_ref[here, :] = a[:, cols[0] : cols[1]]
+
+
+def other_kernel(
+    at, cols, a_ref, o_ref, oo_ref, p_ref, lead_p_ref, g_ref, lead_ref, s_ref, stage_ref, *refs
+):
+    weights, lead_weights = prepare(g_ref, lead_ref, refs)
+    a = a_ref[...]
+    tile = a.shape[0]
+    t = s_ref.shape[1] // 2
+    nq = g_ref.shape[0]
+    start = pl.program_id(0) * tile
+
+    @pl.when(pl.program_id(0) == 0)
+    def _():
+        s_ref[...] = jnp.zeros_like(s_ref)
+
+    here = pl.ds(pl.multiple_of(start, tile), tile)
+    there = pl.ds(pl.multiple_of(t + start, tile), tile)
+    own = p_ref[here, :], lead_p_ref[here, :]
+    other = project_both(a, weights, lead_weights, at)
+    for to, parts, o in ((here, own, o_ref[here, :]), (there, other, oo_ref[here, :])):
+        for i, p in enumerate(parts):
+            for q, row in enumerate(contract(p, o)):
+                s_ref[i * nq + q, to] = row
+    stage_ref[here, :] = a[:, cols[0] : cols[1]]
+
+
+def near_call(kernel, a, others, g, lead, out):
     t = a.shape[0]
     nq, n, r = g.shape
     tile, step = min(t, TILE), min(n, 512)
     return pl.pallas_call(
-        functools.partial(project_kernel, staged),
+        kernel,
         grid=(t // tile,),
-        in_specs=[pl.BlockSpec((tile, n), lambda i: (i, 0)), VMEM],
-        out_specs=[VMEM, VMEM],
-        out_shape=[jax.ShapeDtypeStruct((t, w), F32) for w in (nq * r, staged)],
-        scratch_shapes=[pltpu.VMEM((n // step, step, nq * r), BF16)] * 2,
-        compiler_params=PARAMS,
-        cost_estimate=COST,
-    )(in_hbm(a), g)
-
-
-def near_kernel(staged, a_ref, o_ref, oo_ref, p_ref, g_ref, s_ref, stage_ref, high_ref, low_ref):
-    tile, n = a_ref.shape
-    t = s_ref.shape[1] // 2
-    i = pl.program_id(0)
-    step = high_ref.shape[1]
-
-    @pl.when(i == 0)
-    def _():
-        s_ref[...] = jnp.zeros_like(s_ref)
-        for k, (gh, gl) in enumerate(weigh(g_ref, step)):
-            high_ref[k] = gh
-            low_ref[k] = gl
-
-    a = a_ref[...]
-    p = project(a, [(high_ref.at[k], low_ref.at[k]) for k in range(n // step)], step)
-    here = pl.ds(pl.multiple_of(i * tile, tile), tile)
-    there = pl.ds(pl.multiple_of(t + i * tile, tile), tile)
-    for at, p, o in ((here, p_ref[here, :], o_ref[here, :]), (there, p, oo_ref[here, :])):
-        for q, row in enumerate(contract(p, o)):
-            s_ref[q, at] = row
-    stage_ref[here, :] = a[:, n - staged :]
-
-
-def near_scores(rows, a, outgrads, p, g, staged):
-    t = a.shape[0]
-    nq, n, r = g.shape
-    tile, step = min(t, TILE), min(n, 512)
-    return pl.pallas_call(
-        functools.partial(near_kernel, staged),
-        grid=(t // tile,),
-        in_specs=[pl.BlockSpec((tile, n), lambda i: (i, 0)), VMEM, VMEM, VMEM, VMEM],
-        out_specs=[VMEM, VMEM],
-        out_shape=[jax.ShapeDtypeStruct((rows, 2 * t), F32), jax.ShapeDtypeStruct((t, staged), F32)],
-        scratch_shapes=[pltpu.VMEM((n // step, step, nq * r), BF16)] * 2,
-        compiler_params=PARAMS,
-        cost_estimate=COST,
-    )(in_hbm(a), *outgrads, p, g)
+        in_specs=[pl.BlockSpec((tile, n), lambda i: (i, 0))] + [VMEM] * (len(others) + 2),
+        out_specs=[VMEM] * len(out),
+        out_shape=[jax.ShapeDtypeStruct(shape, F32) for shape in out],
+        scratch_shapes=[pltpu.VMEM((n // step, step, nq * r), BF16)] * 2
+        + [pltpu.VMEM((lead.shape[1], nq * r), BF16)] * 2,
+        compiler_params=PARAMS,
+        cost_estimate=COST,
+    )(in_hbm(a), *others, g, lead)
 
 
 def stream_kernel(first, *refs):
@@ -266,23 +264,28 @@
         if at < d:
             pieces.append((at, n))
         at += n
+    pieces = pieces[-1:] + pieces[:-1]
     cuts = cut(g, pieces[:1])
-    ids_other = to_core(ids)
-    cuts += cut(after(g, ids_other), pieces[1:])
+    lead = lax.ppermute(cuts[0], "blk", pairs(nb, 2))
+    cuts += cut(after(g, cuts[0]), pieces[1:2])
+    a_other = to_core(after(a, cuts[0]))
+    cuts += cut(after(g, lead), pieces[2:])
+    at, last = pieces[0][0], pieces[-1]
+    cols = last[0], sum(last)
+    wide = (t, nq * r), (t, nq * r), (t, last[1])
+    a_own = after(a, lead, *cuts[2:])
+    p, lead_p, stage = near_call(functools.partial(own_kernel, at, cols), a_own, [], g, lead, wide)
     sends = [(j, at, x) for j in range(2, nb, 2) for (at, _), x in zip(pieces, cuts)]
 
     def send(i, *others):
         j, _, x = sends[i]
         return lax.ppermute(after(x, *others), "blk", pairs(nb, j))
 
-    arrived = [send(0), send(1)]
-    a_other = to_core(after(a, ids_other))
+    arrived = [lead, lax.ppermute(cuts[1], "blk", pairs(nb, 2)), send(2, lead)]
 
     rows = own // LANES
     flat = ids.astype(F32).reshape(rows, LANES)
-    mine = after(jnp.concatenate([o, flat], axis=0), ids_other)
-    late = d - pieces[-LATE][0]
-    p, stage = own_projection(a, after(g, ids_other), late)
+    mine = after(jnp.concatenate([o, flat], axis=0), lead)
     table = after(jnp.zeros((t + t // LANES, LANES), F32), p)
     for k in range(nw):
         got = lax.ppermute(mine, "width", pairs(nw, k)) if k else mine
@@ -292,22 +295,31 @@
     other = to_core(table)
 
     both, outgrads = [a, a_other], [table, other]
-    s, stage_other = near_scores(nb // 2 * nq, a_other, outgrads, p, g, late)
+    s, stage_other = near_call(
+        functools.partial(other_kernel, at, cols),
+        a_other,
+        [*outgrads, p, lead_p],
+        g,
+        lead,
+        ((nb // 2 * nq, 2 * t), wide[2]),
+    )
     stages = [stage, stage_other]
-    arrived.append(send(2, s))
+    arrived.append(send(3, s))
     for i, (j, at, x) in enumerate(sends):
-        if i + 3 < len(sends):
-            arrived.append(send(i + 3, s))
+        if i + 4 < len(sends):
+            arrived.append(send(i + 4, s))
         first = j // 2 * nq
-        if at < d - late:
+        if i == 0:
+            continue
+        if at == last[0]:
+            s = staged_scores(s, stages, outgrads, arrived[i], 0, first)
+        else:
             s = stream_scores(s, both, outgrads, arrived[i], at, first)
-        else:
-            s = staged_scores(s, stages, outgrads, arrived[i], at - (d - late), first)
 
     number = jnp.arange(docs, dtype=F32)
     marks = lambda x: (x.reshape(-1)[:, None] == number[None, :]).astype(F32)
-    count = jnp.sum(marks(flat), axis=0) + jnp.sum(marks(ids_other.astype(F32)), axis=0)
     onehot = marks(jnp.concatenate([table[t:], other[t:]], axis=0))
+    count = jnp.sum(onehot, axis=0) / nw
     doc = jnp.dot(s, onehot, precision=lax.Precision.HIGHEST, preferred_element_type=F32)
 
     keep = jnp.concatenate([s[:, :t], doc], axis=1)

time: 69.9 us -> 68.9 us (0.986)
  starting transfers between devices: 19 us -> 16 us
  waiting for transfers between devices: 10.7 us -> 12.2 us
  Pallas kernels: 34.5 us -> 35.5 us
    ppermute x5 -> x3, starting transfers between devices: 7.01 us -> 3.61 us  [send(): return lax.ppermute(after(x, *others), 'blk', pairs(nb, j))]
    ppermute x0 -> x2, starting transfers between devices: none -> 2.68 us  [the longest x1 2.6 us: per_device(): lead = lax.ppermute(cuts[0], 'blk', pairs(nb, 2))]
    ppermute x3, waiting for transfers between devices: 5.63 us -> 7.78 us  [per_device(): lax.ppermute(x, ('blk', 'width'), [(i * nw + k, (i ^ y_bit) * nw + (k ^ z...]
    ppermute x3, starting transfers between devices: 6.54 us -> 4.39 us  [per_device(): lax.ppermute(x, ('blk', 'width'), [(i * nw + k, (i ^ y_bit) * nw + (k ^ z...]
    ppermute x3, waiting for transfers between devices: 1.92 us -> 0.67 us  [per_device(): got = lax.ppermute(mine, 'width', pairs(nw, k)) if k else mine]
    pallas_call x2 -> x3, Pallas kernels: 4.31 us -> 5.44 us  [cut(): pl.pallas_call(functools.partial(cut_kernel, pieces), in_specs=[HBM], out...]
    ppermute x5 -> x3, waiting for transfers between devices: 1.18 us -> 2.3 us  [send(): return lax.ppermute(after(x, *others), 'blk', pairs(nb, j))]
    pallas_call x2, Pallas kernels: 13.6 us -> 14.6 us  [near_call(): pl.pallas_call(kernel, grid=(t // tile,), in_specs=[pl.BlockSpec((tile, n...]
  transfers between devices with their start and end apart: 15 -> 14, of which waited for: 7 -> 9; matrix products, arithmetic and copies ran while one was open for 3% -> 3% of each run, Pallas kernels for 47% -> 48%
where the time goes in v2:
time: 68.9 us; the launch traced here: 68.6 us
  Pallas kernels  35.5 us (52%)
  starting transfers between devices  16 us (23%)
  waiting for transfers between devices  12.2 us (18%)
  other arithmetic  1.92 us (3%)
  local copies, waits for them, and re-layouts  1.84 us (3%)
  between operations  0.92 us (1%)
    pallas_call x2, Pallas kernels, near_call(): pl.pallas_call(kernel, grid=(t // tile,), in_specs=[pl.BlockSpec((tile, n...  14.6 us
    pallas_call x3, Pallas kernels, stream_scores(): pl.pallas_call(functools.partial(stream_kernel, first), grid=(t // tile,)...  13.9 us
    ppermute x3, waiting for transfers between devices, per_device(): lax.ppermute(x, ('blk', 'width'), [(i * nw + k, (i ^ y_bit) * nw + (k ^ z...  7.78 us
    pallas_call x3, Pallas kernels, cut(): pl.pallas_call(functools.partial(cut_kernel, pieces), in_specs=[HBM], out...  5.44 us
    ppermute x3, starting transfers between devices, per_device(): got = lax.ppermute(mine, 'width', pairs(nw, k)) if k else mine  4.64 us
    ppermute x3, starting transfers between devices, per_device(): lax.ppermute(x, ('blk', 'width'), [(i * nw + k, (i ^ y_bit) * nw + (k ^ z...  4.39 us
    ppermute x3, starting transfers between devices, send(): return lax.ppermute(after(x, *others), 'blk', pairs(nb, j))  3.61 us
    ppermute x1, starting transfers between devices, per_device(): lead = lax.ppermute(cuts[0], 'blk', pairs(nb, 2))  2.6 us
  transfers between devices with their start and end apart: 14, of which 9 were waited for; matrix products, arithmetic and copies ran while one was open for 3% of the time, Pallas kernels for 48%

profile of v2, /device:TPU:0, one launch (start us, length us, event | category | flops | bytes accessed | tf_op | source)
XLA Modules:
  0.0 68.6 jit_solution(5008795381826820357)
XLA Ops:
  0.6 0.0 copy-start
  0.6 1.1 %shard_map.59 = f32[2,128,128]{2,1,0:T(8,128)S(1)} custom-call(f32[2,2048,128]{2,1,0:T(8,128)} %g_ref.7), custom_call_target="tpu_custom_call" | custom-call | flops 1 | bytes 1 | tf_op jit(solution)/shard_map/pallas_call | solution.py:46
  1.7 0.5 collective-permute-start.1
  2.2 2.6 %collective-permute-start = (f32[2,128,128]{2,1,0:T(8,128)S(1)}, f32[2,128,128]{2,1,0:T(8,128)S(1)}, u32[]{:S(2)}, u32[]{:S(2)}) collective-permute-start(f32[2,128,128]{2,1,0:T(8,128)S(1)} %shard_map.59), channel_id=1, source_target_pairs={{0,8},{4,12},{8,0},{12,4},{1,9},{5,13},{9,1},{13,5},{2,10},{6,14},... | collective-permute-start | bytes 393224 | tf_op jit(solution)/shard_map/ppermute | solution.py:269
  4.8 2.3 %shard_map.63 = f32[2,1024,128]{2,1,0:T(8,128)} custom-call(f32[2,2048,128]{2,1,0:T(8,128)} %g_ref.7), custom_call_target="tpu_custom_call" | custom-call | flops 1 | bytes 1 | tf_op jit(solution)/shard_map/pallas_call | solution.py:46
  7.1 0.1 collective-permute-start.9
  7.2 0.7 convert_bitcast_fusion
  7.9 0.9 %pad_maximum_fusion = f32[258,128]{1,0:T(8,128)S(1)} fusion(f32[2,128]{1,0:T(2,128)S(1)} %convert_bitcast_fusion, f32[256,128]{1,0:T(8,128)} %param.6), kind=kLoop, calls=%fused_computation | loop fusion | flops 33024 | bytes 264192 | tf_op jit(solution)/shard_map/concatenate | solution.py:288
  8.8 0.1 collective-permute-done.lead_ref
  8.9 2.1 %collective-permute-start.2 = (f32[258,128]{1,0:T(8,128)S(1)}, f32[258,128]{1,0:T(8,128)S(1)}, u32[]{:S(2)}, u32[]{:S(2)}) collective-permute-start(f32[258,128]{1,0:T(8,128)S(1)} %pad_maximum_fusion), channel_id=1, source_target_pairs={{0,1},{1,0},{2,3},{3,2},{4,5},{5,4},{6,7},{7,6},{8,9},{9,8},{10,11... | collective-permute-start | bytes 396296 | tf_op jit(solution)/shard_map/ppermute | solution.py:291
  11.0 2.6 %collective-permute-start.3 = (f32[258,128]{1,0:T(8,128)S(1)}, f32[258,128]{1,0:T(8,128)S(1)}, u32[]{:S(2)}, u32[]{:S(2)}) collective-permute-start(f32[258,128]{1,0:T(8,128)S(1)} %pad_maximum_fusion), channel_id=1, source_target_pairs={{0,2},{1,3},{2,0},{3,1},{4,6},{5,7},{6,4},{7,5},{8,10},{9,11},{10,... | collective-permute-start | bytes 396296 | tf_op jit(solution)/shard_map/ppermute | solution.py:291
  13.6 0.0 collective-permute-start.4
  13.6 2.1 %shard_map.60 = (f32[2,512,128]{2,1,0:T(8,128)}, f32[2,256,128]{2,1,0:T(8,128)}, f32[2,128,128]{2,1,0:T(8,128)S(1)}) custom-call(f32[2,2048,128]{2,1,0:T(8,128)} %g_ref.7), custom_call_target="tpu_custom_call" | custom-call | flops 1 | bytes 1 | tf_op jit(solution)/shard_map/pallas_call | solution.py:46
  15.6 0.0 copy-done
  15.6 6.9 %shard_map.61 = (f32[1024,256]{1,0:T(8,128)S(1)}, f32[1024,256]{1,0:T(8,128)S(1)}, f32[1024,128]{1,0:T(8,128)S(1)}) custom-call(f32[1024,2048]{1,0:T(8,128)} %refs_0_.5, f32[2,2048,128]{2,1,0:T(8,128)S(1)} %copy-done, f32[2,128,128]{2,1,0:T(8,128)S(1)} %collective-permute-done.lead_ref), custom_call_target="tpu_custom_call" | custom-call | flops 1 | bytes 1 | tf_op jit(solution)/shard_map/pallas_call | solution.py:145
  22.6 0.0 copy-start.1
  22.6 0.8 %copy-done.1 = f32[1024,128]{1,0:T(8,128)} copy-done((f32[1024,128]{1,0:T(8,128)}, f32[1024,128]{1,0:T(8,128)S(1)}, u32[]{:S(2)}) %copy-start.1) | copy-done | bytes 524312
  23.5 0.0 collective-permute-done.2
  23.5 0.7 collective-permute-done.3
  24.2 0.0 collective-permute-done.4
  24.2 0.1 collective-permute-start.5
  24.3 1.6 %collective-permute-start.8 = (f32[2,512,128]{2,1,0:T(8,128)}, f32[2,512,128]{2,1,0:T(8,128)}, u32[]{:S(2)}, u32[]{:S(2)}) collective-permute-start(f32[2,512,128]{2,1,0:T(8,128)} %get-tuple-element.36), channel_id=1, source_target_pairs={{0,8},{4,12},{8,0},{12,4},{1,9},{5,13},{9,1},{13,5},{2,10},{6,14},... | collective-permute-start | bytes 1572872 | tf_op jit(solution)/shard_map/ppermute | solution.py:282
  25.9 0.3 collective-permute-done.5.oo_ref.refs_3_
  26.2 0.0 collective-permute-done.1.a_ref.refs_1_
  26.2 7.7 %shard_map.62 = (f32[4,2048]{1,0:T(4,128)S(1)}, f32[1024,128]{1,0:T(8,128)S(1)}) custom-call(f32[1024,2048]{1,0:T(8,128)} %collective-permute-done.1.a_ref.refs_1_, f32[1032,128]{1,0:T(8,128)S(1)} %constant_dynamic-update-slice_fusion.o_ref.refs_2_, f32[1032,128]{1,0:T(8,128)S(1)} %collective-permute-done.5.oo_ref.refs_3_, ...), custom_call_target="tpu_custom_call" | custom-call | flops 1 | bytes 1 | tf_op jit(solution)/shard_map/pallas_call | solution.py:145
  33.9 0.0 copy-start.3
  34.0 0.8 %copy-done.3 = f32[1024,128]{1,0:T(8,128)} copy-done((f32[1024,128]{1,0:T(8,128)}, f32[1024,128]{1,0:T(8,128)S(1)}, u32[]{:S(2)}) %copy-start.3) | copy-done | bytes 524312
  34.7 1.5 %collective-permute-start.7 = (f32[2,256,128]{2,1,0:T(8,128)}, f32[2,256,128]{2,1,0:T(8,128)S(1)}, u32[]{:S(2)}, u32[]{:S(2)}) collective-permute-start(f32[2,256,128]{2,1,0:T(8,128)} %get-tuple-element.35), channel_id=1, source_target_pairs={{0,8},{4,12},{8,0},{12,4},{1,9},{5,13},{9,1},{13,5},{2,10},{6,14},... | collective-permute-start | bytes 786440 | tf_op jit(solution)/shard_map/ppermute | solution.py:282
  36.3 0.5 collective-permute-start.6
  36.8 0.1 convert_reduce_fusion
  36.9 0.0 collective-permute-done.9.refs_4_
  36.9 6.8 %shard_map.64.refs_5_ = f32[4,2048]{1,0:T(4,128)S(1)} custom-call(f32[1024,2048]{1,0:T(8,128)} %refs_0_.5, f32[1024,2048]{1,0:T(8,128)} %collective-permute-done.1.a_ref.refs_1_, f32[1032,128]{1,0:T(8,128)S(1)} %constant_dynamic-update-slice_fusion.o_ref.refs_2_, f32[1032,128]{1,0:T(8,128)S(1)} %collective-permute-done.5.oo_ref.refs_3_, ...), custom_call_target="tpu_custom_call" | custom-call | flops 1 | bytes 1 | tf_op jit(solution)/shard_map/pallas_call | solution.py:188
  43.7 1.1 %collective-permute-done.8.refs_4_ = f32[2,512,128]{2,1,0:T(8,128)} collective-permute-done((f32[2,512,128]{2,1,0:T(8,128)}, f32[2,512,128]{2,1,0:T(8,128)}, u32[]{:S(2)}, u32[]{:S(2)}) %collective-permute-start.8) | collective-permute-done | bytes 524320 | tf_op jit(solution)/shard_map/ppermute | solution.py:282
  44.8 4.2 %shard_map.65.refs_5_ = f32[4,2048]{1,0:T(4,128)S(1)} custom-call(f32[1024,2048]{1,0:T(8,128)} %refs_0_.5, f32[1024,2048]{1,0:T(8,128)} %collective-permute-done.1.a_ref.refs_1_, f32[1032,128]{1,0:T(8,128)S(1)} %constant_dynamic-update-slice_fusion.o_ref.refs_2_, f32[1032,128]{1,0:T(8,128)S(1)} %collective-permute-done.5.oo_ref.refs_3_, ...), custom_call_target="tpu_custom_call" | custom-call | flops 1 | bytes 1 | tf_op jit(solution)/shard_map/pallas_call | solution.py:188
  49.0 0.0 copy-start.2
  49.0 0.0 copy-start.4
  49.0 1.2 %collective-permute-done.7.refs_4_ = f32[2,256,128]{2,1,0:T(8,128)S(1)} collective-permute-done((f32[2,256,128]{2,1,0:T(8,128)}, f32[2,256,128]{2,1,0:T(8,128)S(1)}, u32[]{:S(2)}, u32[]{:S(2)}) %collective-permute-start.7) | collective-permute-done | bytes 262176 | tf_op jit(solution)/shard_map/ppermute | solution.py:282
  50.3 2.9 %shard_map.66.refs_5_ = f32[4,2048]{1,0:T(4,128)S(1)} custom-call(f32[1024,2048]{1,0:T(8,128)} %refs_0_.5, f32[1024,2048]{1,0:T(8,128)} %collective-permute-done.1.a_ref.refs_1_, f32[1032,128]{1,0:T(8,128)S(1)} %constant_dynamic-update-slice_fusion.o_ref.refs_2_, f32[1032,128]{1,0:T(8,128)S(1)} %collective-permute-done.5.oo_ref.refs_3_, ...), custom_call_target="tpu_custom_call" | custom-call | flops 1 | bytes 1 | tf_op jit(solution)/shard_map/pallas_call | solution.py:188
  53.2 0.0 collective-permute-done.6.refs_4_
  53.2 0.0 copy-done.2
  53.2 0.0 copy-done.4
  53.2 0.9 %shard_map.67 = f32[4,2048]{1,0:T(4,128)S(1)} custom-call(f32[1024,128]{1,0:T(8,128)S(1)} %copy-done.2, f32[1024,128]{1,0:T(8,128)S(1)} %copy-done.4, f32[1032,128]{1,0:T(8,128)S(1)} %constant_dynamic-update-slice_fusion.o_ref.refs_2_, f32[1032,128]{1,0:T(8,128)S(1)} %collective-permute-done.5.oo_ref.refs_3_, ...), custom_call_target="tpu_custom_call" | custom-call | flops 1 | bytes 1 | tf_op jit(solution)/shard_map/pallas_call | solution.py:217
  54.1 0.1 fusion
  54.2 0.1 pad_maximum_fusion.2
  54.3 0.1 collective-permute-start.10
  54.4 0.1 pad.6.clone
  54.5 1.1 %collective-permute-done.10 = f32[4,1040]{1,0:T(4,128)S(1)} collective-permute-done((f32[4,1040]{1,0:T(4,128)S(1)}, f32[4,1040]{1,0:T(4,128)S(1)}, u32[]{:S(2)}, u32[]{:S(2)}) %collective-permute-start.10) | collective-permute-done | bytes 16672 | tf_op jit(solution)/shard_map/ppermute | solution.py:256
  55.7 0.1 collective-permute-start.11
  55.8 3.6 %collective-permute-done.11 = f32[8,32]{1,0:T(8,128)S(1)} collective-permute-done((f32[8,32]{1,0:T(8,128)S(1)}, f32[8,32]{1,0:T(8,128)S(1)}, u32[]{:S(2)}, u32[]{:S(2)}) %collective-permute-start.11) | collective-permute-done | bytes 1056 | tf_op jit(solution)/shard_map/ppermute | solution.py:339
  59.4 1.6 %collective-permute-start.12 = (f32[8,544]{1,0:T(8,128)S(1)}, f32[8,544]{1,0:T(8,128)S(1)}, u32[]{:S(2)}, u32[]{:S(2)}) collective-permute-start(f32[8,544]{1,0:T(8,128)S(1)} %pad_maximum_fusion.3), channel_id=1, source_target_pairs={{0,1},{1,0},{2,3},{3,2},{4,5},{5,4},{6,7},{7,6},{8,9},{9,8},{10,11... | collective-permute-start | bytes 52232 | tf_op jit(solution)/shard_map/ppermute | solution.py:339
  61.0 2.2 %collective-permute-done.12 = f32[8,544]{1,0:T(8,128)S(1)} collective-permute-done((f32[8,544]{1,0:T(8,128)S(1)}, f32[8,544]{1,0:T(8,128)S(1)}, u32[]{:S(2)}, u32[]{:S(2)}) %collective-permute-start.12) | collective-permute-done | bytes 17440 | tf_op jit(solution)/shard_map/ppermute | solution.py:339
  63.2 2.6 %collective-permute-start.13 = (f32[8,288]{1,0:T(8,128)S(1)}, f32[8,288]{1,0:T(8,128)S(1)}, u32[]{:S(2)}, u32[]{:S(2)}) collective-permute-start(f32[8,288]{1,0:T(8,128)S(1)} %pad_maximum_fusion.4), channel_id=1, source_target_pairs={{0,2},{1,3},{2,0},{3,1},{4,6},{5,7},{6,4},{7,5},{8,10},{9,11},{10,... | collective-permute-start | bytes 27656 | tf_op jit(solution)/shard_map/ppermute | solution.py:339
  65.9 2.0 %collective-permute-done.13 = f32[8,288]{1,0:T(8,128)S(1)} collective-permute-done((f32[8,288]{1,0:T(8,128)S(1)}, f32[8,288]{1,0:T(8,128)S(1)}, u32[]{:S(2)}, u32[]{:S(2)}) %collective-permute-start.13) | collective-permute-done | bytes 9248 | tf_op jit(solution)/shard_map/ppermute | solution.py:339
  67.9 0.7 shard_map.68
  (26 shorter events, 0.3 us)
Async XLA Ops:
  0.6 15.0 %copy-start = (f32[2,2048,128]{2,1,0:T(8,128)S(1)}, f32[2,2048,128]{2,1,0:T(8,128)}, u32[]{:S(2)}) copy-start(f32[2,2048,128]{2,1,0:T(8,128)} %g_ref.7) | copy-start | bytes 6291460
  1.7 24.5 %collective-permute-start.1 = (f32[1024,2048]{1,0:T(8,128)}, f32[1024,2048]{1,0:T(8,128)}, u32[]{:S(2)}, u32[]{:S(2)}) collective-permute-start(f32[1024,2048]{1,0:T(8,128)} %refs_0_.5), channel_id=1, source_target_pairs={{0,4},{4,0},{8,12},{12,8},{1,5},{5,1},{9,13},{13,9},{2,6},{6,2},{1... | collective-permute-start | bytes 25165832 | tf_op jit(solution)/shard_map/ppermute | solution.py:256
  2.2 6.7 %collective-permute-start = (f32[2,128,128]{2,1,0:T(8,128)S(1)}, f32[2,128,128]{2,1,0:T(8,128)S(1)}, u32[]{:S(2)}, u32[]{:S(2)}) collective-permute-start(f32[2,128,128]{2,1,0:T(8,128)S(1)} %shard_map.59), channel_id=1, source_target_pairs={{0,8},{4,12},{8,0},{12,4},{1,9},{5,13},{9,1},{13,5},{2,10},{6,14},... | collective-permute-start | bytes 393224 | tf_op jit(solution)/shard_map/ppermute | solution.py:269
  7.1 29.8 %collective-permute-start.9 = (f32[2,1024,128]{2,1,0:T(8,128)}, f32[2,1024,128]{2,1,0:T(8,128)}, u32[]{:S(2)}, u32[]{:S(2)}) collective-permute-start(f32[2,1024,128]{2,1,0:T(8,128)} %shard_map.63), channel_id=1, source_target_pairs={{0,8},{4,12},{8,0},{12,4},{1,9},{5,13},{9,1},{13,5},{2,10},{6,14},... | collective-permute-start | bytes 3145736 | tf_op jit(solution)/shard_map/ppermute | solution.py:284
  8.9 14.5 %collective-permute-start.2 = (f32[258,128]{1,0:T(8,128)S(1)}, f32[258,128]{1,0:T(8,128)S(1)}, u32[]{:S(2)}, u32[]{:S(2)}) collective-permute-start(f32[258,128]{1,0:T(8,128)S(1)} %pad_maximum_fusion), channel_id=1, source_target_pairs={{0,1},{1,0},{2,3},{3,2},{4,5},{5,4},{6,7},{7,6},{8,9},{9,8},{10,11... | collective-permute-start | bytes 396296 | tf_op jit(solution)/shard_map/ppermute | solution.py:291
  11.0 13.2 %collective-permute-start.3 = (f32[258,128]{1,0:T(8,128)S(1)}, f32[258,128]{1,0:T(8,128)S(1)}, u32[]{:S(2)}, u32[]{:S(2)}) collective-permute-start(f32[258,128]{1,0:T(8,128)S(1)} %pad_maximum_fusion), channel_id=1, source_target_pairs={{0,2},{1,3},{2,0},{3,1},{4,6},{5,7},{6,4},{7,5},{8,10},{9,11},{10,... | collective-permute-start | bytes 396296 | tf_op jit(solution)/shard_map/ppermute | solution.py:291
  13.6 10.6 %collective-permute-start.4 = (f32[258,128]{1,0:T(8,128)S(1)}, f32[258,128]{1,0:T(8,128)S(1)}, u32[]{:S(2)}, u32[]{:S(2)}) collective-permute-start(f32[258,128]{1,0:T(8,128)S(1)} %pad_maximum_fusion), channel_id=1, source_target_pairs={{0,3},{1,2},{2,1},{3,0},{4,7},{5,6},{6,5},{7,4},{8,11},{9,10},{10,... | collective-permute-start | bytes 396296 | tf_op jit(solution)/shard_map/ppermute | solution.py:291
  22.6 0.8 %copy-start.1 = (f32[1024,128]{1,0:T(8,128)}, f32[1024,128]{1,0:T(8,128)S(1)}, u32[]{:S(2)}) copy-start(f32[1024,128]{1,0:T(8,128)S(1)} %get-tuple-element.26.refs_0_) | copy-start | bytes 1572868
  24.2 2.0 %collective-permute-start.5 = (f32[1032,128]{1,0:T(8,128)S(1)}, f32[1032,128]{1,0:T(8,128)S(1)}, u32[]{:S(2)}, u32[]{:S(2)}) collective-permute-start(f32[1032,128]{1,0:T(8,128)S(1)} %constant_dynamic-update-slice_fusion.o_ref.refs_2_), channel_id=1, source_target_pairs={{0,4},{4,0},{8,12},{12,8},{1,5},{5,1},{9,13},{13,9},{2,6},{6,2},{1... | collective-permute-start | bytes 1585160 | tf_op jit(solution)/shard_map/ppermute | solution.py:256
  24.3 20.4 %collective-permute-start.8 = (f32[2,512,128]{2,1,0:T(8,128)}, f32[2,512,128]{2,1,0:T(8,128)}, u32[]{:S(2)}, u32[]{:S(2)}) collective-permute-start(f32[2,512,128]{2,1,0:T(8,128)} %get-tuple-element.36), channel_id=1, source_target_pairs={{0,8},{4,12},{8,0},{12,4},{1,9},{5,13},{9,1},{13,5},{2,10},{6,14},... | collective-permute-start | bytes 1572872 | tf_op jit(solution)/shard_map/ppermute | solution.py:282
  33.9 0.8 %copy-start.3 = (f32[1024,128]{1,0:T(8,128)}, f32[1024,128]{1,0:T(8,128)S(1)}, u32[]{:S(2)}) copy-start(f32[1024,128]{1,0:T(8,128)S(1)} %get-tuple-element.32.refs_1_) | copy-start | bytes 1572868
  34.7 15.5 %collective-permute-start.7 = (f32[2,256,128]{2,1,0:T(8,128)}, f32[2,256,128]{2,1,0:T(8,128)S(1)}, u32[]{:S(2)}, u32[]{:S(2)}) collective-permute-start(f32[2,256,128]{2,1,0:T(8,128)} %get-tuple-element.35), channel_id=1, source_target_pairs={{0,8},{4,12},{8,0},{12,4},{1,9},{5,13},{9,1},{13,5},{2,10},{6,14},... | collective-permute-start | bytes 786440 | tf_op jit(solution)/shard_map/ppermute | solution.py:282
  36.3 16.9 %collective-permute-start.6 = (f32[2,128,128]{2,1,0:T(8,128)S(1)}, f32[2,128,128]{2,1,0:T(8,128)S(1)}, u32[]{:S(2)}, u32[]{:S(2)}) collective-permute-start(f32[2,128,128]{2,1,0:T(8,128)S(1)} %get-tuple-element.34), channel_id=1, source_target_pairs={{0,8},{4,12},{8,0},{12,4},{1,9},{5,13},{9,1},{13,5},{2,10},{6,14},... | collective-permute-start | bytes 393224 | tf_op jit(solution)/shard_map/ppermute | solution.py:282
  49.0 4.2 %copy-start.2 = (f32[1024,128]{1,0:T(8,128)S(1)}, f32[1024,128]{1,0:T(8,128)}, u32[]{:S(2)}) copy-start(f32[1024,128]{1,0:T(8,128)} %copy-done.1) | copy-start | bytes 1572868
  49.0 4.2 %copy-start.4 = (f32[1024,128]{1,0:T(8,128)S(1)}, f32[1024,128]{1,0:T(8,128)}, u32[]{:S(2)}) copy-start(f32[1024,128]{1,0:T(8,128)} %copy-done.3) | copy-start | bytes 1572868
  54.3 1.3 %collective-permute-start.10 = (f32[4,1040]{1,0:T(4,128)S(1)}, f32[4,1040]{1,0:T(4,128)S(1)}, u32[]{:S(2)}, u32[]{:S(2)}) collective-permute-start(f32[4,1040]{1,0:T(4,128)S(1)} %pad_maximum_fusion.2), channel_id=1, source_target_pairs={{0,4},{4,0},{8,12},{12,8},{1,5},{5,1},{9,13},{13,9},{2,6},{6,2},{1... | collective-permute-start | bytes 49928 | tf_op jit(solution)/shard_map/ppermute | solution.py:256
  55.7 3.7 %collective-permute-start.11 = (f32[8,32]{1,0:T(8,128)S(1)}, f32[8,32]{1,0:T(8,128)S(1)}, u32[]{:S(2)}, u32[]{:S(2)}) collective-permute-start(f32[8,32]{1,0:T(8,128)S(1)} %fusion.3), channel_id=1, source_target_pairs={{0,8},{1,9},{2,10},{3,11},{4,12},{5,13},{6,14},{7,15},{8,0},{9,1},... | collective-permute-start | bytes 3080 | tf_op jit(solution)/shard_map/ppermute | solution.py:339
  59.4 3.8 %collective-permute-start.12 = (f32[8,544]{1,0:T(8,128)S(1)}, f32[8,544]{1,0:T(8,128)S(1)}, u32[]{:S(2)}, u32[]{:S(2)}) collective-permute-start(f32[8,544]{1,0:T(8,128)S(1)} %pad_maximum_fusion.3), channel_id=1, source_target_pairs={{0,1},{1,0},{2,3},{3,2},{4,5},{5,4},{6,7},{7,6},{8,9},{9,8},{10,11... | collective-permute-start | bytes 52232 | tf_op jit(solution)/shard_map/ppermute | solution.py:339
  63.2 4.7 %collective-permute-start.13 = (f32[8,288]{1,0:T(8,128)S(1)}, f32[8,288]{1,0:T(8,128)S(1)}, u32[]{:S(2)}, u32[]{:S(2)}) collective-permute-start(f32[8,288]{1,0:T(8,128)S(1)} %pad_maximum_fusion.4), channel_id=1, source_target_pairs={{0,2},{1,3},{2,0},{3,1},{4,6},{5,7},{6,4},{7,5},{8,10},{9,11},{10,... | collective-permute-start | bytes 27656 | tf_op jit(solution)/shard_map/ppermute | solution.py:339

commit v3 on v2

--- a/solution.py
+++ b/solution.py
@@ -11,8 +11,6 @@
 LANES = 128
 F32, BF16 = jnp.float32, jnp.bfloat16
 TILE = 256
-Z_ORDER = 1
-MERGE = False
 PARTS = (2, 4, 8, 16, 16)
 VMEM = pl.BlockSpec(memory_space=pltpu.VMEM)
 HBM = pl.BlockSpec(memory_space=pltpu.HBM)
@@ -271,8 +269,8 @@
     a_other = to_core(after(a, cuts[0]))
     cuts += cut(after(g, lead), pieces[2:])
     at, last = pieces[0][0], pieces[-1]
-    cols = last[0], sum(last)
-    wide = (t, nq * r), (t, nq * r), (t, last[1])
+    cols = pieces[-2][0], sum(last)
+    wide = (t, nq * r), (t, nq * r), (t, cols[1] - cols[0])
     a_own = after(a, lead, *cuts[2:])
     p, lead_p, stage = near_call(functools.partial(own_kernel, at, cols), a_own, [], g, lead, wide)
     sends = [(j, at, x) for j in range(2, nb, 2) for (at, _), x in zip(pieces, cuts)]
@@ -311,8 +309,8 @@
         first = j // 2 * nq
         if i == 0:
             continue
-        if at == last[0]:
-            s = staged_scores(s, stages, outgrads, arrived[i], 0, first)
+        if cols[0] <= at < cols[1]:
+            s = staged_scores(s, stages, outgrads, arrived[i], at - cols[0], first)
         else:
             s = stream_scores(s, both, outgrads, arrived[i], at, first)
 
@@ -343,7 +341,7 @@
     )
     blocks = {i: s[:, i * own : (i + 1) * own] for i in range(nw)}
     y_bits = [1 << i for i in range(1, nb.bit_length() - 1)]
-    z_bits = [1 << i for i in range(nw.bit_length() - 1)][:: Z_ORDER]
+    z_bits = [1 << i for i in range(nw.bit_length() - 1)]
     for y_bit in y_bits[:-1]:
         doc = doc + swap(doc, y_bit, 0)
     for z_bit in z_bits:
@@ -351,14 +349,12 @@
         at = [i for i in blocks if not i & z_bit]
         give = [jnp.where(low, blocks[i | z_bit], blocks[i]) for i in at]
         keep = [jnp.where(low, blocks[i], blocks[i | z_bit]) for i in at]
-        if z_bit == z_bits[0] and MERGE:
+        if z_bit == z_bits[0]:
             cross, up = swap(doc, y_bits[-1], z_bit), swap(doc, y_bits[-1], 0)
-        elif z_bit == z_bits[0]:
-            doc = doc + swap(doc, y_bits[-1], 0)
         got = swap(jnp.concatenate(give + [doc], axis=1), 0, z_bit)
         blocks = {i: x + got[:, n * own : (n + 1) * own] for n, (i, x) in enumerate(zip(at, keep))}
         side = got[:, len(at) * own :]
-        if z_bit == z_bits[0] and MERGE:
+        if z_bit == z_bits[0]:
             doc, side = doc + up, side + cross
         doc = doc + side
     scores, doc_scores = finish(blocks[0], doc, docs)

time: 68.9 us -> 67.1 us (0.974)
  Pallas kernels: 35.5 us -> 33.7 us
  starting transfers between devices: 16 us -> 17.6 us
  other arithmetic: 1.92 us -> 0.55 us
    pallas_call x3 -> x2, Pallas kernels: 13.9 us -> 11.1 us  [stream_scores(): pl.pallas_call(functools.partial(stream_kernel, first), grid=(t // tile,)...]
    ppermute x3 -> x4, waiting for transfers between devices: 7.78 us -> 5.18 us  [per_device(): lax.ppermute(x, ('blk', 'width'), [(i * nw + k, (i ^ y_bit) * nw + (k ^ z...]
    ppermute x3 -> x4, starting transfers between devices: 4.39 us -> 6.09 us  [per_device(): lax.ppermute(x, ('blk', 'width'), [(i * nw + k, (i ^ y_bit) * nw + (k ^ z...]
    ppermute x1, waiting for transfers between devices: 0.09 us -> 1.61 us  [per_device(): lead = lax.ppermute(cuts[0], 'blk', pairs(nb, 2))]
    pallas_call x1 -> x2, Pallas kernels: 0.87 us -> 2.07 us  [staged_scores(): pl.pallas_call(functools.partial(staged_kernel, start, first), in_specs=[...]
    concatenate x1, other arithmetic: 0.91 us -> 0.01 us  [per_device(): mine = after(jnp.concatenate([o, flat], axis=0), lead)]
    unnamed x10 -> x14, local copies, waits for them, and re-layouts: 1.6 us -> 1.17 us
  transfers between devices with their start and end apart: 14 -> 15, of which waited for: 9 -> 11; matrix products, arithmetic and copies ran while one was open for 3% -> 1% of each run, Pallas kernels for 48% -> 47%
where the time goes in v3:
time: 67.1 us; the launch traced here: 66.8 us
  Pallas kernels  33.7 us (50%)
  starting transfers between devices  17.6 us (26%)
  waiting for transfers between devices  12.5 us (19%)
  local copies, waits for them, and re-layouts  1.34 us (2%)
  between operations  0.94 us (1%)
    pallas_call x2, Pallas kernels, near_call(): pl.pallas_call(kernel, grid=(t // tile,), in_specs=[pl.BlockSpec((tile, n...  14.7 us
    pallas_call x2, Pallas kernels, stream_scores(): pl.pallas_call(functools.partial(stream_kernel, first), grid=(t // tile,)...  11.1 us
    ppermute x4, starting transfers between devices, per_device(): lax.ppermute(x, ('blk', 'width'), [(i * nw + k, (i ^ y_bit) * nw + (k ^ z...  6.09 us
    pallas_call x3, Pallas kernels, cut(): pl.pallas_call(functools.partial(cut_kernel, pieces), in_specs=[HBM], out...  5.19 us
    ppermute x4, waiting for transfers between devices, per_device(): lax.ppermute(x, ('blk', 'width'), [(i * nw + k, (i ^ y_bit) * nw + (k ^ z...  5.18 us
    ppermute x3, starting transfers between devices, per_device(): got = lax.ppermute(mine, 'width', pairs(nw, k)) if k else mine  4.41 us
    ppermute x3, starting transfers between devices, send(): return lax.ppermute(after(x, *others), 'blk', pairs(nb, j))  3.61 us
    ppermute x3, waiting for transfers between devices, send(): return lax.ppermute(after(x, *others), 'blk', pairs(nb, j))  2.95 us
  transfers between devices with their start and end apart: 15, of which 11 were waited for; matrix products, arithmetic and copies ran while one was open for 1% of the time, Pallas kernels for 47%

profile of v3, /device:TPU:0, one launch (start us, length us, event | category | flops | bytes accessed | tf_op | source)
XLA Modules:
  0.0 66.8 jit_solution(3979526286305078540)
XLA Ops:
  0.6 0.9 %shard_map.59 = f32[2,128,128]{2,1,0:T(8,128)S(1)} custom-call(f32[2,2048,128]{2,1,0:T(8,128)} %g_ref.7), custom_call_target="tpu_custom_call" | custom-call | flops 1 | bytes 1 | tf_op jit(solution)/shard_map/pallas_call | solution.py:44
  1.6 0.0 copy-start.6
  1.6 0.0 copy-start.5
  1.6 0.0 copy-start
  1.6 0.5 collective-permute-start.1
  2.1 2.6 %collective-permute-start = (f32[2,128,128]{2,1,0:T(8,128)S(1)}, f32[2,128,128]{2,1,0:T(8,128)S(1)}, u32[]{:S(2)}, u32[]{:S(2)}) collective-permute-start(f32[2,128,128]{2,1,0:T(8,128)S(1)} %shard_map.59), channel_id=1, source_target_pairs={{0,8},{4,12},{8,0},{12,4},{1,9},{5,13},{9,1},{13,5},{2,10},{6,14},... | collective-permute-start | bytes 393224 | tf_op jit(solution)/shard_map/ppermute | solution.py:267
  4.7 2.2 %shard_map.63 = f32[2,1024,128]{2,1,0:T(8,128)} custom-call(f32[2,2048,128]{2,1,0:T(8,128)} %g_ref.7), custom_call_target="tpu_custom_call" | custom-call | flops 1 | bytes 1 | tf_op jit(solution)/shard_map/pallas_call | solution.py:44
  6.9 0.2 collective-permute-start.9
  7.2 0.0 copy-done.6
  7.2 0.0 copy-done.5
  7.2 1.6 %collective-permute-done.lead_ref = f32[2,128,128]{2,1,0:T(8,128)S(1)} collective-permute-done((f32[2,128,128]{2,1,0:T(8,128)S(1)}, f32[2,128,128]{2,1,0:T(8,128)S(1)}, u32[]{:S(2)}, u32[]{:S(2)}) %collective-permute-start) | collective-permute-done | bytes 131104 | tf_op jit(solution)/shard_map/ppermute | solution.py:267
  8.8 1.8 %collective-permute-start.2 = (f32[258,128]{1,0:T(8,128)S(1)}, f32[258,128]{1,0:T(8,128)S(1)}, u32[]{:S(2)}, u32[]{:S(2)}) collective-permute-start(f32[258,128]{1,0:T(8,128)S(1)} %pad_maximum_fusion), channel_id=1, source_target_pairs={{0,1},{1,0},{2,3},{3,2},{4,5},{5,4},{6,7},{7,6},{8,9},{9,8},{10,11... | collective-permute-start | bytes 396296 | tf_op jit(solution)/shard_map/ppermute | solution.py:289
  10.6 2.6 %collective-permute-start.3 = (f32[258,128]{1,0:T(8,128)S(1)}, f32[258,128]{1,0:T(8,128)S(1)}, u32[]{:S(2)}, u32[]{:S(2)}) collective-permute-start(f32[258,128]{1,0:T(8,128)S(1)} %pad_maximum_fusion), channel_id=1, source_target_pairs={{0,2},{1,3},{2,0},{3,1},{4,6},{5,7},{6,4},{7,5},{8,10},{9,11},{10,... | collective-permute-start | bytes 396296 | tf_op jit(solution)/shard_map/ppermute | solution.py:289
  13.2 0.0 collective-permute-start.4
  13.2 2.0 %shard_map.60 = (f32[2,512,128]{2,1,0:T(8,128)}, f32[2,256,128]{2,1,0:T(8,128)}, f32[2,128,128]{2,1,0:T(8,128)S(1)}) custom-call(f32[2,2048,128]{2,1,0:T(8,128)} %g_ref.7), custom_call_target="tpu_custom_call" | custom-call | flops 1 | bytes 1 | tf_op jit(solution)/shard_map/pallas_call | solution.py:44
  15.2 0.0 copy-done
  15.3 6.9 %shard_map.61 = (f32[1024,256]{1,0:T(8,128)S(1)}, f32[1024,256]{1,0:T(8,128)S(1)}, f32[1024,384]{1,0:T(8,128)S(1)}) custom-call(f32[1024,2048]{1,0:T(8,128)} %refs_0_.3, f32[2,2048,128]{2,1,0:T(8,128)S(1)} %copy-done, f32[2,128,128]{2,1,0:T(8,128)S(1)} %collective-permute-done.lead_ref), custom_call_target="tpu_custom_call" | custom-call | flops 1 | bytes 1 | tf_op jit(solution)/shard_map/pallas_call | solution.py:143
  22.2 0.0 copy-start.1
  22.3 0.0 collective-permute-done.2
  22.3 1.3 %collective-permute-done.3 = f32[258,128]{1,0:T(8,128)S(1)} collective-permute-done((f32[258,128]{1,0:T(8,128)S(1)}, f32[258,128]{1,0:T(8,128)S(1)}, u32[]{:S(2)}, u32[]{:S(2)}) %collective-permute-start.3) | collective-permute-done | bytes 132128 | tf_op jit(solution)/shard_map/ppermute | solution.py:289
  23.7 0.0 collective-permute-done.4
  23.7 0.1 collective-permute-start.5
  23.8 1.6 %collective-permute-start.8 = (f32[2,512,128]{2,1,0:T(8,128)}, f32[2,512,128]{2,1,0:T(8,128)}, u32[]{:S(2)}, u32[]{:S(2)}) collective-permute-start(f32[2,512,128]{2,1,0:T(8,128)} %get-tuple-element.36), channel_id=1, source_target_pairs={{0,8},{4,12},{8,0},{12,4},{1,9},{5,13},{9,1},{13,5},{2,10},{6,14},... | collective-permute-start | bytes 1572872 | tf_op jit(solution)/shard_map/ppermute | solution.py:280
  25.4 0.3 collective-permute-done.5.oo_ref.refs_3_
  25.7 0.0 collective-permute-done.1.a_ref.refs_1_
  25.7 7.8 %shard_map.62 = (f32[4,2048]{1,0:T(4,128)S(1)}, f32[1024,384]{1,0:T(8,128)S(1)}) custom-call(f32[1024,2048]{1,0:T(8,128)} %collective-permute-done.1.a_ref.refs_1_, f32[1032,128]{1,0:T(8,128)S(1)} %constant_dynamic-update-slice_fusion.o_ref.refs_2_, f32[1032,128]{1,0:T(8,128)S(1)} %collective-permute-done.5.oo_ref.refs_3_, ...), custom_call_target="tpu_custom_call" | custom-call | flops 1 | bytes 1 | tf_op jit(solution)/shard_map/pallas_call | solution.py:143
  33.5 0.0 copy-done.1
  33.5 0.0 copy-start.3
  33.5 1.1 %copy-done.3 = f32[1024,384]{1,0:T(8,128)} copy-done((f32[1024,384]{1,0:T(8,128)}, f32[1024,384]{1,0:T(8,128)S(1)}, u32[]{:S(2)}) %copy-start.3) | copy-done | bytes 1572888
  34.7 1.5 %collective-permute-start.7 = (f32[2,256,128]{2,1,0:T(8,128)}, f32[2,256,128]{2,1,0:T(8,128)S(1)}, u32[]{:S(2)}, u32[]{:S(2)}) collective-permute-start(f32[2,256,128]{2,1,0:T(8,128)} %get-tuple-element.35), channel_id=1, source_target_pairs={{0,8},{4,12},{8,0},{12,4},{1,9},{5,13},{9,1},{13,5},{2,10},{6,14},... | collective-permute-start | bytes 786440 | tf_op jit(solution)/shard_map/ppermute | solution.py:280
  36.2 0.5 collective-permute-start.6
  36.7 0.1 convert_reduce_fusion
  36.8 0.0 collective-permute-done.9.refs_4_
  36.8 6.8 %shard_map.64.refs_5_ = f32[4,2048]{1,0:T(4,128)S(1)} custom-call(f32[1024,2048]{1,0:T(8,128)} %refs_0_.3, f32[1024,2048]{1,0:T(8,128)} %collective-permute-done.1.a_ref.refs_1_, f32[1032,128]{1,0:T(8,128)S(1)} %constant_dynamic-update-slice_fusion.o_ref.refs_2_, f32[1032,128]{1,0:T(8,128)S(1)} %collective-permute-done.5.oo_ref.refs_3_, ...), custom_call_target="tpu_custom_call" | custom-call | flops 1 | bytes 1 | tf_op jit(solution)/shard_map/pallas_call | solution.py:186
  43.6 0.0 copy-start.2
  43.7 0.0 copy-start.4
  43.7 0.9 %collective-permute-done.8.refs_4_ = f32[2,512,128]{2,1,0:T(8,128)} collective-permute-done((f32[2,512,128]{2,1,0:T(8,128)}, f32[2,512,128]{2,1,0:T(8,128)}, u32[]{:S(2)}, u32[]{:S(2)}) %collective-permute-start.8) | collective-permute-done | bytes 524320 | tf_op jit(solution)/shard_map/ppermute | solution.py:280
  44.6 4.3 %shard_map.65.refs_5_ = f32[4,2048]{1,0:T(4,128)S(1)} custom-call(f32[1024,2048]{1,0:T(8,128)} %refs_0_.3, f32[1024,2048]{1,0:T(8,128)} %collective-permute-done.1.a_ref.refs_1_, f32[1032,128]{1,0:T(8,128)S(1)} %constant_dynamic-update-slice_fusion.o_ref.refs_2_, f32[1032,128]{1,0:T(8,128)S(1)} %collective-permute-done.5.oo_ref.refs_3_, ...), custom_call_target="tpu_custom_call" | custom-call | flops 1 | bytes 1 | tf_op jit(solution)/shard_map/pallas_call | solution.py:186
  48.9 1.2 %collective-permute-done.7.refs_4_ = f32[2,256,128]{2,1,0:T(8,128)S(1)} collective-permute-done((f32[2,256,128]{2,1,0:T(8,128)}, f32[2,256,128]{2,1,0:T(8,128)S(1)}, u32[]{:S(2)}, u32[]{:S(2)}) %collective-permute-start.7) | collective-permute-done | bytes 262176 | tf_op jit(solution)/shard_map/ppermute | solution.py:280
  50.1 0.0 copy-done.2
  50.1 0.0 copy-done.4
  50.1 1.2 %shard_map.66.refs_5_ = f32[4,2048]{1,0:T(4,128)S(1)} custom-call(f32[1024,384]{1,0:T(8,128)S(1)} %copy-done.2, f32[1024,384]{1,0:T(8,128)S(1)} %copy-done.4, f32[1032,128]{1,0:T(8,128)S(1)} %constant_dynamic-update-slice_fusion.o_ref.refs_2_, f32[1032,128]{1,0:T(8,128)S(1)} %collective-permute-done.5.oo_ref.refs_3_, ...), custom_call_target="tpu_custom_call" | custom-call | flops 1 | bytes 1 | tf_op jit(solution)/shard_map/pallas_call | solution.py:215
  51.3 0.8 %collective-permute-done.6.refs_4_ = f32[2,128,128]{2,1,0:T(8,128)S(1)} collective-permute-done((f32[2,128,128]{2,1,0:T(8,128)S(1)}, f32[2,128,128]{2,1,0:T(8,128)S(1)}, u32[]{:S(2)}, u32[]{:S(2)}) %collective-permute-start.6) | collective-permute-done | bytes 131104 | tf_op jit(solution)/shard_map/ppermute | solution.py:280
  52.1 0.9 %shard_map.67 = f32[4,2048]{1,0:T(4,128)S(1)} custom-call(f32[1024,384]{1,0:T(8,128)S(1)} %copy-done.2, f32[1024,384]{1,0:T(8,128)S(1)} %copy-done.4, f32[1032,128]{1,0:T(8,128)S(1)} %constant_dynamic-update-slice_fusion.o_ref.refs_2_, f32[1032,128]{1,0:T(8,128)S(1)} %collective-permute-done.5.oo_ref.refs_3_, ...), custom_call_target="tpu_custom_call" | custom-call | flops 1 | bytes 1 | tf_op jit(solution)/shard_map/pallas_call | solution.py:215
  53.0 0.1 fusion
  53.1 0.1 pad_maximum_fusion.2
  53.2 0.1 collective-permute-start.10
  53.3 1.2 %collective-permute-done.10 = f32[4,1040]{1,0:T(4,128)S(1)} collective-permute-done((f32[4,1040]{1,0:T(4,128)S(1)}, f32[4,1040]{1,0:T(4,128)S(1)}, u32[]{:S(2)}, u32[]{:S(2)}) %collective-permute-start.10) | collective-permute-done | bytes 16672 | tf_op jit(solution)/shard_map/ppermute | solution.py:254
  54.6 0.1 pad_maximum_fusion.3
  54.7 1.6 %collective-permute-start.11 = (f32[8,544]{1,0:T(8,128)S(1)}, f32[8,544]{1,0:T(8,128)S(1)}, u32[]{:S(2)}, u32[]{:S(2)}) collective-permute-start(f32[8,544]{1,0:T(8,128)S(1)} %pad_maximum_fusion.3), channel_id=1, source_target_pairs={{0,1},{1,0},{2,3},{3,2},{4,5},{5,4},{6,7},{7,6},{8,9},{9,8},{10,11... | collective-permute-start | bytes 52232 | tf_op jit(solution)/shard_map/ppermute | solution.py:337
  56.3 0.1 pad_maximum_fusion.7
  56.3 0.6 collective-permute-start.12
  56.9 1.3 %collective-permute-start.13 = (f32[8,32]{1,0:T(8,128)S(1)}, f32[8,32]{1,0:T(8,128)S(1)}, u32[]{:S(2)}, u32[]{:S(2)}) collective-permute-start(f32[8,32]{1,0:T(8,128)S(1)} %pad_maximum_fusion.7), channel_id=1, source_target_pairs={{0,9},{1,8},{2,11},{3,10},{4,13},{5,12},{6,15},{7,14},{8,1},{9,0},... | collective-permute-start | bytes 3080 | tf_op jit(solution)/shard_map/ppermute | solution.py:337
  58.2 0.2 collective-permute-done.11
  58.5 1.5 %collective-permute-done.12 = f32[8,32]{1,0:T(8,128)S(1)} collective-permute-done((f32[8,32]{1,0:T(8,128)S(1)}, f32[8,32]{1,0:T(8,128)S(1)}, u32[]{:S(2)}, u32[]{:S(2)}) %collective-permute-start.12) | collective-permute-done | bytes 1056 | tf_op jit(solution)/shard_map/ppermute | solution.py:337
  59.9 1.5 %collective-permute-done.13 = f32[8,32]{1,0:T(8,128)S(1)} collective-permute-done((f32[8,32]{1,0:T(8,128)S(1)}, f32[8,32]{1,0:T(8,128)S(1)}, u32[]{:S(2)}, u32[]{:S(2)}) %collective-permute-start.13) | collective-permute-done | bytes 1056 | tf_op jit(solution)/shard_map/ppermute | solution.py:337
  61.4 0.1 fusion.3
  61.5 2.6 %collective-permute-start.14 = (f32[8,288]{1,0:T(8,128)S(1)}, f32[8,288]{1,0:T(8,128)S(1)}, u32[]{:S(2)}, u32[]{:S(2)}) collective-permute-start(f32[8,288]{1,0:T(8,128)S(1)} %pad_maximum_fusion.4), channel_id=1, source_target_pairs={{0,2},{1,3},{2,0},{3,1},{4,6},{5,7},{6,4},{7,5},{8,10},{9,11},{10,... | collective-permute-start | bytes 27656 | tf_op jit(solution)/shard_map/ppermute | solution.py:337
  64.1 2.0 %collective-permute-done.14 = f32[8,288]{1,0:T(8,128)S(1)} collective-permute-done((f32[8,288]{1,0:T(8,128)S(1)}, f32[8,288]{1,0:T(8,128)S(1)}, u32[]{:S(2)}, u32[]{:S(2)}) %collective-permute-start.14) | collective-permute-done | bytes 9248 | tf_op jit(solution)/shard_map/ppermute | solution.py:337
  66.1 0.7 %shard_map.68 = (f32[8,256]{1,0:T(8,128)}, f32[8,16]{1,0:T(8,128)}) custom-call(f32[8,256]{1,0:T(8,128)S(1)} %slice_add_fusion.s_ref, f32[8,32]{1,0:T(8,128)S(1)} %slice_add_fusion.3.doc_ref), custom_call_target="tpu_custom_call" | custom-call | flops 1 | bytes 1 | tf_op jit(solution)/shard_map/pallas_call | solution.py:233
  (26 shorter events, 0.3 us)
Async XLA Ops:
  1.6 5.6 %copy-start.6 = (s32[256]{0:T(256)S(1)}, s32[256]{0:T(256)}, u32[]{:S(2)}) copy-start(s32[256]{0:T(256)} %param.7) | copy-start | bytes 3076
  1.6 5.6 %copy-start.5 = (f32[256,128]{1,0:T(8,128)S(1)}, f32[256,128]{1,0:T(8,128)}, u32[]{:S(2)}) copy-start(f32[256,128]{1,0:T(8,128)} %param.6) | copy-start | bytes 393220
  1.6 13.7 %copy-start = (f32[2,2048,128]{2,1,0:T(8,128)S(1)}, f32[2,2048,128]{2,1,0:T(8,128)}, u32[]{:S(2)}) copy-start(f32[2,2048,128]{2,1,0:T(8,128)} %g_ref.7) | copy-start | bytes 6291460
  1.6 24.1 %collective-permute-start.1 = (f32[1024,2048]{1,0:T(8,128)}, f32[1024,2048]{1,0:T(8,128)}, u32[]{:S(2)}, u32[]{:S(2)}) collective-permute-start(f32[1024,2048]{1,0:T(8,128)} %refs_0_.3), channel_id=1, source_target_pairs={{0,4},{4,0},{8,12},{12,8},{1,5},{5,1},{9,13},{13,9},{2,6},{6,2},{1... | collective-permute-start | bytes 25165832 | tf_op jit(solution)/shard_map/ppermute | solution.py:254
  2.1 6.7 %collective-permute-start = (f32[2,128,128]{2,1,0:T(8,128)S(1)}, f32[2,128,128]{2,1,0:T(8,128)S(1)}, u32[]{:S(2)}, u32[]{:S(2)}) collective-permute-start(f32[2,128,128]{2,1,0:T(8,128)S(1)} %shard_map.59), channel_id=1, source_target_pairs={{0,8},{4,12},{8,0},{12,4},{1,9},{5,13},{9,1},{13,5},{2,10},{6,14},... | collective-permute-start | bytes 393224 | tf_op jit(solution)/shard_map/ppermute | solution.py:267
  6.9 29.9 %collective-permute-start.9 = (f32[2,1024,128]{2,1,0:T(8,128)}, f32[2,1024,128]{2,1,0:T(8,128)}, u32[]{:S(2)}, u32[]{:S(2)}) collective-permute-start(f32[2,1024,128]{2,1,0:T(8,128)} %shard_map.63), channel_id=1, source_target_pairs={{0,8},{4,12},{8,0},{12,4},{1,9},{5,13},{9,1},{13,5},{2,10},{6,14},... | collective-permute-start | bytes 3145736 | tf_op jit(solution)/shard_map/ppermute | solution.py:282
  8.8 13.5 %collective-permute-start.2 = (f32[258,128]{1,0:T(8,128)S(1)}, f32[258,128]{1,0:T(8,128)S(1)}, u32[]{:S(2)}, u32[]{:S(2)}) collective-permute-start(f32[258,128]{1,0:T(8,128)S(1)} %pad_maximum_fusion), channel_id=1, source_target_pairs={{0,1},{1,0},{2,3},{3,2},{4,5},{5,4},{6,7},{7,6},{8,9},{9,8},{10,11... | collective-permute-start | bytes 396296 | tf_op jit(solution)/shard_map/ppermute | solution.py:289
  10.6 13.0 %collective-permute-start.3 = (f32[258,128]{1,0:T(8,128)S(1)}, f32[258,128]{1,0:T(8,128)S(1)}, u32[]{:S(2)}, u32[]{:S(2)}) collective-permute-start(f32[258,128]{1,0:T(8,128)S(1)} %pad_maximum_fusion), channel_id=1, source_target_pairs={{0,2},{1,3},{2,0},{3,1},{4,6},{5,7},{6,4},{7,5},{8,10},{9,11},{10,... | collective-permute-start | bytes 396296 | tf_op jit(solution)/shard_map/ppermute | solution.py:289
  13.2 10.5 %collective-permute-start.4 = (f32[258,128]{1,0:T(8,128)S(1)}, f32[258,128]{1,0:T(8,128)S(1)}, u32[]{:S(2)}, u32[]{:S(2)}) collective-permute-start(f32[258,128]{1,0:T(8,128)S(1)} %pad_maximum_fusion), channel_id=1, source_target_pairs={{0,3},{1,2},{2,1},{3,0},{4,7},{5,6},{6,5},{7,4},{8,11},{9,10},{10,... | collective-permute-start | bytes 396296 | tf_op jit(solution)/shard_map/ppermute | solution.py:289
  22.2 11.3 %copy-start.1 = (f32[1024,384]{1,0:T(8,128)}, f32[1024,384]{1,0:T(8,128)S(1)}, u32[]{:S(2)}) copy-start(f32[1024,384]{1,0:T(8,128)S(1)} %get-tuple-element.26.refs_0_) | copy-start | bytes 4718596
  23.7 2.0 %collective-permute-start.5 = (f32[1032,128]{1,0:T(8,128)S(1)}, f32[1032,128]{1,0:T(8,128)S(1)}, u32[]{:S(2)}, u32[]{:S(2)}) collective-permute-start(f32[1032,128]{1,0:T(8,128)S(1)} %constant_dynamic-update-slice_fusion.o_ref.refs_2_), channel_id=1, source_target_pairs={{0,4},{4,0},{8,12},{12,8},{1,5},{5,1},{9,13},{13,9},{2,6},{6,2},{1... | collective-permute-start | bytes 1585160 | tf_op jit(solution)/shard_map/ppermute | solution.py:254
  23.8 20.8 %collective-permute-start.8 = (f32[2,512,128]{2,1,0:T(8,128)}, f32[2,512,128]{2,1,0:T(8,128)}, u32[]{:S(2)}, u32[]{:S(2)}) collective-permute-start(f32[2,512,128]{2,1,0:T(8,128)} %get-tuple-element.36), channel_id=1, source_target_pairs={{0,8},{4,12},{8,0},{12,4},{1,9},{5,13},{9,1},{13,5},{2,10},{6,14},... | collective-permute-start | bytes 1572872 | tf_op jit(solution)/shard_map/ppermute | solution.py:280
  33.5 1.1 %copy-start.3 = (f32[1024,384]{1,0:T(8,128)}, f32[1024,384]{1,0:T(8,128)S(1)}, u32[]{:S(2)}) copy-start(f32[1024,384]{1,0:T(8,128)S(1)} %get-tuple-element.32.refs_1_) | copy-start | bytes 4718596
  34.7 15.4 %collective-permute-start.7 = (f32[2,256,128]{2,1,0:T(8,128)}, f32[2,256,128]{2,1,0:T(8,128)S(1)}, u32[]{:S(2)}, u32[]{:S(2)}) collective-permute-start(f32[2,256,128]{2,1,0:T(8,128)} %get-tuple-element.35), channel_id=1, source_target_pairs={{0,8},{4,12},{8,0},{12,4},{1,9},{5,13},{9,1},{13,5},{2,10},{6,14},... | collective-permute-start | bytes 786440 | tf_op jit(solution)/shard_map/ppermute | solution.py:280
  36.2 15.9 %collective-permute-start.6 = (f32[2,128,128]{2,1,0:T(8,128)S(1)}, f32[2,128,128]{2,1,0:T(8,128)S(1)}, u32[]{:S(2)}, u32[]{:S(2)}) collective-permute-start(f32[2,128,128]{2,1,0:T(8,128)S(1)} %get-tuple-element.34), channel_id=1, source_target_pairs={{0,8},{4,12},{8,0},{12,4},{1,9},{5,13},{9,1},{13,5},{2,10},{6,14},... | collective-permute-start | bytes 393224 | tf_op jit(solution)/shard_map/ppermute | solution.py:280
  43.6 6.4 %copy-start.2 = (f32[1024,384]{1,0:T(8,128)S(1)}, f32[1024,384]{1,0:T(8,128)}, u32[]{:S(2)}) copy-start(f32[1024,384]{1,0:T(8,128)} %copy-done.1) | copy-start | bytes 4718596
  43.7 6.4 %copy-start.4 = (f32[1024,384]{1,0:T(8,128)S(1)}, f32[1024,384]{1,0:T(8,128)}, u32[]{:S(2)}) copy-start(f32[1024,384]{1,0:T(8,128)} %copy-done.3) | copy-start | bytes 4718596
  53.2 1.3 %collective-permute-start.10 = (f32[4,1040]{1,0:T(4,128)S(1)}, f32[4,1040]{1,0:T(4,128)S(1)}, u32[]{:S(2)}, u32[]{:S(2)}) collective-permute-start(f32[4,1040]{1,0:T(4,128)S(1)} %pad_maximum_fusion.2), channel_id=1, source_target_pairs={{0,4},{4,0},{8,12},{12,8},{1,5},{5,1},{9,13},{13,9},{2,6},{6,2},{1... | collective-permute-start | bytes 49928 | tf_op jit(solution)/shard_map/ppermute | solution.py:254
  54.7 3.8 %collective-permute-start.11 = (f32[8,544]{1,0:T(8,128)S(1)}, f32[8,544]{1,0:T(8,128)S(1)}, u32[]{:S(2)}, u32[]{:S(2)}) collective-permute-start(f32[8,544]{1,0:T(8,128)S(1)} %pad_maximum_fusion.3), channel_id=1, source_target_pairs={{0,1},{1,0},{2,3},{3,2},{4,5},{5,4},{6,7},{7,6},{8,9},{9,8},{10,11... | collective-permute-start | bytes 52232 | tf_op jit(solution)/shard_map/ppermute | solution.py:337
  56.3 3.6 %collective-permute-start.12 = (f32[8,32]{1,0:T(8,128)S(1)}, f32[8,32]{1,0:T(8,128)S(1)}, u32[]{:S(2)}, u32[]{:S(2)}) collective-permute-start(f32[8,32]{1,0:T(8,128)S(1)} %pad_maximum_fusion.7), channel_id=1, source_target_pairs={{0,8},{1,9},{2,10},{3,11},{4,12},{5,13},{6,14},{7,15},{8,0},{9,1},... | collective-permute-start | bytes 3080 | tf_op jit(solution)/shard_map/ppermute | solution.py:337
  56.9 4.5 %collective-permute-start.13 = (f32[8,32]{1,0:T(8,128)S(1)}, f32[8,32]{1,0:T(8,128)S(1)}, u32[]{:S(2)}, u32[]{:S(2)}) collective-permute-start(f32[8,32]{1,0:T(8,128)S(1)} %pad_maximum_fusion.7), channel_id=1, source_target_pairs={{0,9},{1,8},{2,11},{3,10},{4,13},{5,12},{6,15},{7,14},{8,1},{9,0},... | collective-permute-start | bytes 3080 | tf_op jit(solution)/shard_map/ppermute | solution.py:337
  61.5 4.6 %collective-permute-start.14 = (f32[8,288]{1,0:T(8,128)S(1)}, f32[8,288]{1,0:T(8,128)S(1)}, u32[]{:S(2)}, u32[]{:S(2)}) collective-permute-start(f32[8,288]{1,0:T(8,128)S(1)} %pad_maximum_fusion.4), channel_id=1, source_target_pairs={{0,2},{1,3},{2,0},{3,1},{4,6},{5,7},{6,4},{7,5},{8,10},{9,11},{10,... | collective-permute-start | bytes 27656 | tf_op jit(solution)/shard_map/ppermute | solution.py:337

commit v4 on v3

--- a/solution.py
+++ b/solution.py
@@ -11,6 +11,7 @@
 LANES = 128
 F32, BF16 = jnp.float32, jnp.bfloat16
 TILE = 256
+LEADS = 1
 PARTS = (2, 4, 8, 16, 16)
 VMEM = pl.BlockSpec(memory_space=pltpu.VMEM)
 HBM = pl.BlockSpec(memory_space=pltpu.HBM)
@@ -83,7 +84,7 @@
     return contract(project(a, weights, step), o)
 
 
-def prepare(g_ref, lead_ref, refs):
+def prepare(g_ref, lead_refs, refs):
     high_ref, low_ref, lead_high_ref, lead_low_ref = refs
     step = high_ref.shape[1]
 
@@ -92,29 +93,30 @@
         for k, (gh, gl) in enumerate(weigh(g_ref, step)):
             high_ref[k] = gh
             low_ref[k] = gl
-        lead_high_ref[...], lead_low_ref[...] = weigh(lead_ref, lead_ref.shape[1])[0]
+        for k, lead_ref in enumerate(lead_refs):
+            lead_high_ref[k], lead_low_ref[k] = weigh(lead_ref, lead_ref.shape[1])[0]
 
     weights = [(high_ref.at[k], low_ref.at[k]) for k in range(high_ref.shape[0])]
-    return weights, [(lead_high_ref, lead_low_ref)]
+    return weights, [(lead_high_ref.at[k], lead_low_ref.at[k]) for k in range(LEADS)]
 
 
 def project_both(a, weights, lead_weights, at):
     step, n = weights[0][0].shape[0], lead_weights[0][0].shape[0]
-    return project(a, weights, step), project(a[:, at : at + n], lead_weights, n)
-
-
-def own_kernel(at, cols, a_ref, g_ref, lead_ref, p_ref, lead_p_ref, stage_ref, *refs):
-    weights, lead_weights = prepare(g_ref, lead_ref, refs)
+    lead_p = project(a[:, at : at + LEADS * n], lead_weights, n)
+    return project(a, weights, step), lead_p
+
+
+def own_kernel(at, cols, a_ref, g_ref, *refs):
+    lead_refs, (p_ref, stage_ref, *refs) = refs[:LEADS], refs[LEADS:]
+    weights, lead_weights = prepare(g_ref, lead_refs, refs)
     a = a_ref[...]
-    here = pl.ds(pl.multiple_of(pl.program_id(0) * a.shape[0], a.shape[0]), a.shape[0])
-    p_ref[here, :], lead_p_ref[here, :] = project_both(a, weights, lead_weights, at)
-    stage_ref[here, :] = a[:, cols[0] : cols[1]]
-
-
-def other_kernel(
-    at, cols, a_ref, o_ref, oo_ref, p_ref, lead_p_ref, g_ref, lead_ref, s_ref, stage_ref, *refs
-):
-    weights, lead_weights = prepare(g_ref, lead_ref, refs)
+    p_ref[...] = jnp.concatenate(project_both(a, weights, lead_weights, at), axis=1)
+    stage_ref[...] = a[:, cols[0] : cols[1]]
+
+
+def other_kernel(at, cols, a_ref, p_ref, o_ref, oo_ref, g_ref, *refs):
+    lead_refs, (s_ref, stage_ref, *refs) = refs[:LEADS], refs[LEADS:]
+    weights, lead_weights = prepare(g_ref, lead_refs, refs)
     a = a_ref[...]
     tile = a.shape[0]
     t = s_ref.shape[1] // 2
@@ -127,30 +129,32 @@
 
     here = pl.ds(pl.multiple_of(start, tile), tile)
     there = pl.ds(pl.multiple_of(t + start, tile), tile)
-    own = p_ref[here, :], lead_p_ref[here, :]
+    own = jnp.split(p_ref[...], 2, axis=1)
     other = project_both(a, weights, lead_weights, at)
     for to, parts, o in ((here, own, o_ref[here, :]), (there, other, oo_ref[here, :])):
         for i, p in enumerate(parts):
             for q, row in enumerate(contract(p, o)):
                 s_ref[i * nq + q, to] = row
-    stage_ref[here, :] = a[:, cols[0] : cols[1]]
-
-
-def near_call(kernel, a, others, g, lead, out):
-    t = a.shape[0]
-    nq, n, r = g.shape
+    stage_ref[...] = a[:, cols[0] : cols[1]]
+
+
+def near_call(kernel, tiled, others, g, leads, whole_out, tiled_out):
+    t, n = tiled[0].shape
+    nq, _, r = g.shape
     tile, step = min(t, TILE), min(n, 512)
+    tiles = lambda width: pl.BlockSpec((tile, width), lambda i: (i, 0))
     return pl.pallas_call(
         kernel,
         grid=(t // tile,),
-        in_specs=[pl.BlockSpec((tile, n), lambda i: (i, 0))] + [VMEM] * (len(others) + 2),
-        out_specs=[VMEM] * len(out),
-        out_shape=[jax.ShapeDtypeStruct(shape, F32) for shape in out],
+        in_specs=[tiles(x.shape[1]) for x in tiled] + [VMEM] * (len(others) + 1 + LEADS),
+        out_specs=[VMEM] * len(whole_out) + [tiles(width) for width in tiled_out],
+        out_shape=[jax.ShapeDtypeStruct(shape, F32) for shape in whole_out]
+        + [pltpu.HBM((t, width), F32) for width in tiled_out],
         scratch_shapes=[pltpu.VMEM((n // step, step, nq * r), BF16)] * 2
-        + [pltpu.VMEM((lead.shape[1], nq * r), BF16)] * 2,
-        compiler_params=PARAMS,
-        cost_estimate=COST,
-    )(in_hbm(a), *others, g, lead)
+        + [pltpu.VMEM((LEADS, leads[0].shape[1], nq * r), BF16)] * 2,
+        compiler_params=PARAMS,
+        cost_estimate=COST,
+    )(*[in_hbm(x) for x in tiled], *others, g, *leads)
 
 
 def stream_kernel(first, *refs):
@@ -262,24 +266,32 @@
         if at < d:
             pieces.append((at, n))
         at += n
-    pieces = pieces[-1:] + pieces[:-1]
-    cuts = cut(g, pieces[:1])
-    lead = lax.ppermute(cuts[0], "blk", pairs(nb, 2))
-    cuts += cut(after(g, cuts[0]), pieces[1:2])
+    pieces = pieces[-LEADS:] + pieces[:-LEADS]
+    cuts = [g[:, at : at + n] for at, n in pieces[:LEADS]]
+    leads = [lax.ppermute(x, "blk", pairs(nb, 2)) for x in cuts]
+    lead = leads[0]
+    cuts += cut(after(g, cuts[0]), pieces[LEADS : LEADS + 1])
     a_other = to_core(after(a, cuts[0]))
-    cuts += cut(after(g, lead), pieces[2:])
-    at, last = pieces[0][0], pieces[-1]
-    cols = pieces[-2][0], sum(last)
-    wide = (t, nq * r), (t, nq * r), (t, cols[1] - cols[0])
-    a_own = after(a, lead, *cuts[2:])
-    p, lead_p, stage = near_call(functools.partial(own_kernel, at, cols), a_own, [], g, lead, wide)
+    cuts += cut(after(g, lead), pieces[LEADS + 1 :])
+    at = pieces[0][0]
+    cols = min(i for i, n in pieces if n <= 512 and i < at), at
+    a_own = after(a, lead, *cuts[LEADS + 1 :])
+    p, stage = near_call(
+        functools.partial(own_kernel, at, cols),
+        [a_own],
+        [],
+        g,
+        leads,
+        [],
+        [2 * nq * r, cols[1] - cols[0]],
+    )
     sends = [(j, at, x) for j in range(2, nb, 2) for (at, _), x in zip(pieces, cuts)]
 
     def send(i, *others):
         j, _, x = sends[i]
         return lax.ppermute(after(x, *others), "blk", pairs(nb, j))
 
-    arrived = [lead, lax.ppermute(cuts[1], "blk", pairs(nb, 2)), send(2, lead)]
+    arrived = leads + [lax.ppermute(cuts[LEADS], "blk", pairs(nb, 2)), send(LEADS + 1, lead)]
 
     rows = own // LANES
     flat = ids.astype(F32).reshape(rows, LANES)
@@ -295,19 +307,20 @@
     both, outgrads = [a, a_other], [table, other]
     s, stage_other = near_call(
         functools.partial(other_kernel, at, cols),
-        a_other,
-        [*outgrads, p, lead_p],
+        [a_other, p],
+        outgrads,
         g,
-        lead,
-        ((nb // 2 * nq, 2 * t), wide[2]),
+        leads,
+        [(nb // 2 * nq, 2 * t)],
+        [cols[1] - cols[0]],
     )
     stages = [stage, stage_other]
-    arrived.append(send(3, s))
+    arrived.append(send(LEADS + 2, s))
     for i, (j, at, x) in enumerate(sends):
-        if i + 4 < len(sends):
-            arrived.append(send(i + 4, s))
+        if i + LEADS + 3 < len(sends):
+            arrived.append(send(i + LEADS + 3, s))
         first = j // 2 * nq
-        if i == 0:
+        if i < LEADS:
             continue
         if cols[0] <= at < cols[1]:
             s = staged_scores(s, stages, outgrads, arrived[i], at - cols[0], first)

time: 67.1 us -> 67.3 us (level)
  other arithmetic: 0.55 us -> 2.13 us
  waiting for transfers between devices: 12.5 us -> 11.7 us
    pallas_call x2 -> x1, Pallas kernels: 11.1 us -> 6.93 us  [stream_scores(): pl.pallas_call(functools.partial(stream_kernel, first), grid=(t // tile,)...]
    pallas_call x2 -> x3, Pallas kernels: 2.07 us -> 5.12 us  [staged_scores(): pl.pallas_call(functools.partial(staged_kernel, start, first), in_specs=[...]
    pallas_call x2, Pallas kernels: 14.7 us -> 16.2 us  [near_call(): pl.pallas_call(kernel, grid=(t // tile,), in_specs=[tiles(x.shape[1]) for...]
    ppermute x3, waiting for transfers between devices: 2.95 us -> 4.44 us  [send(): return lax.ppermute(after(x, *others), 'blk', pairs(nb, j))]
    ppermute x2, waiting for transfers between devices: 1.61 us -> 0.17 us  [the longest x1 0.17 us: per_device(): leads = [lax.ppermute(x, 'blk', pairs(nb, 2)) for x in cuts]]
    unnamed x14 -> x6, local copies, waits for them, and re-layouts: 1.17 us -> 0.01 us
    slice x0 -> x1, local copies, waits for them, and re-layouts: none -> 1.07 us  [per_device(): cuts = [g[:, at:at + n] for at, n in pieces[:LEADS]]]
    ppermute x3, waiting for transfers between devices: 1.33 us -> 0.4 us  [per_device(): got = lax.ppermute(mine, 'width', pairs(nw, k)) if k else mine]
  transfers between devices with their start and end apart: 15 -> 15, of which waited for: 11 -> 11; matrix products, arithmetic and copies ran while one was open for 1% -> 3% of each run, Pallas kernels for 47% -> 47%
where the time goes in v4:
time: 67.3 us; the launch traced here: 66.9 us
  Pallas kernels  33.3 us (49%)
  starting transfers between devices  17.6 us (26%)
  waiting for transfers between devices  11.7 us (17%)
  other arithmetic  2.13 us (3%)
  local copies, waits for them, and re-layouts  1.24 us (2%)
  between operations  0.87 us (1%)
    pallas_call x2, Pallas kernels, near_call(): pl.pallas_call(kernel, grid=(t // tile,), in_specs=[tiles(x.shape[1]) for...  16.2 us
    pallas_call x1, Pallas kernels, stream_scores(): pl.pallas_call(functools.partial(stream_kernel, first), grid=(t // tile,)...  6.93 us
    ppermute x4, starting transfers between devices, per_device(): lax.ppermute(x, ('blk', 'width'), [(i * nw + k, (i ^ y_bit) * nw + (k ^ z...  6.09 us
    ppermute x4, waiting for transfers between devices, per_device(): lax.ppermute(x, ('blk', 'width'), [(i * nw + k, (i ^ y_bit) * nw + (k ^ z...  5.18 us
    pallas_call x3, Pallas kernels, staged_scores(): pl.pallas_call(functools.partial(staged_kernel, start, first), in_specs=[...  5.12 us
    ppermute x3, starting transfers between devices, per_device(): got = lax.ppermute(mine, 'width', pairs(nw, k)) if k else mine  4.57 us
    ppermute x3, waiting for transfers between devices, send(): return lax.ppermute(after(x, *others), 'blk', pairs(nb, j))  4.44 us
    pallas_call x2, Pallas kernels, cut(): pl.pallas_call(functools.partial(cut_kernel, pieces), in_specs=[HBM], out...  4.29 us
  transfers between devices with their start and end apart: 15, of which 11 were waited for; matrix products, arithmetic and copies ran while one was open for 3% of the time, Pallas kernels for 47%

profile of v4, /device:TPU:0, one launch (start us, length us, event | category | flops | bytes accessed | tf_op | source)
XLA Modules:
  0.0 66.9 jit_solution(12060609483356556222)
XLA Ops:
  0.6 0.0 copy-start
  0.6 1.1 %slice.86 = f32[2,128,128]{2,1,0:T(8,128)S(1)} slice(f32[2,2048,128]{2,1,0:T(8,128)} %g_ref.5), slice={[0:2], [1920:2048], [0:128]} | slice | bytes 262144 | tf_op jit(solution)/shard_map/slice | solution.py:270
  1.7 0.5 collective-permute-start.1
  2.2 2.6 %collective-permute-start = (f32[2,128,128]{2,1,0:T(8,128)S(1)}, f32[2,128,128]{2,1,0:T(8,128)S(1)}, u32[]{:S(2)}, u32[]{:S(2)}) collective-permute-start(f32[2,128,128]{2,1,0:T(8,128)S(1)} %slice.86), channel_id=1, source_target_pairs={{0,8},{4,12},{8,0},{12,4},{1,9},{5,13},{9,1},{13,5},{2,10},{6,14},... | collective-permute-start | bytes 393224 | tf_op jit(solution)/shard_map/ppermute | solution.py:271
  4.8 2.2 %shard_map.62 = f32[2,1024,128]{2,1,0:T(8,128)} custom-call(f32[2,2048,128]{2,1,0:T(8,128)} %g_ref.5), custom_call_target="tpu_custom_call" | custom-call | flops 1 | bytes 1 | tf_op jit(solution)/shard_map/pallas_call | solution.py:45
  7.1 0.1 collective-permute-start.9
  7.1 0.7 %convert_bitcast_fusion = f32[2,128]{1,0:T(2,128)S(1)} fusion(s32[256]{0:T(256)} %param.7), kind=kLoop, calls=%fused_computation.41 | loop fusion | flops 256 | bytes 2048 | tf_op jit(solution)/shard_map/reshape | solution.py:297
  7.8 0.9 %pad_maximum_fusion = f32[258,128]{1,0:T(8,128)S(1)} fusion(f32[2,128]{1,0:T(2,128)S(1)} %convert_bitcast_fusion, f32[256,128]{1,0:T(8,128)} %param.6), kind=kLoop, calls=%fused_computation | loop fusion | flops 33024 | bytes 264192 | tf_op jit(solution)/shard_map/concatenate | solution.py:298
  8.7 0.2 collective-permute-done.refs_0_
  8.9 2.0 %collective-permute-start.2 = (f32[258,128]{1,0:T(8,128)S(1)}, f32[258,128]{1,0:T(8,128)S(1)}, u32[]{:S(2)}, u32[]{:S(2)}) collective-permute-start(f32[258,128]{1,0:T(8,128)S(1)} %pad_maximum_fusion), channel_id=1, source_target_pairs={{0,1},{1,0},{2,3},{3,2},{4,5},{5,4},{6,7},{7,6},{8,9},{9,8},{10,11... | collective-permute-start | bytes 396296 | tf_op jit(solution)/shard_map/ppermute | solution.py:301
  10.9 2.6 %collective-permute-start.3 = (f32[258,128]{1,0:T(8,128)S(1)}, f32[258,128]{1,0:T(8,128)S(1)}, u32[]{:S(2)}, u32[]{:S(2)}) collective-permute-start(f32[258,128]{1,0:T(8,128)S(1)} %pad_maximum_fusion), channel_id=1, source_target_pairs={{0,2},{1,3},{2,0},{3,1},{4,6},{5,7},{6,4},{7,5},{8,10},{9,11},{10,... | collective-permute-start | bytes 396296 | tf_op jit(solution)/shard_map/ppermute | solution.py:301
  13.5 0.0 collective-permute-start.4
  13.5 2.1 %shard_map.59 = (f32[2,512,128]{2,1,0:T(8,128)}, f32[2,256,128]{2,1,0:T(8,128)}, f32[2,128,128]{2,1,0:T(8,128)S(1)}) custom-call(f32[2,2048,128]{2,1,0:T(8,128)} %g_ref.5), custom_call_target="tpu_custom_call" | custom-call | flops 1 | bytes 1 | tf_op jit(solution)/shard_map/pallas_call | solution.py:45
  15.6 0.0 copy-done
  15.6 8.0 %shard_map.60 = (f32[1024,512]{1,0:T(8,128)}, f32[1024,896]{1,0:T(8,128)}) custom-call(f32[1024,2048]{1,0:T(8,128)} %refs_0_.1, f32[2,2048,128]{2,1,0:T(8,128)S(1)} %copy-done, f32[2,128,128]{2,1,0:T(8,128)S(1)} %collective-permute-done.refs_0_), custom_call_target="tpu_custom_call" | custom-call | flops 1 | bytes 1 | tf_op jit(solution)/shard_map/pallas_call | solution.py:146
  23.6 0.0 collective-permute-done.2
  23.7 0.4 collective-permute-done.3
  24.1 0.0 collective-permute-done.4
  24.2 0.1 collective-permute-start.5
  24.3 1.6 %collective-permute-start.8 = (f32[2,512,128]{2,1,0:T(8,128)}, f32[2,512,128]{2,1,0:T(8,128)}, u32[]{:S(2)}, u32[]{:S(2)}) collective-permute-start(f32[2,512,128]{2,1,0:T(8,128)} %get-tuple-element.34), channel_id=1, source_target_pairs={{0,8},{4,12},{8,0},{12,4},{1,9},{5,13},{9,1},{13,5},{2,10},{6,14},... | collective-permute-start | bytes 1572872 | tf_op jit(solution)/shard_map/ppermute | solution.py:292
  25.8 0.3 collective-permute-done.5.oo_ref.refs_3_
  26.2 0.0 collective-permute-done.1.a_ref.refs_1_
  26.2 8.2 %shard_map.61 = (f32[4,2048]{1,0:T(4,128)S(1)}, f32[1024,896]{1,0:T(8,128)}) custom-call(f32[1024,2048]{1,0:T(8,128)} %collective-permute-done.1.a_ref.refs_1_, f32[1024,512]{1,0:T(8,128)} %get-tuple-element.27.p_ref, f32[1032,128]{1,0:T(8,128)S(1)} %constant_dynamic-update-slice_fusion.o_ref.refs_2_, f32[1032,128]{1,0:T(8,128)S(1)} %collective-permute-done.5.oo_ref.refs_3_, ...), custom_call_target="tpu_custom_call" | custom-call | flops 1 | bytes 1 | tf_op jit(solution)/shard_map/pallas_call | solution.py:146
  34.4 1.5 %collective-permute-start.7 = (f32[2,256,128]{2,1,0:T(8,128)}, f32[2,256,128]{2,1,0:T(8,128)S(1)}, u32[]{:S(2)}, u32[]{:S(2)}) collective-permute-start(f32[2,256,128]{2,1,0:T(8,128)} %get-tuple-element.33), channel_id=1, source_target_pairs={{0,8},{4,12},{8,0},{12,4},{1,9},{5,13},{9,1},{13,5},{2,10},{6,14},... | collective-permute-start | bytes 786440 | tf_op jit(solution)/shard_map/ppermute | solution.py:292
  35.9 0.5 collective-permute-start.6
  36.4 0.1 convert_reduce_fusion
  36.6 0.0 copy-start.1
  36.6 0.0 copy-start.2
  36.6 0.0 collective-permute-done.9.refs_4_
  36.6 6.9 %shard_map.63.refs_5_ = f32[4,2048]{1,0:T(4,128)S(1)} custom-call(f32[1024,2048]{1,0:T(8,128)} %refs_0_.1, f32[1024,2048]{1,0:T(8,128)} %collective-permute-done.1.a_ref.refs_1_, f32[1032,128]{1,0:T(8,128)S(1)} %constant_dynamic-update-slice_fusion.o_ref.refs_2_, f32[1032,128]{1,0:T(8,128)S(1)} %collective-permute-done.5.oo_ref.refs_3_, ...), custom_call_target="tpu_custom_call" | custom-call | flops 1 | bytes 1 | tf_op jit(solution)/shard_map/pallas_call | solution.py:190
  43.5 1.2 %collective-permute-done.8.refs_4_ = f32[2,512,128]{2,1,0:T(8,128)} collective-permute-done((f32[2,512,128]{2,1,0:T(8,128)}, f32[2,512,128]{2,1,0:T(8,128)}, u32[]{:S(2)}, u32[]{:S(2)}) %collective-permute-start.8) | collective-permute-done | bytes 524320 | tf_op jit(solution)/shard_map/ppermute | solution.py:292
  44.7 0.0 copy-done.1
  44.7 0.0 copy-done.2
  44.7 3.1 %shard_map.64.refs_5_ = f32[4,2048]{1,0:T(4,128)S(1)} custom-call(f32[1024,896]{1,0:T(8,128)S(1)} %copy-done.1, f32[1024,896]{1,0:T(8,128)S(1)} %copy-done.2, f32[1032,128]{1,0:T(8,128)S(1)} %constant_dynamic-update-slice_fusion.o_ref.refs_2_, f32[1032,128]{1,0:T(8,128)S(1)} %collective-permute-done.5.oo_ref.refs_3_, ...), custom_call_target="tpu_custom_call" | custom-call | flops 1 | bytes 1 | tf_op jit(solution)/shard_map/pallas_call | solution.py:219
  47.8 2.4 %collective-permute-done.7.refs_4_ = f32[2,256,128]{2,1,0:T(8,128)S(1)} collective-permute-done((f32[2,256,128]{2,1,0:T(8,128)}, f32[2,256,128]{2,1,0:T(8,128)S(1)}, u32[]{:S(2)}, u32[]{:S(2)}) %collective-permute-start.7) | collective-permute-done | bytes 262176 | tf_op jit(solution)/shard_map/ppermute | solution.py:292
  50.2 1.2 %shard_map.65.refs_5_ = f32[4,2048]{1,0:T(4,128)S(1)} custom-call(f32[1024,896]{1,0:T(8,128)S(1)} %copy-done.1, f32[1024,896]{1,0:T(8,128)S(1)} %copy-done.2, f32[1032,128]{1,0:T(8,128)S(1)} %constant_dynamic-update-slice_fusion.o_ref.refs_2_, f32[1032,128]{1,0:T(8,128)S(1)} %collective-permute-done.5.oo_ref.refs_3_, ...), custom_call_target="tpu_custom_call" | custom-call | flops 1 | bytes 1 | tf_op jit(solution)/shard_map/pallas_call | solution.py:219
  51.4 0.8 %collective-permute-done.6.refs_4_ = f32[2,128,128]{2,1,0:T(8,128)S(1)} collective-permute-done((f32[2,128,128]{2,1,0:T(8,128)S(1)}, f32[2,128,128]{2,1,0:T(8,128)S(1)}, u32[]{:S(2)}, u32[]{:S(2)}) %collective-permute-start.6) | collective-permute-done | bytes 131104 | tf_op jit(solution)/shard_map/ppermute | solution.py:292
  52.2 0.9 %shard_map.66 = f32[4,2048]{1,0:T(4,128)S(1)} custom-call(f32[1024,896]{1,0:T(8,128)S(1)} %copy-done.1, f32[1024,896]{1,0:T(8,128)S(1)} %copy-done.2, f32[1032,128]{1,0:T(8,128)S(1)} %constant_dynamic-update-slice_fusion.o_ref.refs_2_, f32[1032,128]{1,0:T(8,128)S(1)} %collective-permute-done.5.oo_ref.refs_3_, ...), custom_call_target="tpu_custom_call" | custom-call | flops 1 | bytes 1 | tf_op jit(solution)/shard_map/pallas_call | solution.py:219
  53.1 0.1 fusion
  53.3 0.1 pad_maximum_fusion.2
  53.3 0.1 collective-permute-start.10
  53.4 1.2 %collective-permute-done.10 = f32[4,1040]{1,0:T(4,128)S(1)} collective-permute-done((f32[4,1040]{1,0:T(4,128)S(1)}, f32[4,1040]{1,0:T(4,128)S(1)}, u32[]{:S(2)}, u32[]{:S(2)}) %collective-permute-start.10) | collective-permute-done | bytes 16672 | tf_op jit(solution)/shard_map/ppermute | solution.py:258
  54.7 0.1 pad_maximum_fusion.3
  54.8 1.6 %collective-permute-start.11 = (f32[8,544]{1,0:T(8,128)S(1)}, f32[8,544]{1,0:T(8,128)S(1)}, u32[]{:S(2)}, u32[]{:S(2)}) collective-permute-start(f32[8,544]{1,0:T(8,128)S(1)} %pad_maximum_fusion.3), channel_id=1, source_target_pairs={{0,1},{1,0},{2,3},{3,2},{4,5},{5,4},{6,7},{7,6},{8,9},{9,8},{10,11... | collective-permute-start | bytes 52232 | tf_op jit(solution)/shard_map/ppermute | solution.py:350
  56.4 0.1 pad_maximum_fusion.7
  56.4 0.6 collective-permute-start.12
  57.0 1.3 %collective-permute-start.13 = (f32[8,32]{1,0:T(8,128)S(1)}, f32[8,32]{1,0:T(8,128)S(1)}, u32[]{:S(2)}, u32[]{:S(2)}) collective-permute-start(f32[8,32]{1,0:T(8,128)S(1)} %pad_maximum_fusion.7), channel_id=1, source_target_pairs={{0,9},{1,8},{2,11},{3,10},{4,13},{5,12},{6,15},{7,14},{8,1},{9,0},... | collective-permute-start | bytes 3080 | tf_op jit(solution)/shard_map/ppermute | solution.py:350
  58.4 0.2 collective-permute-done.11
  58.6 1.5 %collective-permute-done.12 = f32[8,32]{1,0:T(8,128)S(1)} collective-permute-done((f32[8,32]{1,0:T(8,128)S(1)}, f32[8,32]{1,0:T(8,128)S(1)}, u32[]{:S(2)}, u32[]{:S(2)}) %collective-permute-start.12) | collective-permute-done | bytes 1056 | tf_op jit(solution)/shard_map/ppermute | solution.py:350
  60.1 1.5 %collective-permute-done.13 = f32[8,32]{1,0:T(8,128)S(1)} collective-permute-done((f32[8,32]{1,0:T(8,128)S(1)}, f32[8,32]{1,0:T(8,128)S(1)}, u32[]{:S(2)}, u32[]{:S(2)}) %collective-permute-start.13) | collective-permute-done | bytes 1056 | tf_op jit(solution)/shard_map/ppermute | solution.py:350
  61.5 0.1 fusion.3
  61.6 2.6 %collective-permute-start.14 = (f32[8,288]{1,0:T(8,128)S(1)}, f32[8,288]{1,0:T(8,128)S(1)}, u32[]{:S(2)}, u32[]{:S(2)}) collective-permute-start(f32[8,288]{1,0:T(8,128)S(1)} %pad_maximum_fusion.4), channel_id=1, source_target_pairs={{0,2},{1,3},{2,0},{3,1},{4,6},{5,7},{6,4},{7,5},{8,10},{9,11},{10,... | collective-permute-start | bytes 27656 | tf_op jit(solution)/shard_map/ppermute | solution.py:350
  64.2 2.0 %collective-permute-done.14 = f32[8,288]{1,0:T(8,128)S(1)} collective-permute-done((f32[8,288]{1,0:T(8,128)S(1)}, f32[8,288]{1,0:T(8,128)S(1)}, u32[]{:S(2)}, u32[]{:S(2)}) %collective-permute-start.14) | collective-permute-done | bytes 9248 | tf_op jit(solution)/shard_map/ppermute | solution.py:350
  66.2 0.7 %shard_map.67 = (f32[8,256]{1,0:T(8,128)}, f32[8,16]{1,0:T(8,128)}) custom-call(f32[8,256]{1,0:T(8,128)S(1)} %slice_add_fusion.s_ref, f32[8,32]{1,0:T(8,128)S(1)} %slice_add_fusion.3.doc_ref), custom_call_target="tpu_custom_call" | custom-call | flops 1 | bytes 1 | tf_op jit(solution)/shard_map/pallas_call | solution.py:237
  (24 shorter events, 0.3 us)
Async XLA Ops:
  0.6 14.9 %copy-start = (f32[2,2048,128]{2,1,0:T(8,128)S(1)}, f32[2,2048,128]{2,1,0:T(8,128)}, u32[]{:S(2)}) copy-start(f32[2,2048,128]{2,1,0:T(8,128)} %g_ref.5) | copy-start | bytes 6291460
  1.7 24.4 %collective-permute-start.1 = (f32[1024,2048]{1,0:T(8,128)}, f32[1024,2048]{1,0:T(8,128)}, u32[]{:S(2)}, u32[]{:S(2)}) collective-permute-start(f32[1024,2048]{1,0:T(8,128)} %refs_0_.1), channel_id=1, source_target_pairs={{0,4},{4,0},{8,12},{12,8},{1,5},{5,1},{9,13},{13,9},{2,6},{6,2},{1... | collective-permute-start | bytes 25165832 | tf_op jit(solution)/shard_map/ppermute | solution.py:258
  2.2 6.7 %collective-permute-start = (f32[2,128,128]{2,1,0:T(8,128)S(1)}, f32[2,128,128]{2,1,0:T(8,128)S(1)}, u32[]{:S(2)}, u32[]{:S(2)}) collective-permute-start(f32[2,128,128]{2,1,0:T(8,128)S(1)} %slice.86), channel_id=1, source_target_pairs={{0,8},{4,12},{8,0},{12,4},{1,9},{5,13},{9,1},{13,5},{2,10},{6,14},... | collective-permute-start | bytes 393224 | tf_op jit(solution)/shard_map/ppermute | solution.py:271
  7.1 29.5 %collective-permute-start.9 = (f32[2,1024,128]{2,1,0:T(8,128)}, f32[2,1024,128]{2,1,0:T(8,128)}, u32[]{:S(2)}, u32[]{:S(2)}) collective-permute-start(f32[2,1024,128]{2,1,0:T(8,128)} %shard_map.62), channel_id=1, source_target_pairs={{0,8},{4,12},{8,0},{12,4},{1,9},{5,13},{9,1},{13,5},{2,10},{6,14},... | collective-permute-start | bytes 3145736 | tf_op jit(solution)/shard_map/ppermute | solution.py:294
  8.9 14.7 %collective-permute-start.2 = (f32[258,128]{1,0:T(8,128)S(1)}, f32[258,128]{1,0:T(8,128)S(1)}, u32[]{:S(2)}, u32[]{:S(2)}) collective-permute-start(f32[258,128]{1,0:T(8,128)S(1)} %pad_maximum_fusion), channel_id=1, source_target_pairs={{0,1},{1,0},{2,3},{3,2},{4,5},{5,4},{6,7},{7,6},{8,9},{9,8},{10,11... | collective-permute-start | bytes 396296 | tf_op jit(solution)/shard_map/ppermute | solution.py:301
  10.9 13.2 %collective-permute-start.3 = (f32[258,128]{1,0:T(8,128)S(1)}, f32[258,128]{1,0:T(8,128)S(1)}, u32[]{:S(2)}, u32[]{:S(2)}) collective-permute-start(f32[258,128]{1,0:T(8,128)S(1)} %pad_maximum_fusion), channel_id=1, source_target_pairs={{0,2},{1,3},{2,0},{3,1},{4,6},{5,7},{6,4},{7,5},{8,10},{9,11},{10,... | collective-permute-start | bytes 396296 | tf_op jit(solution)/shard_map/ppermute | solution.py:301
  13.5 10.6 %collective-permute-start.4 = (f32[258,128]{1,0:T(8,128)S(1)}, f32[258,128]{1,0:T(8,128)S(1)}, u32[]{:S(2)}, u32[]{:S(2)}) collective-permute-start(f32[258,128]{1,0:T(8,128)S(1)} %pad_maximum_fusion), channel_id=1, source_target_pairs={{0,3},{1,2},{2,1},{3,0},{4,7},{5,6},{6,5},{7,4},{8,11},{9,10},{10,... | collective-permute-start | bytes 396296 | tf_op jit(solution)/shard_map/ppermute | solution.py:301
  24.2 2.0 %collective-permute-start.5 = (f32[1032,128]{1,0:T(8,128)S(1)}, f32[1032,128]{1,0:T(8,128)S(1)}, u32[]{:S(2)}, u32[]{:S(2)}) collective-permute-start(f32[1032,128]{1,0:T(8,128)S(1)} %constant_dynamic-update-slice_fusion.o_ref.refs_2_), channel_id=1, source_target_pairs={{0,4},{4,0},{8,12},{12,8},{1,5},{5,1},{9,13},{13,9},{2,6},{6,2},{1... | collective-permute-start | bytes 1585160 | tf_op jit(solution)/shard_map/ppermute | solution.py:258
  24.3 20.4 %collective-permute-start.8 = (f32[2,512,128]{2,1,0:T(8,128)}, f32[2,512,128]{2,1,0:T(8,128)}, u32[]{:S(2)}, u32[]{:S(2)}) collective-permute-start(f32[2,512,128]{2,1,0:T(8,128)} %get-tuple-element.34), channel_id=1, source_target_pairs={{0,8},{4,12},{8,0},{12,4},{1,9},{5,13},{9,1},{13,5},{2,10},{6,14},... | collective-permute-start | bytes 1572872 | tf_op jit(solution)/shard_map/ppermute | solution.py:292
  34.4 15.8 %collective-permute-start.7 = (f32[2,256,128]{2,1,0:T(8,128)}, f32[2,256,128]{2,1,0:T(8,128)S(1)}, u32[]{:S(2)}, u32[]{:S(2)}) collective-permute-start(f32[2,256,128]{2,1,0:T(8,128)} %get-tuple-element.33), channel_id=1, source_target_pairs={{0,8},{4,12},{8,0},{12,4},{1,9},{5,13},{9,1},{13,5},{2,10},{6,14},... | collective-permute-start | bytes 786440 | tf_op jit(solution)/shard_map/ppermute | solution.py:292
  35.9 16.3 %collective-permute-start.6 = (f32[2,128,128]{2,1,0:T(8,128)S(1)}, f32[2,128,128]{2,1,0:T(8,128)S(1)}, u32[]{:S(2)}, u32[]{:S(2)}) collective-permute-start(f32[2,128,128]{2,1,0:T(8,128)S(1)} %get-tuple-element.32), channel_id=1, source_target_pairs={{0,8},{4,12},{8,0},{12,4},{1,9},{5,13},{9,1},{13,5},{2,10},{6,14},... | collective-permute-start | bytes 393224 | tf_op jit(solution)/shard_map/ppermute | solution.py:292
  36.6 8.1 %copy-start.1 = (f32[1024,896]{1,0:T(8,128)S(1)}, f32[1024,896]{1,0:T(8,128)}, u32[]{:S(2)}) copy-start(f32[1024,896]{1,0:T(8,128)} %get-tuple-element.25.refs_0_) | copy-start | bytes 11010052
  36.6 8.1 %copy-start.2 = (f32[1024,896]{1,0:T(8,128)S(1)}, f32[1024,896]{1,0:T(8,128)}, u32[]{:S(2)}) copy-start(f32[1024,896]{1,0:T(8,128)} %get-tuple-element.30.refs_1_) | copy-start | bytes 11010052
  53.3 1.3 %collective-permute-start.10 = (f32[4,1040]{1,0:T(4,128)S(1)}, f32[4,1040]{1,0:T(4,128)S(1)}, u32[]{:S(2)}, u32[]{:S(2)}) collective-permute-start(f32[4,1040]{1,0:T(4,128)S(1)} %pad_maximum_fusion.2), channel_id=1, source_target_pairs={{0,4},{4,0},{8,12},{12,8},{1,5},{5,1},{9,13},{13,9},{2,6},{6,2},{1... | collective-permute-start | bytes 49928 | tf_op jit(solution)/shard_map/ppermute | solution.py:258
  54.8 3.8 %collective-permute-start.11 = (f32[8,544]{1,0:T(8,128)S(1)}, f32[8,544]{1,0:T(8,128)S(1)}, u32[]{:S(2)}, u32[]{:S(2)}) collective-permute-start(f32[8,544]{1,0:T(8,128)S(1)} %pad_maximum_fusion.3), channel_id=1, source_target_pairs={{0,1},{1,0},{2,3},{3,2},{4,5},{5,4},{6,7},{7,6},{8,9},{9,8},{10,11... | collective-permute-start | bytes 52232 | tf_op jit(solution)/shard_map/ppermute | solution.py:350
  56.4 3.6 %collective-permute-start.12 = (f32[8,32]{1,0:T(8,128)S(1)}, f32[8,32]{1,0:T(8,128)S(1)}, u32[]{:S(2)}, u32[]{:S(2)}) collective-permute-start(f32[8,32]{1,0:T(8,128)S(1)} %pad_maximum_fusion.7), channel_id=1, source_target_pairs={{0,8},{1,9},{2,10},{3,11},{4,12},{5,13},{6,14},{7,15},{8,0},{9,1},... | collective-permute-start | bytes 3080 | tf_op jit(solution)/shard_map/ppermute | solution.py:350
  57.0 4.5 %collective-permute-start.13 = (f32[8,32]{1,0:T(8,128)S(1)}, f32[8,32]{1,0:T(8,128)S(1)}, u32[]{:S(2)}, u32[]{:S(2)}) collective-permute-start(f32[8,32]{1,0:T(8,128)S(1)} %pad_maximum_fusion.7), channel_id=1, source_target_pairs={{0,9},{1,8},{2,11},{3,10},{4,13},{5,12},{6,15},{7,14},{8,1},{9,0},... | collective-permute-start | bytes 3080 | tf_op jit(solution)/shard_map/ppermute | solution.py:350
  61.6 4.6 %collective-permute-start.14 = (f32[8,288]{1,0:T(8,128)S(1)}, f32[8,288]{1,0:T(8,128)S(1)}, u32[]{:S(2)}, u32[]{:S(2)}) collective-permute-start(f32[8,288]{1,0:T(8,128)S(1)} %pad_maximum_fusion.4), channel_id=1, source_target_pairs={{0,2},{1,3},{2,0},{3,1},{4,6},{5,7},{6,4},{7,5},{8,10},{9,11},{10,... | collective-permute-start | bytes 27656 | tf_op jit(solution)/shard_map/ppermute | solution.py:350

commit v5 on v3

--- a/solution.py
+++ b/solution.py
@@ -263,7 +263,7 @@
             pieces.append((at, n))
         at += n
     pieces = pieces[-1:] + pieces[:-1]
-    cuts = cut(g, pieces[:1])
+    cuts = [g[:, at : at + n] for at, n in pieces[:1]]
     lead = lax.ppermute(cuts[0], "blk", pairs(nb, 2))
     cuts += cut(after(g, cuts[0]), pieces[1:2])
     a_other = to_core(after(a, cuts[0]))

time: 67.1 us -> 67.1 us (level)
  local copies, waits for them, and re-layouts: 1.34 us -> 2.29 us
  Pallas kernels: 33.7 us -> 32.8 us
    slice x0 -> x1, local copies, waits for them, and re-layouts: none -> 0.96 us  [per_device(): cuts = [g[:, at:at + n] for at, n in pieces[:1]]]
    pallas_call x3 -> x2, Pallas kernels: 5.19 us -> 4.27 us  [cut(): pl.pallas_call(functools.partial(cut_kernel, pieces), in_specs=[HBM], out...]
where the time goes in v5:
time: 67.1 us; the launch traced here: 66.8 us
  Pallas kernels  32.8 us (49%)
  starting transfers between devices  17.6 us (26%)
  waiting for transfers between devices  12.6 us (19%)
  local copies, waits for them, and re-layouts  2.29 us (3%)
  between operations  0.93 us (1%)
    pallas_call x2, Pallas kernels, near_call(): pl.pallas_call(kernel, grid=(t // tile,), in_specs=[pl.BlockSpec((tile, n...  14.7 us
    pallas_call x2, Pallas kernels, stream_scores(): pl.pallas_call(functools.partial(stream_kernel, first), grid=(t // tile,)...  11.1 us
    ppermute x4, starting transfers between devices, per_device(): lax.ppermute(x, ('blk', 'width'), [(i * nw + k, (i ^ y_bit) * nw + (k ^ z...  6.09 us
    ppermute x4, waiting for transfers between devices, per_device(): lax.ppermute(x, ('blk', 'width'), [(i * nw + k, (i ^ y_bit) * nw + (k ^ z...  5.18 us
    ppermute x3, starting transfers between devices, per_device(): got = lax.ppermute(mine, 'width', pairs(nw, k)) if k else mine  4.41 us
    pallas_call x2, Pallas kernels, cut(): pl.pallas_call(functools.partial(cut_kernel, pieces), in_specs=[HBM], out...  4.27 us
    ppermute x3, starting transfers between devices, send(): return lax.ppermute(after(x, *others), 'blk', pairs(nb, j))  3.61 us
    ppermute x3, waiting for transfers between devices, send(): return lax.ppermute(after(x, *others), 'blk', pairs(nb, j))  2.94 us
  transfers between devices with their start and end apart: 15, of which 11 were waited for; matrix products, arithmetic and copies ran while one was open for 1% of the time, Pallas kernels for 47%

profile of v5, /device:TPU:0, one launch (start us, length us, event | category | flops | bytes accessed | tf_op | source)
XLA Modules:
  0.0 66.8 jit_solution(1007007520697757190)
XLA Ops:
  0.6 0.0 copy-start.6
  0.6 0.0 copy-start.5
  0.6 1.0 %slice.86 = f32[2,128,128]{2,1,0:T(8,128)S(1)} slice(f32[2,2048,128]{2,1,0:T(8,128)} %g_ref.5), slice={[0:2], [1920:2048], [0:128]} | slice | bytes 262144 | tf_op jit(solution)/shard_map/slice | solution.py:266
  1.6 0.0 copy-start
  1.6 0.5 collective-permute-start.1
  2.1 2.6 %collective-permute-start = (f32[2,128,128]{2,1,0:T(8,128)S(1)}, f32[2,128,128]{2,1,0:T(8,128)S(1)}, u32[]{:S(2)}, u32[]{:S(2)}) collective-permute-start(f32[2,128,128]{2,1,0:T(8,128)S(1)} %slice.86), channel_id=1, source_target_pairs={{0,8},{4,12},{8,0},{12,4},{1,9},{5,13},{9,1},{13,5},{2,10},{6,14},... | collective-permute-start | bytes 393224 | tf_op jit(solution)/shard_map/ppermute | solution.py:267
  4.7 2.2 %shard_map.62 = f32[2,1024,128]{2,1,0:T(8,128)} custom-call(f32[2,2048,128]{2,1,0:T(8,128)} %g_ref.5), custom_call_target="tpu_custom_call" | custom-call | flops 1 | bytes 1 | tf_op jit(solution)/shard_map/pallas_call | solution.py:44
  7.0 0.2 collective-permute-start.9
  7.2 0.0 copy-done.6
  7.2 0.0 copy-done.5
  7.2 1.6 %collective-permute-done.lead_ref = f32[2,128,128]{2,1,0:T(8,128)S(1)} collective-permute-done((f32[2,128,128]{2,1,0:T(8,128)S(1)}, f32[2,128,128]{2,1,0:T(8,128)S(1)}, u32[]{:S(2)}, u32[]{:S(2)}) %collective-permute-start) | collective-permute-done | bytes 131104 | tf_op jit(solution)/shard_map/ppermute | solution.py:267
  8.8 1.8 %collective-permute-start.2 = (f32[258,128]{1,0:T(8,128)S(1)}, f32[258,128]{1,0:T(8,128)S(1)}, u32[]{:S(2)}, u32[]{:S(2)}) collective-permute-start(f32[258,128]{1,0:T(8,128)S(1)} %pad_maximum_fusion), channel_id=1, source_target_pairs={{0,1},{1,0},{2,3},{3,2},{4,5},{5,4},{6,7},{7,6},{8,9},{9,8},{10,11... | collective-permute-start | bytes 396296 | tf_op jit(solution)/shard_map/ppermute | solution.py:289
  10.6 2.6 %collective-permute-start.3 = (f32[258,128]{1,0:T(8,128)S(1)}, f32[258,128]{1,0:T(8,128)S(1)}, u32[]{:S(2)}, u32[]{:S(2)}) collective-permute-start(f32[258,128]{1,0:T(8,128)S(1)} %pad_maximum_fusion), channel_id=1, source_target_pairs={{0,2},{1,3},{2,0},{3,1},{4,6},{5,7},{6,4},{7,5},{8,10},{9,11},{10,... | collective-permute-start | bytes 396296 | tf_op jit(solution)/shard_map/ppermute | solution.py:289
  13.2 0.0 collective-permute-start.4
  13.2 2.0 %shard_map.59 = (f32[2,512,128]{2,1,0:T(8,128)}, f32[2,256,128]{2,1,0:T(8,128)}, f32[2,128,128]{2,1,0:T(8,128)S(1)}) custom-call(f32[2,2048,128]{2,1,0:T(8,128)} %g_ref.5), custom_call_target="tpu_custom_call" | custom-call | flops 1 | bytes 1 | tf_op jit(solution)/shard_map/pallas_call | solution.py:44
  15.3 0.0 copy-done
  15.3 6.9 %shard_map.60 = (f32[1024,256]{1,0:T(8,128)S(1)}, f32[1024,256]{1,0:T(8,128)S(1)}, f32[1024,384]{1,0:T(8,128)S(1)}) custom-call(f32[1024,2048]{1,0:T(8,128)} %refs_0_.3, f32[2,2048,128]{2,1,0:T(8,128)S(1)} %copy-done, f32[2,128,128]{2,1,0:T(8,128)S(1)} %collective-permute-done.lead_ref), custom_call_target="tpu_custom_call" | custom-call | flops 1 | bytes 1 | tf_op jit(solution)/shard_map/pallas_call | solution.py:143
  22.2 0.0 copy-start.1
  22.3 0.0 collective-permute-done.2
  22.4 1.3 %collective-permute-done.3 = f32[258,128]{1,0:T(8,128)S(1)} collective-permute-done((f32[258,128]{1,0:T(8,128)S(1)}, f32[258,128]{1,0:T(8,128)S(1)}, u32[]{:S(2)}, u32[]{:S(2)}) %collective-permute-start.3) | collective-permute-done | bytes 132128 | tf_op jit(solution)/shard_map/ppermute | solution.py:289
  23.7 0.0 collective-permute-done.4
  23.8 0.1 collective-permute-start.5
  23.8 1.6 %collective-permute-start.8 = (f32[2,512,128]{2,1,0:T(8,128)}, f32[2,512,128]{2,1,0:T(8,128)}, u32[]{:S(2)}, u32[]{:S(2)}) collective-permute-start(f32[2,512,128]{2,1,0:T(8,128)} %get-tuple-element.36), channel_id=1, source_target_pairs={{0,8},{4,12},{8,0},{12,4},{1,9},{5,13},{9,1},{13,5},{2,10},{6,14},... | collective-permute-start | bytes 1572872 | tf_op jit(solution)/shard_map/ppermute | solution.py:280
  25.4 0.3 collective-permute-done.5.oo_ref.refs_3_
  25.8 0.0 collective-permute-done.1.a_ref.refs_1_
  25.8 7.8 %shard_map.61 = (f32[4,2048]{1,0:T(4,128)S(1)}, f32[1024,384]{1,0:T(8,128)S(1)}) custom-call(f32[1024,2048]{1,0:T(8,128)} %collective-permute-done.1.a_ref.refs_1_, f32[1032,128]{1,0:T(8,128)S(1)} %constant_dynamic-update-slice_fusion.o_ref.refs_2_, f32[1032,128]{1,0:T(8,128)S(1)} %collective-permute-done.5.oo_ref.refs_3_, ...), custom_call_target="tpu_custom_call" | custom-call | flops 1 | bytes 1 | tf_op jit(solution)/shard_map/pallas_call | solution.py:143
  33.5 0.0 copy-done.1
  33.6 0.0 copy-start.3
  33.6 1.1 %copy-done.3 = f32[1024,384]{1,0:T(8,128)} copy-done((f32[1024,384]{1,0:T(8,128)}, f32[1024,384]{1,0:T(8,128)S(1)}, u32[]{:S(2)}) %copy-start.3) | copy-done | bytes 1572888
  34.7 1.5 %collective-permute-start.7 = (f32[2,256,128]{2,1,0:T(8,128)}, f32[2,256,128]{2,1,0:T(8,128)S(1)}, u32[]{:S(2)}, u32[]{:S(2)}) collective-permute-start(f32[2,256,128]{2,1,0:T(8,128)} %get-tuple-element.35), channel_id=1, source_target_pairs={{0,8},{4,12},{8,0},{12,4},{1,9},{5,13},{9,1},{13,5},{2,10},{6,14},... | collective-permute-start | bytes 786440 | tf_op jit(solution)/shard_map/ppermute | solution.py:280
  36.2 0.5 collective-permute-start.6
  36.7 0.1 convert_reduce_fusion
  36.9 0.0 collective-permute-done.9.refs_4_
  36.9 6.8 %shard_map.63.refs_5_ = f32[4,2048]{1,0:T(4,128)S(1)} custom-call(f32[1024,2048]{1,0:T(8,128)} %refs_0_.3, f32[1024,2048]{1,0:T(8,128)} %collective-permute-done.1.a_ref.refs_1_, f32[1032,128]{1,0:T(8,128)S(1)} %constant_dynamic-update-slice_fusion.o_ref.refs_2_, f32[1032,128]{1,0:T(8,128)S(1)} %collective-permute-done.5.oo_ref.refs_3_, ...), custom_call_target="tpu_custom_call" | custom-call | flops 1 | bytes 1 | tf_op jit(solution)/shard_map/pallas_call | solution.py:186
  43.7 0.0 copy-start.2
  43.7 0.0 copy-start.4
  43.7 0.9 %collective-permute-done.8.refs_4_ = f32[2,512,128]{2,1,0:T(8,128)} collective-permute-done((f32[2,512,128]{2,1,0:T(8,128)}, f32[2,512,128]{2,1,0:T(8,128)}, u32[]{:S(2)}, u32[]{:S(2)}) %collective-permute-start.8) | collective-permute-done | bytes 524320 | tf_op jit(solution)/shard_map/ppermute | solution.py:280
  44.6 4.3 %shard_map.64.refs_5_ = f32[4,2048]{1,0:T(4,128)S(1)} custom-call(f32[1024,2048]{1,0:T(8,128)} %refs_0_.3, f32[1024,2048]{1,0:T(8,128)} %collective-permute-done.1.a_ref.refs_1_, f32[1032,128]{1,0:T(8,128)S(1)} %constant_dynamic-update-slice_fusion.o_ref.refs_2_, f32[1032,128]{1,0:T(8,128)S(1)} %collective-permute-done.5.oo_ref.refs_3_, ...), custom_call_target="tpu_custom_call" | custom-call | flops 1 | bytes 1 | tf_op jit(solution)/shard_map/pallas_call | solution.py:186
  48.9 1.2 %collective-permute-done.7.refs_4_ = f32[2,256,128]{2,1,0:T(8,128)S(1)} collective-permute-done((f32[2,256,128]{2,1,0:T(8,128)}, f32[2,256,128]{2,1,0:T(8,128)S(1)}, u32[]{:S(2)}, u32[]{:S(2)}) %collective-permute-start.7) | collective-permute-done | bytes 262176 | tf_op jit(solution)/shard_map/ppermute | solution.py:280
  50.1 0.0 copy-done.2
  50.1 0.0 copy-done.4
  50.1 1.2 %shard_map.65.refs_5_ = f32[4,2048]{1,0:T(4,128)S(1)} custom-call(f32[1024,384]{1,0:T(8,128)S(1)} %copy-done.2, f32[1024,384]{1,0:T(8,128)S(1)} %copy-done.4, f32[1032,128]{1,0:T(8,128)S(1)} %constant_dynamic-update-slice_fusion.o_ref.refs_2_, f32[1032,128]{1,0:T(8,128)S(1)} %collective-permute-done.5.oo_ref.refs_3_, ...), custom_call_target="tpu_custom_call" | custom-call | flops 1 | bytes 1 | tf_op jit(solution)/shard_map/pallas_call | solution.py:215
  51.3 0.8 %collective-permute-done.6.refs_4_ = f32[2,128,128]{2,1,0:T(8,128)S(1)} collective-permute-done((f32[2,128,128]{2,1,0:T(8,128)S(1)}, f32[2,128,128]{2,1,0:T(8,128)S(1)}, u32[]{:S(2)}, u32[]{:S(2)}) %collective-permute-start.6) | collective-permute-done | bytes 131104 | tf_op jit(solution)/shard_map/ppermute | solution.py:280
  52.1 0.9 %shard_map.66 = f32[4,2048]{1,0:T(4,128)S(1)} custom-call(f32[1024,384]{1,0:T(8,128)S(1)} %copy-done.2, f32[1024,384]{1,0:T(8,128)S(1)} %copy-done.4, f32[1032,128]{1,0:T(8,128)S(1)} %constant_dynamic-update-slice_fusion.o_ref.refs_2_, f32[1032,128]{1,0:T(8,128)S(1)} %collective-permute-done.5.oo_ref.refs_3_, ...), custom_call_target="tpu_custom_call" | custom-call | flops 1 | bytes 1 | tf_op jit(solution)/shard_map/pallas_call | solution.py:215
  53.0 0.1 fusion
  53.2 0.1 pad_maximum_fusion.2
  53.3 0.1 collective-permute-start.10
  53.3 1.2 %collective-permute-done.10 = f32[4,1040]{1,0:T(4,128)S(1)} collective-permute-done((f32[4,1040]{1,0:T(4,128)S(1)}, f32[4,1040]{1,0:T(4,128)S(1)}, u32[]{:S(2)}, u32[]{:S(2)}) %collective-permute-start.10) | collective-permute-done | bytes 16672 | tf_op jit(solution)/shard_map/ppermute | solution.py:254
  54.6 0.1 pad_maximum_fusion.3
  54.7 1.6 %collective-permute-start.11 = (f32[8,544]{1,0:T(8,128)S(1)}, f32[8,544]{1,0:T(8,128)S(1)}, u32[]{:S(2)}, u32[]{:S(2)}) collective-permute-start(f32[8,544]{1,0:T(8,128)S(1)} %pad_maximum_fusion.3), channel_id=1, source_target_pairs={{0,1},{1,0},{2,3},{3,2},{4,5},{5,4},{6,7},{7,6},{8,9},{9,8},{10,11... | collective-permute-start | bytes 52232 | tf_op jit(solution)/shard_map/ppermute | solution.py:337
  56.3 0.1 pad_maximum_fusion.7
  56.4 0.6 collective-permute-start.12
  56.9 1.3 %collective-permute-start.13 = (f32[8,32]{1,0:T(8,128)S(1)}, f32[8,32]{1,0:T(8,128)S(1)}, u32[]{:S(2)}, u32[]{:S(2)}) collective-permute-start(f32[8,32]{1,0:T(8,128)S(1)} %pad_maximum_fusion.7), channel_id=1, source_target_pairs={{0,9},{1,8},{2,11},{3,10},{4,13},{5,12},{6,15},{7,14},{8,1},{9,0},... | collective-permute-start | bytes 3080 | tf_op jit(solution)/shard_map/ppermute | solution.py:337
  58.3 0.2 collective-permute-done.11
  58.5 1.5 %collective-permute-done.12 = f32[8,32]{1,0:T(8,128)S(1)} collective-permute-done((f32[8,32]{1,0:T(8,128)S(1)}, f32[8,32]{1,0:T(8,128)S(1)}, u32[]{:S(2)}, u32[]{:S(2)}) %collective-permute-start.12) | collective-permute-done | bytes 1056 | tf_op jit(solution)/shard_map/ppermute | solution.py:337
  60.0 1.5 %collective-permute-done.13 = f32[8,32]{1,0:T(8,128)S(1)} collective-permute-done((f32[8,32]{1,0:T(8,128)S(1)}, f32[8,32]{1,0:T(8,128)S(1)}, u32[]{:S(2)}, u32[]{:S(2)}) %collective-permute-start.13) | collective-permute-done | bytes 1056 | tf_op jit(solution)/shard_map/ppermute | solution.py:337
  61.4 0.1 fusion.3
  61.5 2.6 %collective-permute-start.14 = (f32[8,288]{1,0:T(8,128)S(1)}, f32[8,288]{1,0:T(8,128)S(1)}, u32[]{:S(2)}, u32[]{:S(2)}) collective-permute-start(f32[8,288]{1,0:T(8,128)S(1)} %pad_maximum_fusion.4), channel_id=1, source_target_pairs={{0,2},{1,3},{2,0},{3,1},{4,6},{5,7},{6,4},{7,5},{8,10},{9,11},{10,... | collective-permute-start | bytes 27656 | tf_op jit(solution)/shard_map/ppermute | solution.py:337
  64.1 2.0 %collective-permute-done.14 = f32[8,288]{1,0:T(8,128)S(1)} collective-permute-done((f32[8,288]{1,0:T(8,128)S(1)}, f32[8,288]{1,0:T(8,128)S(1)}, u32[]{:S(2)}, u32[]{:S(2)}) %collective-permute-start.14) | collective-permute-done | bytes 9248 | tf_op jit(solution)/shard_map/ppermute | solution.py:337
  66.1 0.7 %shard_map.67 = (f32[8,256]{1,0:T(8,128)}, f32[8,16]{1,0:T(8,128)}) custom-call(f32[8,256]{1,0:T(8,128)S(1)} %slice_add_fusion.s_ref, f32[8,32]{1,0:T(8,128)S(1)} %slice_add_fusion.3.doc_ref), custom_call_target="tpu_custom_call" | custom-call | flops 1 | bytes 1 | tf_op jit(solution)/shard_map/pallas_call | solution.py:233
  (26 shorter events, 0.3 us)
Async XLA Ops:
  0.6 6.6 %copy-start.6 = (s32[256]{0:T(256)S(1)}, s32[256]{0:T(256)}, u32[]{:S(2)}) copy-start(s32[256]{0:T(256)} %param.7) | copy-start | bytes 3076
  0.6 6.5 %copy-start.5 = (f32[256,128]{1,0:T(8,128)S(1)}, f32[256,128]{1,0:T(8,128)}, u32[]{:S(2)}) copy-start(f32[256,128]{1,0:T(8,128)} %param.6) | copy-start | bytes 393220
  1.6 13.7 %copy-start = (f32[2,2048,128]{2,1,0:T(8,128)S(1)}, f32[2,2048,128]{2,1,0:T(8,128)}, u32[]{:S(2)}) copy-start(f32[2,2048,128]{2,1,0:T(8,128)} %g_ref.5) | copy-start | bytes 6291460
  1.6 24.1 %collective-permute-start.1 = (f32[1024,2048]{1,0:T(8,128)}, f32[1024,2048]{1,0:T(8,128)}, u32[]{:S(2)}, u32[]{:S(2)}) collective-permute-start(f32[1024,2048]{1,0:T(8,128)} %refs_0_.3), channel_id=1, source_target_pairs={{0,4},{4,0},{8,12},{12,8},{1,5},{5,1},{9,13},{13,9},{2,6},{6,2},{1... | collective-permute-start | bytes 25165832 | tf_op jit(solution)/shard_map/ppermute | solution.py:254
  2.1 6.7 %collective-permute-start = (f32[2,128,128]{2,1,0:T(8,128)S(1)}, f32[2,128,128]{2,1,0:T(8,128)S(1)}, u32[]{:S(2)}, u32[]{:S(2)}) collective-permute-start(f32[2,128,128]{2,1,0:T(8,128)S(1)} %slice.86), channel_id=1, source_target_pairs={{0,8},{4,12},{8,0},{12,4},{1,9},{5,13},{9,1},{13,5},{2,10},{6,14},... | collective-permute-start | bytes 393224 | tf_op jit(solution)/shard_map/ppermute | solution.py:267
  7.0 29.9 %collective-permute-start.9 = (f32[2,1024,128]{2,1,0:T(8,128)}, f32[2,1024,128]{2,1,0:T(8,128)}, u32[]{:S(2)}, u32[]{:S(2)}) collective-permute-start(f32[2,1024,128]{2,1,0:T(8,128)} %shard_map.62), channel_id=1, source_target_pairs={{0,8},{4,12},{8,0},{12,4},{1,9},{5,13},{9,1},{13,5},{2,10},{6,14},... | collective-permute-start | bytes 3145736 | tf_op jit(solution)/shard_map/ppermute | solution.py:282
  8.8 13.5 %collective-permute-start.2 = (f32[258,128]{1,0:T(8,128)S(1)}, f32[258,128]{1,0:T(8,128)S(1)}, u32[]{:S(2)}, u32[]{:S(2)}) collective-permute-start(f32[258,128]{1,0:T(8,128)S(1)} %pad_maximum_fusion), channel_id=1, source_target_pairs={{0,1},{1,0},{2,3},{3,2},{4,5},{5,4},{6,7},{7,6},{8,9},{9,8},{10,11... | collective-permute-start | bytes 396296 | tf_op jit(solution)/shard_map/ppermute | solution.py:289
  10.6 13.0 %collective-permute-start.3 = (f32[258,128]{1,0:T(8,128)S(1)}, f32[258,128]{1,0:T(8,128)S(1)}, u32[]{:S(2)}, u32[]{:S(2)}) collective-permute-start(f32[258,128]{1,0:T(8,128)S(1)} %pad_maximum_fusion), channel_id=1, source_target_pairs={{0,2},{1,3},{2,0},{3,1},{4,6},{5,7},{6,4},{7,5},{8,10},{9,11},{10,... | collective-permute-start | bytes 396296 | tf_op jit(solution)/shard_map/ppermute | solution.py:289
  13.2 10.5 %collective-permute-start.4 = (f32[258,128]{1,0:T(8,128)S(1)}, f32[258,128]{1,0:T(8,128)S(1)}, u32[]{:S(2)}, u32[]{:S(2)}) collective-permute-start(f32[258,128]{1,0:T(8,128)S(1)} %pad_maximum_fusion), channel_id=1, source_target_pairs={{0,3},{1,2},{2,1},{3,0},{4,7},{5,6},{6,5},{7,4},{8,11},{9,10},{10,... | collective-permute-start | bytes 396296 | tf_op jit(solution)/shard_map/ppermute | solution.py:289
  22.2 11.3 %copy-start.1 = (f32[1024,384]{1,0:T(8,128)}, f32[1024,384]{1,0:T(8,128)S(1)}, u32[]{:S(2)}) copy-start(f32[1024,384]{1,0:T(8,128)S(1)} %get-tuple-element.26.refs_0_) | copy-start | bytes 4718596
  23.8 2.0 %collective-permute-start.5 = (f32[1032,128]{1,0:T(8,128)S(1)}, f32[1032,128]{1,0:T(8,128)S(1)}, u32[]{:S(2)}, u32[]{:S(2)}) collective-permute-start(f32[1032,128]{1,0:T(8,128)S(1)} %constant_dynamic-update-slice_fusion.o_ref.refs_2_), channel_id=1, source_target_pairs={{0,4},{4,0},{8,12},{12,8},{1,5},{5,1},{9,13},{13,9},{2,6},{6,2},{1... | collective-permute-start | bytes 1585160 | tf_op jit(solution)/shard_map/ppermute | solution.py:254
  23.8 20.8 %collective-permute-start.8 = (f32[2,512,128]{2,1,0:T(8,128)}, f32[2,512,128]{2,1,0:T(8,128)}, u32[]{:S(2)}, u32[]{:S(2)}) collective-permute-start(f32[2,512,128]{2,1,0:T(8,128)} %get-tuple-element.36), channel_id=1, source_target_pairs={{0,8},{4,12},{8,0},{12,4},{1,9},{5,13},{9,1},{13,5},{2,10},{6,14},... | collective-permute-start | bytes 1572872 | tf_op jit(solution)/shard_map/ppermute | solution.py:280
  33.6 1.1 %copy-start.3 = (f32[1024,384]{1,0:T(8,128)}, f32[1024,384]{1,0:T(8,128)S(1)}, u32[]{:S(2)}) copy-start(f32[1024,384]{1,0:T(8,128)S(1)} %get-tuple-element.32.refs_1_) | copy-start | bytes 4718596
  34.7 15.4 %collective-permute-start.7 = (f32[2,256,128]{2,1,0:T(8,128)}, f32[2,256,128]{2,1,0:T(8,128)S(1)}, u32[]{:S(2)}, u32[]{:S(2)}) collective-permute-start(f32[2,256,128]{2,1,0:T(8,128)} %get-tuple-element.35), channel_id=1, source_target_pairs={{0,8},{4,12},{8,0},{12,4},{1,9},{5,13},{9,1},{13,5},{2,10},{6,14},... | collective-permute-start | bytes 786440 | tf_op jit(solution)/shard_map/ppermute | solution.py:280
  36.2 15.9 %collective-permute-start.6 = (f32[2,128,128]{2,1,0:T(8,128)S(1)}, f32[2,128,128]{2,1,0:T(8,128)S(1)}, u32[]{:S(2)}, u32[]{:S(2)}) collective-permute-start(f32[2,128,128]{2,1,0:T(8,128)S(1)} %get-tuple-element.34), channel_id=1, source_target_pairs={{0,8},{4,12},{8,0},{12,4},{1,9},{5,13},{9,1},{13,5},{2,10},{6,14},... | collective-permute-start | bytes 393224 | tf_op jit(solution)/shard_map/ppermute | solution.py:280
  43.7 6.4 %copy-start.2 = (f32[1024,384]{1,0:T(8,128)S(1)}, f32[1024,384]{1,0:T(8,128)}, u32[]{:S(2)}) copy-start(f32[1024,384]{1,0:T(8,128)} %copy-done.1) | copy-start | bytes 4718596
  43.7 6.4 %copy-start.4 = (f32[1024,384]{1,0:T(8,128)S(1)}, f32[1024,384]{1,0:T(8,128)}, u32[]{:S(2)}) copy-start(f32[1024,384]{1,0:T(8,128)} %copy-done.3) | copy-start | bytes 4718596
  53.3 1.3 %collective-permute-start.10 = (f32[4,1040]{1,0:T(4,128)S(1)}, f32[4,1040]{1,0:T(4,128)S(1)}, u32[]{:S(2)}, u32[]{:S(2)}) collective-permute-start(f32[4,1040]{1,0:T(4,128)S(1)} %pad_maximum_fusion.2), channel_id=1, source_target_pairs={{0,4},{4,0},{8,12},{12,8},{1,5},{5,1},{9,13},{13,9},{2,6},{6,2},{1... | collective-permute-start | bytes 49928 | tf_op jit(solution)/shard_map/ppermute | solution.py:254
  54.7 3.8 %collective-permute-start.11 = (f32[8,544]{1,0:T(8,128)S(1)}, f32[8,544]{1,0:T(8,128)S(1)}, u32[]{:S(2)}, u32[]{:S(2)}) collective-permute-start(f32[8,544]{1,0:T(8,128)S(1)} %pad_maximum_fusion.3), channel_id=1, source_target_pairs={{0,1},{1,0},{2,3},{3,2},{4,5},{5,4},{6,7},{7,6},{8,9},{9,8},{10,11... | collective-permute-start | bytes 52232 | tf_op jit(solution)/shard_map/ppermute | solution.py:337
  56.4 3.6 %collective-permute-start.12 = (f32[8,32]{1,0:T(8,128)S(1)}, f32[8,32]{1,0:T(8,128)S(1)}, u32[]{:S(2)}, u32[]{:S(2)}) collective-permute-start(f32[8,32]{1,0:T(8,128)S(1)} %pad_maximum_fusion.7), channel_id=1, source_target_pairs={{0,8},{1,9},{2,10},{3,11},{4,12},{5,13},{6,14},{7,15},{8,0},{9,1},... | collective-permute-start | bytes 3080 | tf_op jit(solution)/shard_map/ppermute | solution.py:337
  56.9 4.5 %collective-permute-start.13 = (f32[8,32]{1,0:T(8,128)S(1)}, f32[8,32]{1,0:T(8,128)S(1)}, u32[]{:S(2)}, u32[]{:S(2)}) collective-permute-start(f32[8,32]{1,0:T(8,128)S(1)} %pad_maximum_fusion.7), channel_id=1, source_target_pairs={{0,9},{1,8},{2,11},{3,10},{4,13},{5,12},{6,15},{7,14},{8,1},{9,0},... | collective-permute-start | bytes 3080 | tf_op jit(solution)/shard_map/ppermute | solution.py:337
  61.5 4.6 %collective-permute-start.14 = (f32[8,288]{1,0:T(8,128)S(1)}, f32[8,288]{1,0:T(8,128)S(1)}, u32[]{:S(2)}, u32[]{:S(2)}) collective-permute-start(f32[8,288]{1,0:T(8,128)S(1)} %pad_maximum_fusion.4), channel_id=1, source_target_pairs={{0,2},{1,3},{2,0},{3,1},{4,6},{5,7},{6,4},{7,5},{8,10},{9,11},{10,... | collective-permute-start | bytes 27656 | tf_op jit(solution)/shard_map/ppermute | solution.py:337

commit v6 on v4

--- a/solution.py
+++ b/solution.py
@@ -11,8 +11,8 @@
 LANES = 128
 F32, BF16 = jnp.float32, jnp.bfloat16
 TILE = 256
-LEADS = 1
-PARTS = (2, 4, 8, 16, 16)
+LEADS = 2
+PARTS = (2, 4, 16, 16, 16, 16)
 VMEM = pl.BlockSpec(memory_space=pltpu.VMEM)
 HBM = pl.BlockSpec(memory_space=pltpu.HBM)
 PARAMS = pltpu.CompilerParams(vmem_limit_bytes=16 << 20)

time: 67.3 us -> 67.4 us (level)
  starting transfers between devices: 17.6 us -> 19.9 us
  other arithmetic: 2.13 us -> 0.55 us
    ppermute x1, starting transfers between devices: 0.08 us -> 2 us  [per_device(): lax.ppermute(cuts[LEADS], 'blk', pairs(nb, 2))]
    ppermute x3, waiting for transfers between devices: 4.44 us -> 3.18 us  [send(): return lax.ppermute(after(x, *others), 'blk', pairs(nb, j))]
    ppermute x4, waiting for transfers between devices: 5.18 us -> 6.37 us  [per_device(): lax.ppermute(x, ('blk', 'width'), [(i * nw + k, (i ^ y_bit) * nw + (k ^ z...]
    concatenate x1, other arithmetic: 0.91 us -> 0.01 us  [per_device(): mine = after(jnp.concatenate([o, flat], axis=0), lead)]
    reshape x1, other arithmetic: 0.68 us -> 0.01 us  [per_device(): flat = ids.astype(F32).reshape(rows, LANES)]
    ppermute x1 -> x2, starting transfers between devices: 2.6 us -> 2.69 us  [per_device(): leads = [lax.ppermute(x, 'blk', pairs(nb, 2)) for x in cuts]]
  transfers between devices with their start and end apart: 15 -> 16, of which waited for: 11 -> 8; matrix products, arithmetic and copies ran while one was open for 3% -> 1% of each run, Pallas kernels for 47% -> 47%
where the time goes in v6:
time: 67.4 us; the launch traced here: 67 us
  Pallas kernels  33.1 us (49%)
  starting transfers between devices  19.9 us (30%)
  waiting for transfers between devices  11.1 us (16%)
  local copies, waits for them, and re-layouts  1.34 us (2%)
  between operations  0.92 us (1%)
    pallas_call x2, Pallas kernels, near_call(): pl.pallas_call(kernel, grid=(t // tile,), in_specs=[tiles(x.shape[1]) for...  16.5 us
    pallas_call x1, Pallas kernels, stream_scores(): pl.pallas_call(functools.partial(stream_kernel, first), grid=(t // tile,)...  6.93 us
    ppermute x4, waiting for transfers between devices, per_device(): lax.ppermute(x, ('blk', 'width'), [(i * nw + k, (i ^ y_bit) * nw + (k ^ z...  6.37 us
    ppermute x4, starting transfers between devices, per_device(): lax.ppermute(x, ('blk', 'width'), [(i * nw + k, (i ^ y_bit) * nw + (k ^ z...  6.09 us
    ppermute x3, starting transfers between devices, per_device(): got = lax.ppermute(mine, 'width', pairs(nw, k)) if k else mine  4.87 us
    pallas_call x3, Pallas kernels, staged_scores(): pl.pallas_call(functools.partial(staged_kernel, start, first), in_specs=[...  4.79 us
    pallas_call x2, Pallas kernels, cut(): pl.pallas_call(functools.partial(cut_kernel, pieces), in_specs=[HBM], out...  4.14 us
    ppermute x3, starting transfers between devices, send(): return lax.ppermute(after(x, *others), 'blk', pairs(nb, j))  3.63 us
  transfers between devices with their start and end apart: 16, of which 8 were waited for; matrix products, arithmetic and copies ran while one was open for 1% of the time, Pallas kernels for 47%

profile of v6, /device:TPU:0, one launch (start us, length us, event | category | flops | bytes accessed | tf_op | source)
XLA Modules:
  0.0 67.0 jit_solution(12054475377780972618)
XLA Ops:
  0.6 0.0 copy-start
  0.6 0.0 copy-start.6
  0.7 0.0 copy-start.5
  0.7 1.1 %fusion.5 = (f32[2,128,128]{2,1,0:T(8,128)S(1)}, f32[2,128,128]{2,1,0:T(8,128)S(1)}) fusion(f32[2,2048,128]{2,1,0:T(8,128)} %g_ref.5), kind=kLoop, calls=%fused_computation.43 | loop fusion | bytes 524288 | tf_op jit(solution)/shard_map/slice | solution.py:270
  1.8 0.5 collective-permute-start.2
  2.3 2.6 %collective-permute-start = (f32[2,128,128]{2,1,0:T(8,128)S(1)}, f32[2,128,128]{2,1,0:T(8,128)S(1)}, u32[]{:S(2)}, u32[]{:S(2)}) collective-permute-start(f32[2,128,128]{2,1,0:T(8,128)S(1)} %get-tuple-element.45), channel_id=1, source_target_pairs={{0,8},{4,12},{8,0},{12,4},{1,9},{5,13},{9,1},{13,5},{2,10},{6,14},... | collective-permute-start | bytes 393224 | tf_op jit(solution)/shard_map/ppermute | solution.py:271
  4.9 0.1 collective-permute-start.1
  5.0 2.2 %shard_map.62 = f32[2,1024,128]{2,1,0:T(8,128)} custom-call(f32[2,2048,128]{2,1,0:T(8,128)} %g_ref.5), custom_call_target="tpu_custom_call" | custom-call | flops 1 | bytes 1 | tf_op jit(solution)/shard_map/pallas_call | solution.py:45
  7.2 2.0 %collective-permute-start.10 = (f32[2,1024,128]{2,1,0:T(8,128)}, f32[2,1024,128]{2,1,0:T(8,128)}, u32[]{:S(2)}, u32[]{:S(2)}) collective-permute-start(f32[2,1024,128]{2,1,0:T(8,128)} %shard_map.62), channel_id=1, source_target_pairs={{0,8},{4,12},{8,0},{12,4},{1,9},{5,13},{9,1},{13,5},{2,10},{6,14},... | collective-permute-start | bytes 3145736 | tf_op jit(solution)/shard_map/ppermute | solution.py:294
  9.2 0.0 copy-done.6
  9.2 0.0 copy-done.5
  9.2 0.0 collective-permute-done.refs_0_
  9.3 2.0 %collective-permute-start.3 = (f32[258,128]{1,0:T(8,128)S(1)}, f32[258,128]{1,0:T(8,128)S(1)}, u32[]{:S(2)}, u32[]{:S(2)}) collective-permute-start(f32[258,128]{1,0:T(8,128)S(1)} %pad_maximum_fusion), channel_id=1, source_target_pairs={{0,1},{1,0},{2,3},{3,2},{4,5},{5,4},{6,7},{7,6},{8,9},{9,8},{10,11... | collective-permute-start | bytes 396296 | tf_op jit(solution)/shard_map/ppermute | solution.py:301
  11.3 2.6 %collective-permute-start.4 = (f32[258,128]{1,0:T(8,128)S(1)}, f32[258,128]{1,0:T(8,128)S(1)}, u32[]{:S(2)}, u32[]{:S(2)}) collective-permute-start(f32[258,128]{1,0:T(8,128)S(1)} %pad_maximum_fusion), channel_id=1, source_target_pairs={{0,2},{1,3},{2,0},{3,1},{4,6},{5,7},{6,4},{7,5},{8,10},{9,11},{10,... | collective-permute-start | bytes 396296 | tf_op jit(solution)/shard_map/ppermute | solution.py:301
  13.9 1.9 %shard_map.59 = (f32[2,512,128]{2,1,0:T(8,128)}, f32[2,128,128]{2,1,0:T(8,128)S(1)}, f32[2,128,128]{2,1,0:T(8,128)S(1)}) custom-call(f32[2,2048,128]{2,1,0:T(8,128)} %g_ref.5), custom_call_target="tpu_custom_call" | custom-call | flops 1 | bytes 1 | tf_op jit(solution)/shard_map/pallas_call | solution.py:45
  15.8 0.0 copy-start.3
  15.8 0.0 collective-permute-done.1.refs_1_
  15.9 0.3 collective-permute-start.5
  16.1 0.0 copy-done
  16.1 8.1 %shard_map.60 = (f32[1024,512]{1,0:T(8,128)}, f32[1024,768]{1,0:T(8,128)}) custom-call(f32[1024,2048]{1,0:T(8,128)} %refs_0_.1, f32[2,2048,128]{2,1,0:T(8,128)S(1)} %copy-done, f32[2,128,128]{2,1,0:T(8,128)S(1)} %collective-permute-done.refs_0_, f32[2,128,128]{2,1,0:T(8,128)S(1)} %collective-permute-done.1.refs_1_), custom_call_target="tpu_custom_call" | custom-call | flops 1 | bytes 1 | tf_op jit(solution)/shard_map/pallas_call | solution.py:146
  24.3 0.0 copy-done.3
  24.4 0.0 collective-permute-done.3
  24.4 0.0 collective-permute-done.4
  24.5 0.0 collective-permute-done.5
  24.5 0.1 collective-permute-start.6
  24.6 1.6 %collective-permute-start.9 = (f32[2,512,128]{2,1,0:T(8,128)}, f32[2,512,128]{2,1,0:T(8,128)}, u32[]{:S(2)}, u32[]{:S(2)}) collective-permute-start(f32[2,512,128]{2,1,0:T(8,128)} %get-tuple-element.34), channel_id=1, source_target_pairs={{0,8},{4,12},{8,0},{12,4},{1,9},{5,13},{9,1},{13,5},{2,10},{6,14},... | collective-permute-start | bytes 1572872 | tf_op jit(solution)/shard_map/ppermute | solution.py:292
  26.2 0.3 collective-permute-done.6.oo_ref.refs_3_
  26.5 0.0 copy-start.4
  26.5 0.0 collective-permute-done.2.a_ref.refs_1_
  26.5 8.4 %shard_map.61 = (f32[4,2048]{1,0:T(4,128)S(1)}, f32[1024,768]{1,0:T(8,128)}) custom-call(f32[1024,2048]{1,0:T(8,128)} %collective-permute-done.2.a_ref.refs_1_, f32[1024,512]{1,0:T(8,128)} %get-tuple-element.27.p_ref, f32[1032,128]{1,0:T(8,128)S(1)} %constant_dynamic-update-slice_fusion.o_ref.refs_2_, f32[1032,128]{1,0:T(8,128)S(1)} %collective-permute-done.6.oo_ref.refs_3_, ...), custom_call_target="tpu_custom_call" | custom-call | flops 1 | bytes 1 | tf_op jit(solution)/shard_map/pallas_call | solution.py:146
  34.9 0.0 copy-done.4
  34.9 1.5 %collective-permute-start.8 = (f32[2,128,128]{2,1,0:T(8,128)S(1)}, f32[2,128,128]{2,1,0:T(8,128)S(1)}, u32[]{:S(2)}, u32[]{:S(2)}) collective-permute-start(f32[2,128,128]{2,1,0:T(8,128)S(1)} %copy-done.4), channel_id=1, source_target_pairs={{0,8},{4,12},{8,0},{12,4},{1,9},{5,13},{9,1},{13,5},{2,10},{6,14},... | collective-permute-start | bytes 393224 | tf_op jit(solution)/shard_map/ppermute | solution.py:292
  36.4 0.5 collective-permute-start.7
  36.9 0.1 convert_reduce_fusion
  37.1 0.0 copy-start.1
  37.1 0.0 copy-start.2
  37.1 0.0 collective-permute-done.10.refs_4_
  37.1 6.9 %shard_map.63.refs_5_ = f32[4,2048]{1,0:T(4,128)S(1)} custom-call(f32[1024,2048]{1,0:T(8,128)} %refs_0_.1, f32[1024,2048]{1,0:T(8,128)} %collective-permute-done.2.a_ref.refs_1_, f32[1032,128]{1,0:T(8,128)S(1)} %constant_dynamic-update-slice_fusion.o_ref.refs_2_, f32[1032,128]{1,0:T(8,128)S(1)} %collective-permute-done.6.oo_ref.refs_3_, ...), custom_call_target="tpu_custom_call" | custom-call | flops 1 | bytes 1 | tf_op jit(solution)/shard_map/pallas_call | solution.py:190
  44.0 1.9 %collective-permute-done.9.refs_4_ = f32[2,512,128]{2,1,0:T(8,128)} collective-permute-done((f32[2,512,128]{2,1,0:T(8,128)}, f32[2,512,128]{2,1,0:T(8,128)}, u32[]{:S(2)}, u32[]{:S(2)}) %collective-permute-start.9) | collective-permute-done | bytes 524320 | tf_op jit(solution)/shard_map/ppermute | solution.py:292
  45.9 0.0 copy-done.1
  45.9 0.0 copy-done.2
  45.9 3.0 %shard_map.64.refs_5_ = f32[4,2048]{1,0:T(4,128)S(1)} custom-call(f32[1024,768]{1,0:T(8,128)S(1)} %copy-done.1, f32[1024,768]{1,0:T(8,128)S(1)} %copy-done.2, f32[1032,128]{1,0:T(8,128)S(1)} %constant_dynamic-update-slice_fusion.o_ref.refs_2_, f32[1032,128]{1,0:T(8,128)S(1)} %collective-permute-done.6.oo_ref.refs_3_, ...), custom_call_target="tpu_custom_call" | custom-call | flops 1 | bytes 1 | tf_op jit(solution)/shard_map/pallas_call | solution.py:219
  48.9 0.0 collective-permute-done.8.refs_4_
  49.0 0.9 %shard_map.65.refs_5_ = f32[4,2048]{1,0:T(4,128)S(1)} custom-call(f32[1024,768]{1,0:T(8,128)S(1)} %copy-done.1, f32[1024,768]{1,0:T(8,128)S(1)} %copy-done.2, f32[1032,128]{1,0:T(8,128)S(1)} %constant_dynamic-update-slice_fusion.o_ref.refs_2_, f32[1032,128]{1,0:T(8,128)S(1)} %collective-permute-done.6.oo_ref.refs_3_, ...), custom_call_target="tpu_custom_call" | custom-call | flops 1 | bytes 1 | tf_op jit(solution)/shard_map/pallas_call | solution.py:219
  49.8 1.3 %collective-permute-done.7.refs_4_ = f32[2,128,128]{2,1,0:T(8,128)S(1)} collective-permute-done((f32[2,128,128]{2,1,0:T(8,128)S(1)}, f32[2,128,128]{2,1,0:T(8,128)S(1)}, u32[]{:S(2)}, u32[]{:S(2)}) %collective-permute-start.7) | collective-permute-done | bytes 131104 | tf_op jit(solution)/shard_map/ppermute | solution.py:292
  51.1 0.9 %shard_map.66 = f32[4,2048]{1,0:T(4,128)S(1)} custom-call(f32[1024,768]{1,0:T(8,128)S(1)} %copy-done.1, f32[1024,768]{1,0:T(8,128)S(1)} %copy-done.2, f32[1032,128]{1,0:T(8,128)S(1)} %constant_dynamic-update-slice_fusion.o_ref.refs_2_, f32[1032,128]{1,0:T(8,128)S(1)} %collective-permute-done.6.oo_ref.refs_3_, ...), custom_call_target="tpu_custom_call" | custom-call | flops 1 | bytes 1 | tf_op jit(solution)/shard_map/pallas_call | solution.py:219
  52.0 0.1 fusion
  52.2 0.1 pad_maximum_fusion.2
  52.2 0.1 collective-permute-start.11
  52.3 1.2 %collective-permute-done.11 = f32[4,1040]{1,0:T(4,128)S(1)} collective-permute-done((f32[4,1040]{1,0:T(4,128)S(1)}, f32[4,1040]{1,0:T(4,128)S(1)}, u32[]{:S(2)}, u32[]{:S(2)}) %collective-permute-start.11) | collective-permute-done | bytes 16672 | tf_op jit(solution)/shard_map/ppermute | solution.py:258
  53.6 0.1 pad_maximum_fusion.3
  53.7 1.8 %collective-permute-start.12 = (f32[8,544]{1,0:T(8,128)S(1)}, f32[8,544]{1,0:T(8,128)S(1)}, u32[]{:S(2)}, u32[]{:S(2)}) collective-permute-start(f32[8,544]{1,0:T(8,128)S(1)} %pad_maximum_fusion.3), channel_id=1, source_target_pairs={{0,1},{1,0},{2,3},{3,2},{4,5},{5,4},{6,7},{7,6},{8,9},{9,8},{10,11... | collective-permute-start | bytes 52232 | tf_op jit(solution)/shard_map/ppermute | solution.py:350
  55.5 0.1 pad_maximum_fusion.7
  55.6 1.5 %collective-permute-start.13 = (f32[8,32]{1,0:T(8,128)S(1)}, f32[8,32]{1,0:T(8,128)S(1)}, u32[]{:S(2)}, u32[]{:S(2)}) collective-permute-start(f32[8,32]{1,0:T(8,128)S(1)} %pad_maximum_fusion.7), channel_id=1, source_target_pairs={{0,8},{1,9},{2,10},{3,11},{4,12},{5,13},{6,14},{7,15},{8,0},{9,1},... | collective-permute-start | bytes 3080 | tf_op jit(solution)/shard_map/ppermute | solution.py:350
  57.1 0.2 collective-permute-start.14
  57.3 0.2 collective-permute-done.12
  57.5 1.7 %collective-permute-done.13 = f32[8,32]{1,0:T(8,128)S(1)} collective-permute-done((f32[8,32]{1,0:T(8,128)S(1)}, f32[8,32]{1,0:T(8,128)S(1)}, u32[]{:S(2)}, u32[]{:S(2)}) %collective-permute-start.13) | collective-permute-done | bytes 1056 | tf_op jit(solution)/shard_map/ppermute | solution.py:350
  59.2 2.4 %collective-permute-done.14 = f32[8,32]{1,0:T(8,128)S(1)} collective-permute-done((f32[8,32]{1,0:T(8,128)S(1)}, f32[8,32]{1,0:T(8,128)S(1)}, u32[]{:S(2)}, u32[]{:S(2)}) %collective-permute-start.14) | collective-permute-done | bytes 1056 | tf_op jit(solution)/shard_map/ppermute | solution.py:350
  61.6 0.1 fusion.3
  61.7 2.6 %collective-permute-start.15 = (f32[8,288]{1,0:T(8,128)S(1)}, f32[8,288]{1,0:T(8,128)S(1)}, u32[]{:S(2)}, u32[]{:S(2)}) collective-permute-start(f32[8,288]{1,0:T(8,128)S(1)} %pad_maximum_fusion.4), channel_id=1, source_target_pairs={{0,2},{1,3},{2,0},{3,1},{4,6},{5,7},{6,4},{7,5},{8,10},{9,11},{10,... | collective-permute-start | bytes 27656 | tf_op jit(solution)/shard_map/ppermute | solution.py:350
  64.3 2.0 %collective-permute-done.15 = f32[8,288]{1,0:T(8,128)S(1)} collective-permute-done((f32[8,288]{1,0:T(8,128)S(1)}, f32[8,288]{1,0:T(8,128)S(1)}, u32[]{:S(2)}, u32[]{:S(2)}) %collective-permute-start.15) | collective-permute-done | bytes 9248 | tf_op jit(solution)/shard_map/ppermute | solution.py:350
  66.3 0.7 %shard_map.67 = (f32[8,256]{1,0:T(8,128)}, f32[8,16]{1,0:T(8,128)}) custom-call(f32[8,256]{1,0:T(8,128)S(1)} %slice_add_fusion.s_ref, f32[8,32]{1,0:T(8,128)S(1)} %slice_add_fusion.3.doc_ref), custom_call_target="tpu_custom_call" | custom-call | flops 1 | bytes 1 | tf_op jit(solution)/shard_map/pallas_call | solution.py:237
  (26 shorter events, 0.3 us)
Async XLA Ops:
  0.6 15.5 %copy-start = (f32[2,2048,128]{2,1,0:T(8,128)S(1)}, f32[2,2048,128]{2,1,0:T(8,128)}, u32[]{:S(2)}) copy-start(f32[2,2048,128]{2,1,0:T(8,128)} %g_ref.5) | copy-start | bytes 6291460
  0.6 8.6 %copy-start.6 = (s32[256]{0:T(256)S(1)}, s32[256]{0:T(256)}, u32[]{:S(2)}) copy-start(s32[256]{0:T(256)} %param.7) | copy-start | bytes 3076
  0.7 8.6 %copy-start.5 = (f32[256,128]{1,0:T(8,128)S(1)}, f32[256,128]{1,0:T(8,128)}, u32[]{:S(2)}) copy-start(f32[256,128]{1,0:T(8,128)} %param.6) | copy-start | bytes 393220
  1.8 24.7 %collective-permute-start.2 = (f32[1024,2048]{1,0:T(8,128)}, f32[1024,2048]{1,0:T(8,128)}, u32[]{:S(2)}, u32[]{:S(2)}) collective-permute-start(f32[1024,2048]{1,0:T(8,128)} %refs_0_.1), channel_id=1, source_target_pairs={{0,4},{4,0},{8,12},{12,8},{1,5},{5,1},{9,13},{13,9},{2,6},{6,2},{1... | collective-permute-start | bytes 25165832 | tf_op jit(solution)/shard_map/ppermute | solution.py:258
  2.3 6.9 %collective-permute-start = (f32[2,128,128]{2,1,0:T(8,128)S(1)}, f32[2,128,128]{2,1,0:T(8,128)S(1)}, u32[]{:S(2)}, u32[]{:S(2)}) collective-permute-start(f32[2,128,128]{2,1,0:T(8,128)S(1)} %get-tuple-element.45), channel_id=1, source_target_pairs={{0,8},{4,12},{8,0},{12,4},{1,9},{5,13},{9,1},{13,5},{2,10},{6,14},... | collective-permute-start | bytes 393224 | tf_op jit(solution)/shard_map/ppermute | solution.py:271
  4.9 10.9 %collective-permute-start.1 = (f32[2,128,128]{2,1,0:T(8,128)S(1)}, f32[2,128,128]{2,1,0:T(8,128)S(1)}, u32[]{:S(2)}, u32[]{:S(2)}) collective-permute-start(f32[2,128,128]{2,1,0:T(8,128)S(1)} %get-tuple-element.44), channel_id=1, source_target_pairs={{0,8},{4,12},{8,0},{12,4},{1,9},{5,13},{9,1},{13,5},{2,10},{6,14},... | collective-permute-start | bytes 393224 | tf_op jit(solution)/shard_map/ppermute | solution.py:271
  7.2 29.9 %collective-permute-start.10 = (f32[2,1024,128]{2,1,0:T(8,128)}, f32[2,1024,128]{2,1,0:T(8,128)}, u32[]{:S(2)}, u32[]{:S(2)}) collective-permute-start(f32[2,1024,128]{2,1,0:T(8,128)} %shard_map.62), channel_id=1, source_target_pairs={{0,8},{4,12},{8,0},{12,4},{1,9},{5,13},{9,1},{13,5},{2,10},{6,14},... | collective-permute-start | bytes 3145736 | tf_op jit(solution)/shard_map/ppermute | solution.py:294
  9.3 15.1 %collective-permute-start.3 = (f32[258,128]{1,0:T(8,128)S(1)}, f32[258,128]{1,0:T(8,128)S(1)}, u32[]{:S(2)}, u32[]{:S(2)}) collective-permute-start(f32[258,128]{1,0:T(8,128)S(1)} %pad_maximum_fusion), channel_id=1, source_target_pairs={{0,1},{1,0},{2,3},{3,2},{4,5},{5,4},{6,7},{7,6},{8,9},{9,8},{10,11... | collective-permute-start | bytes 396296 | tf_op jit(solution)/shard_map/ppermute | solution.py:301
  11.3 13.1 %collective-permute-start.4 = (f32[258,128]{1,0:T(8,128)S(1)}, f32[258,128]{1,0:T(8,128)S(1)}, u32[]{:S(2)}, u32[]{:S(2)}) collective-permute-start(f32[258,128]{1,0:T(8,128)S(1)} %pad_maximum_fusion), channel_id=1, source_target_pairs={{0,2},{1,3},{2,0},{3,1},{4,6},{5,7},{6,4},{7,5},{8,10},{9,11},{10,... | collective-permute-start | bytes 396296 | tf_op jit(solution)/shard_map/ppermute | solution.py:301
  15.8 8.4 %copy-start.3 = (f32[2,128,128]{2,1,0:T(8,128)}, f32[2,128,128]{2,1,0:T(8,128)S(1)}, u32[]{:S(2)}) copy-start(f32[2,128,128]{2,1,0:T(8,128)S(1)} %get-tuple-element.33) | copy-start | bytes 393220
  15.9 8.6 %collective-permute-start.5 = (f32[258,128]{1,0:T(8,128)S(1)}, f32[258,128]{1,0:T(8,128)S(1)}, u32[]{:S(2)}, u32[]{:S(2)}) collective-permute-start(f32[258,128]{1,0:T(8,128)S(1)} %pad_maximum_fusion), channel_id=1, source_target_pairs={{0,3},{1,2},{2,1},{3,0},{4,7},{5,6},{6,5},{7,4},{8,11},{9,10},{10,... | collective-permute-start | bytes 396296 | tf_op jit(solution)/shard_map/ppermute | solution.py:301
  24.5 2.0 %collective-permute-start.6 = (f32[1032,128]{1,0:T(8,128)S(1)}, f32[1032,128]{1,0:T(8,128)S(1)}, u32[]{:S(2)}, u32[]{:S(2)}) collective-permute-start(f32[1032,128]{1,0:T(8,128)S(1)} %constant_dynamic-update-slice_fusion.o_ref.refs_2_), channel_id=1, source_target_pairs={{0,4},{4,0},{8,12},{12,8},{1,5},{5,1},{9,13},{13,9},{2,6},{6,2},{1... | collective-permute-start | bytes 1585160 | tf_op jit(solution)/shard_map/ppermute | solution.py:258
  24.6 21.3 %collective-permute-start.9 = (f32[2,512,128]{2,1,0:T(8,128)}, f32[2,512,128]{2,1,0:T(8,128)}, u32[]{:S(2)}, u32[]{:S(2)}) collective-permute-start(f32[2,512,128]{2,1,0:T(8,128)} %get-tuple-element.34), channel_id=1, source_target_pairs={{0,8},{4,12},{8,0},{12,4},{1,9},{5,13},{9,1},{13,5},{2,10},{6,14},... | collective-permute-start | bytes 1572872 | tf_op jit(solution)/shard_map/ppermute | solution.py:292
  26.5 8.4 %copy-start.4 = (f32[2,128,128]{2,1,0:T(8,128)S(1)}, f32[2,128,128]{2,1,0:T(8,128)}, u32[]{:S(2)}) copy-start(f32[2,128,128]{2,1,0:T(8,128)} %copy-done.3) | copy-start | bytes 393220
  34.9 14.1 %collective-permute-start.8 = (f32[2,128,128]{2,1,0:T(8,128)S(1)}, f32[2,128,128]{2,1,0:T(8,128)S(1)}, u32[]{:S(2)}, u32[]{:S(2)}) collective-permute-start(f32[2,128,128]{2,1,0:T(8,128)S(1)} %copy-done.4), channel_id=1, source_target_pairs={{0,8},{4,12},{8,0},{12,4},{1,9},{5,13},{9,1},{13,5},{2,10},{6,14},... | collective-permute-start | bytes 393224 | tf_op jit(solution)/shard_map/ppermute | solution.py:292
  36.4 14.7 %collective-permute-start.7 = (f32[2,128,128]{2,1,0:T(8,128)S(1)}, f32[2,128,128]{2,1,0:T(8,128)S(1)}, u32[]{:S(2)}, u32[]{:S(2)}) collective-permute-start(f32[2,128,128]{2,1,0:T(8,128)S(1)} %get-tuple-element.32), channel_id=1, source_target_pairs={{0,8},{4,12},{8,0},{12,4},{1,9},{5,13},{9,1},{13,5},{2,10},{6,14},... | collective-permute-start | bytes 393224 | tf_op jit(solution)/shard_map/ppermute | solution.py:292
  37.1 8.8 %copy-start.1 = (f32[1024,768]{1,0:T(8,128)S(1)}, f32[1024,768]{1,0:T(8,128)}, u32[]{:S(2)}) copy-start(f32[1024,768]{1,0:T(8,128)} %get-tuple-element.25.refs_0_) | copy-start | bytes 9437188
  37.1 8.8 %copy-start.2 = (f32[1024,768]{1,0:T(8,128)S(1)}, f32[1024,768]{1,0:T(8,128)}, u32[]{:S(2)}) copy-start(f32[1024,768]{1,0:T(8,128)} %get-tuple-element.30.refs_1_) | copy-start | bytes 9437188
  52.2 1.3 %collective-permute-start.11 = (f32[4,1040]{1,0:T(4,128)S(1)}, f32[4,1040]{1,0:T(4,128)S(1)}, u32[]{:S(2)}, u32[]{:S(2)}) collective-permute-start(f32[4,1040]{1,0:T(4,128)S(1)} %pad_maximum_fusion.2), channel_id=1, source_target_pairs={{0,4},{4,0},{8,12},{12,8},{1,5},{5,1},{9,13},{13,9},{2,6},{6,2},{1... | collective-permute-start | bytes 49928 | tf_op jit(solution)/shard_map/ppermute | solution.py:258
  53.7 3.8 %collective-permute-start.12 = (f32[8,544]{1,0:T(8,128)S(1)}, f32[8,544]{1,0:T(8,128)S(1)}, u32[]{:S(2)}, u32[]{:S(2)}) collective-permute-start(f32[8,544]{1,0:T(8,128)S(1)} %pad_maximum_fusion.3), channel_id=1, source_target_pairs={{0,1},{1,0},{2,3},{3,2},{4,5},{5,4},{6,7},{7,6},{8,9},{9,8},{10,11... | collective-permute-start | bytes 52232 | tf_op jit(solution)/shard_map/ppermute | solution.py:350
  55.6 3.6 %collective-permute-start.13 = (f32[8,32]{1,0:T(8,128)S(1)}, f32[8,32]{1,0:T(8,128)S(1)}, u32[]{:S(2)}, u32[]{:S(2)}) collective-permute-start(f32[8,32]{1,0:T(8,128)S(1)} %pad_maximum_fusion.7), channel_id=1, source_target_pairs={{0,8},{1,9},{2,10},{3,11},{4,12},{5,13},{6,14},{7,15},{8,0},{9,1},... | collective-permute-start | bytes 3080 | tf_op jit(solution)/shard_map/ppermute | solution.py:350
  57.1 4.5 %collective-permute-start.14 = (f32[8,32]{1,0:T(8,128)S(1)}, f32[8,32]{1,0:T(8,128)S(1)}, u32[]{:S(2)}, u32[]{:S(2)}) collective-permute-start(f32[8,32]{1,0:T(8,128)S(1)} %pad_maximum_fusion.7), channel_id=1, source_target_pairs={{0,9},{1,8},{2,11},{3,10},{4,13},{5,12},{6,15},{7,14},{8,1},{9,0},... | collective-permute-start | bytes 3080 | tf_op jit(solution)/shard_map/ppermute | solution.py:350
  61.7 4.6 %collective-permute-start.15 = (f32[8,288]{1,0:T(8,128)S(1)}, f32[8,288]{1,0:T(8,128)S(1)}, u32[]{:S(2)}, u32[]{:S(2)}) collective-permute-start(f32[8,288]{1,0:T(8,128)S(1)} %pad_maximum_fusion.4), channel_id=1, source_target_pairs={{0,2},{1,3},{2,0},{3,1},{4,6},{5,7},{6,4},{7,5},{8,10},{9,11},{10,... | collective-permute-start | bytes 27656 | tf_op jit(solution)/shard_map/ppermute | solution.py:350
